TPU v7x, 512 devices: a whole 4x8x8 slice. The times are simulated.
512 devices in a mesh: vol: 64 (over x, y, z_hi), src: 8 (over z_lo, core).
Axes of the slice: x: 4, y: 8, z: 8 (z_hi: 2, z_lo: 4; z = z_hi * 4 + z_lo), core: 2. Of those that a mesh axis runs over, the one named last changes fastest.
Arguments:
- excitation: float32 [32, 128, 128, 128], P(None, 'vol', 'src'), may hold values from -6 to 6
- start: float32 [32, 128, 128, 128], P(None, 'vol', 'src'), may hold values from -4 to 4
- material: int32 [128, 128, 128], P('vol', 'src'), may hold values from 0 to 2
- face_cell: int32 [64, 8, 256], P('vol', 'src'), may hold values from 0 to 4095
- face_count: int32 [64, 8, 64], P('vol', 'src'), may hold values from 0 to 4, as said below
- face_weight: float32 [64, 8, 256], P('vol', 'src'), may hold values from 0.5 to 1.5
- slot_panel: int32 [64, 8, 256], P('vol', 'src'), may hold values from 0 to 127
- target_points: float32 [3, 65536], P(None, 'vol'), may hold values from 0 to 1
- source_points: float32 [3, 65536], P(None, 'src'), may hold values from 0 to 1
Outputs:
- potential: float32 [32, 128, 128, 128], P(None, 'vol', 'src')
- flux: float32 [32, 65536], P(None, ('vol', 'src'))
Inputs may be any that keep to these rules, and one draw needn't show every extreme that they name: A device has at most 4 live slots for one owner (the first face_count ones); in every draw some owner receives 4 live faces from every device.
All inputs are finite; a program needn't handle non-finite values.
Results may differ from a plain program's by a relative error of at most 0.0023.
The roundings to bfloat16 on the way count: a program that leaves them out, or rounds other values in their place, can miss the bound.
Values may be sent and summed in bfloat16 or wider, within the bound.
No kernel may reach another device: no remote copies, remote signals or barrier semaphores. Data moves between devices by JAX's collectives and lax.ppermute only.
A program may use at most 64 MiB of HBM per device.

v0:
```python
import jax
import jax.numpy as jnp
from jax import lax
from jax.sharding import PartitionSpec as P

P_SIZE = 65536
ITERS = 2
SWEEPS = 2


NU_BASE = (1.0, 0.05, 0.4)
NU_SATURATION = (0.0, 0.9, 0.3)
RELAXATION = 0.8
SOFTENING = 0.05


def extended(block, sides, width):
    for axis, dim in sides:
        count = lax.axis_size(axis)
        forward = [(i, i + 1) for i in range(count - 1)]
        backward = [(target, source) for source, target in forward]
        low = lax.ppermute(
            lax.slice_in_dim(block, block.shape[dim] - width, None, axis=dim), axis, forward
        )
        high = lax.ppermute(lax.slice_in_dim(block, 0, width, axis=dim), axis, backward)
        block = jnp.concatenate([low, block, high], axis=dim)
    return block


def reluctivity(grad_sq, material):
    base_value = jnp.zeros(material.shape, jnp.float32)
    slope_value = jnp.zeros(material.shape, jnp.float32)
    for material_id in range(3):
        picked = material == material_id
        base_value = jnp.where(picked, NU_BASE[material_id], base_value)
        slope_value = jnp.where(picked, NU_SATURATION[material_id], slope_value)
    return base_value[None] + slope_value[None] * grad_sq / (1.0 + grad_sq)


def gradient_sq(padded):
    along_x = 0.5 * (padded[:, 2:, 1:-1, 1:-1] - padded[:, :-2, 1:-1, 1:-1])
    along_y = 0.5 * (padded[:, 1:-1, 2:, 1:-1] - padded[:, 1:-1, :-2, 1:-1])
    along_z = 0.5 * (padded[:, 1:-1, 1:-1, 2:] - padded[:, 1:-1, 1:-1, :-2])
    return along_x * along_x + along_y * along_y + along_z * along_z


def pad_depth(values):
    return jnp.pad(values, ((0, 0), (0, 0), (0, 0), (1, 1)))


def face_weights(nu_ext, domain_edges):
    first_x, last_x, first_y, last_y = domain_edges
    interior = nu_ext[:, 1:-1, 1:-1]
    low_x = jnp.where(first_x, interior[:, :1], nu_ext[:, :1, 1:-1])
    high_x = jnp.where(last_x, interior[:, -1:], nu_ext[:, -1:, 1:-1])
    column = jnp.concatenate([low_x, interior, high_x], axis=1)
    low_y = jnp.where(first_y, interior[:, :, :1], nu_ext[:, 1:-1, :1])
    high_y = jnp.where(last_y, interior[:, :, -1:], nu_ext[:, 1:-1, -1:])
    row_ext = jnp.concatenate([low_y, interior, high_y], axis=2)
    depth_ext = jnp.pad(interior, ((0, 0), (0, 0), (0, 0), (1, 1)), mode="edge")
    return (
        0.5 * (interior + column[:, 2:]),
        0.5 * (interior + column[:, :-2]),
        0.5 * (interior + row_ext[:, :, 2:]),
        0.5 * (interior + row_ext[:, :, :-2]),
        0.5 * (interior + depth_ext[:, :, :, 2:]),
        0.5 * (interior + depth_ext[:, :, :, :-2]),
    )


def relax(padded, weights, diagonal, forcing):
    center = padded[:, 1:-1, 1:-1, 1:-1]
    neighbours = (
        padded[:, 2:, 1:-1, 1:-1],
        padded[:, :-2, 1:-1, 1:-1],
        padded[:, 1:-1, 2:, 1:-1],
        padded[:, 1:-1, :-2, 1:-1],
        padded[:, 1:-1, 1:-1, 2:],
        padded[:, 1:-1, 1:-1, :-2],
    )
    applied = diagonal * center
    for weight, neighbour in zip(weights, neighbours):
        applied = applied - weight * neighbour
    return center + RELAXATION * (forcing - applied) / diagonal


def with_rim(potential):
    return extended(potential, (("vol", 1), ("src", 2)), 1)


def per_device(
    excitation,
    start,
    material,
    face_cell,
    face_count,
    face_weight,
    slot_panel,
    target_points,
    source_points,
):
    vol_count = lax.axis_size("vol")
    first_x = lax.axis_index("vol") == 0
    last_x = lax.axis_index("vol") == vol_count - 1
    first_y = lax.axis_index("src") == 0
    last_y = lax.axis_index("src") == lax.axis_size("src") - 1
    domain_edges = (first_x, last_x, first_y, last_y)
    exc_count, width_x, width_y, depth_len = excitation.shape
    cell_count = width_x * width_y * depth_len
    slot_cells = face_cell.reshape(-1)
    slot_count = slot_cells.shape[0]
    capacity = slot_count // vol_count
    piece_len = source_points.shape[1] // vol_count
    target_len = target_points.shape[1]
    slot_rank = jnp.arange(slot_count, dtype=jnp.int32) % capacity
    live_count = jnp.repeat(face_count.reshape(-1), capacity, total_repeat_length=slot_count)
    slot_scale = jnp.where(slot_rank < live_count, face_weight.reshape(-1), 0.0)
    owner_table = (
        slot_panel.reshape(-1)[:, None] == jnp.arange(piece_len, dtype=jnp.int32)[None, :]
    ).astype(jnp.float32)
    flux_scale = float(P_SIZE) ** (-0.5)
    potential = start
    flux_own = jnp.zeros((exc_count, piece_len), jnp.float32)
    for outer_index in range(ITERS):
        current = with_rim(potential)
        nu_own = reluctivity(gradient_sq(pad_depth(current)), material)
        nu_ext = extended(nu_own, (("vol", 1), ("src", 2)), 1)
        weights = face_weights(nu_ext, domain_edges)
        diagonal = weights[0] + weights[1] + weights[2] + weights[3] + weights[4] + weights[5]
        cell_values = jnp.take(potential.reshape(exc_count, cell_count), slot_cells, axis=1)
        outgoing = (cell_values * slot_scale[None, :]).T.reshape(vol_count, capacity * exc_count)
        arrived = lax.all_to_all(outgoing, "vol", split_axis=0, concat_axis=0, tiled=True).reshape(
            slot_count, exc_count
        )
        density = jnp.dot(
            arrived.T,
            owner_table,
            precision=lax.Precision.HIGHEST,
            preferred_element_type=jnp.float32,
        ).astype(jnp.bfloat16)
        block_piece = lax.all_gather(density, "vol", axis=1, tiled=True)
        piece_count = block_piece.shape[1]
        step_len = 1024

        def one_step(step_index, partial_value):
            offset_index = step_index * step_len
            segment = lax.dynamic_slice_in_dim(block_piece, offset_index, step_len, 1)
            places = lax.dynamic_slice_in_dim(source_points, offset_index, step_len, 1)
            dist_sq = jnp.zeros((target_len, step_len), jnp.float32)
            for component in range(3):
                offset = target_points[component][:, None] - places[component][None, :]
                dist_sq = dist_sq + offset * offset
            kernel = lax.rsqrt(dist_sq + SOFTENING * SOFTENING).astype(jnp.bfloat16)
            return partial_value + jnp.einsum(
                "en,tn->et", segment, kernel, preferred_element_type=jnp.float32
            )

        partial_flux = lax.fori_loop(
            0, piece_count // step_len, one_step, jnp.zeros((exc_count, target_len), jnp.float32)
        )
        whole_sum = lax.psum(partial_flux, "src")
        flux_sum = lax.dynamic_slice_in_dim(
            whole_sum, lax.axis_index("src") * piece_len, piece_len, 1
        )
        flux_own = flux_sum * flux_scale
        per_slot = jnp.dot(
            flux_own,
            owner_table.T,
            precision=lax.Precision.HIGHEST,
            preferred_element_type=jnp.float32,
        )
        returned = lax.all_to_all(
            per_slot.T.reshape(vol_count, capacity * exc_count),
            "vol",
            split_axis=0,
            concat_axis=0,
            tiled=True,
        ).reshape(slot_count, exc_count)
        contribution = returned.T * slot_scale[None, :]
        surface = (
            jnp.zeros((exc_count, cell_count), jnp.float32).at[:, slot_cells].add(contribution)
        )
        forcing = excitation + surface.reshape(excitation.shape)
        for sweep_index in range(SWEEPS):
            if sweep_index > 0:
                current = with_rim(potential)
            potential = relax(pad_depth(current), weights, diagonal, forcing)
    return (potential, flux_own)


def solution(mesh):
    return jax.shard_map(
        per_device,
        mesh=mesh,
        in_specs=(
            P(None, "vol", "src", None),
            P(None, "vol", "src", None),
            P("vol", "src", None),
            P("vol", "src", None),
            P("vol", "src", None),
            P("vol", "src", None),
            P("vol", "src", None),
            P(None, "vol"),
            P(None, "src"),
        ),
        out_specs=(P(None, "vol", "src", None), P(None, ("vol", "src"))),
        check_vma=False,
    )
```

profile of v0, /device:TPU:1, one launch (start us, length us, event | category | flops | bytes accessed | tf_op | source)
XLA Modules:
  0.0 964.7 jit_solution(8178900089417844450)
XLA Ops:
  14.7 19.6 %all-to-all-start = ((f32[64,1,128]{2,1,0:T(1,128)}), f32[64,1,128]{2,1,0:T(1,128)S(1)}, u32[]{:S(2)}, u32[]{:S(2)}) async-start(f32[64,1,128]{2,1,0:T(1,128)} %bitcast.14), calls=%async_computation | async-start | bytes 65536 | tf_op jit(solution)/shard_map/all_to_all | solution.py:132
  35.6 7.9 collective-permute-start.1
  43.5 3.8 all-to-all-done
  49.2 208.1 %all_gather.6 = bf16[32,8192]{1,0:T(8,128)(2,1)S(1)} all-gather(bf16[32,128]{1,0:T(8,128)(2,1)S(1)} %convolution_convert_fusion.1), channel_id=1, replica_groups=mesh['vol'=64,'src'=8] {'vol'}, dimensions={1}, use_global_device_ids=true | all-gather | bytes 532480 | tf_op jit(solution)/shard_map/all_gather | solution.py:141
  257.3 21.4 %while.29 = (s32[]{:T(128)}, f32[32,1024]{1,0:T(8,128)S(1)}, bf16[32,8192]{1,0:T(8,128)(2,1)S(1)}, f32[3,1024]{1,0:T(4,128)S(1)}, f32[3,8192]{1,0:T(4,128)}, /*i...) while((s32[]{:T(128)}, f32[32,1024]{1,0:T(8,128)S(1)}, ...), condition=%wide.region_1.3_spmd.clone, body=%wide.region_0.2_spmd.clone.sunk | while | flops 77660168 | bytes 401621 | solution.py:158
  279.4 89.0 %all-reduce.7.cloned.1.call-done = f32[32,1024]{1,0:T(8,128)} async-done(((f32[32,1024]{1,0:T(8,128)}), f32[32,1024]{1,0:T(8,128)}) %all-reduce.7.cloned.1.call-update) | async-done | bytes 131088 | tf_op jit(solution)/shard_map/psum | solution.py:161
  370.2 14.4 %all-to-all-start.1 = ((f32[64,1,128]{2,1,0:T(1,128)}), f32[64,1,128]{2,1,0:T(1,128)S(1)}, u32[]{:S(2)}, u32[]{:S(2)}) async-start(f32[64,1,128]{2,1,0:T(1,128)} %bitcast.15), calls=%async_computation.1 | async-start | bytes 65536 | tf_op jit(solution)/shard_map/all_to_all | solution.py:172
  386.8 3.0 collective-permute-start.2
  389.8 7.8 all-to-all-done.1
  398.5 2.9 scatter_custom_fusion
  401.4 3.0 copy.25
  412.3 27.2 %collective-permute-done.4 = f32[32,1,16,128]{3,2,1,0:T(8,128)S(1)} collective-permute-done((f32[32,1,16,128]{3,2,1,0:T(8,128)S(1)}, f32[32,1,16,128]{3,2,1,0:T(8,128)S(1)}, u32[]{:S(2)}, u32[]{:S(2)}) %collective-permute-start.4) | collective-permute-done | bytes 262176 | tf_op jit(solution)/shard_map/ppermute | solution.py:25
  441.5 2.6 collective-permute-start.6
  444.2 2.9 collective-permute-done.6
  452.1 3.2 collective-permute-done.9
  455.3 26.0 %collective-permute-done.8 = f32[32,1,16,128]{3,2,1,0:T(8,128)S(1)} collective-permute-done((f32[32,1,16,128]{3,2,1,0:T(8,128)S(1)}, f32[32,1,16,128]{3,2,1,0:T(8,128)S(1)}, u32[]{:S(2)}, u32[]{:S(2)}) %collective-permute-start.8) | collective-permute-done | bytes 262176 | tf_op jit(solution)/shard_map/ppermute | solution.py:25
  485.7 3.1 collective-permute-done.10
  495.6 5.4 all-to-all-start.2
  501.1 6.8 collective-permute-start.13
  509.3 5.5 all-to-all-done.2
  516.0 203.6 %all_gather.7 = bf16[32,8192]{1,0:T(8,128)(2,1)S(1)} all-gather(bf16[32,128]{1,0:T(8,128)(2,1)S(1)} %convolution_convert_fusion), channel_id=1, replica_groups=mesh['vol'=64,'src'=8] {'vol'}, dimensions={1}, use_global_device_ids=true | all-gather | bytes 532480 | tf_op jit(solution)/shard_map/all_gather | solution.py:141
  719.6 21.4 %while.30 = (s32[]{:T(128)}, f32[32,1024]{1,0:T(8,128)S(1)}, bf16[32,8192]{1,0:T(8,128)(2,1)S(1)}, f32[3,1024]{1,0:T(4,128)S(1)}, f32[3,8192]{1,0:T(4,128)}, /*i...) while((s32[]{:T(128)}, f32[32,1024]{1,0:T(8,128)S(1)}, ...), condition=%wide.region_5.7_spmd.clone, body=%wide.region_4.6_spmd.clone.sunk | while | flops 77660168 | bytes 401621 | solution.py:158
  741.7 88.8 %all-reduce.9.cloned.1.call-done = f32[32,1024]{1,0:T(8,128)} async-done(((f32[32,1024]{1,0:T(8,128)}), f32[32,1024]{1,0:T(8,128)}) %all-reduce.9.cloned.1.call-update) | async-done | bytes 131088 | tf_op jit(solution)/shard_map/psum | solution.py:161
  832.0 3.3 collective-permute-start.15
  835.3 3.0 collective-permute-start.14
  838.7 25.7 %all_to_all.36 = f32[64,1,128]{2,1,0:T(1,128)S(1)} all-to-all(f32[64,1,128]{2,1,0:T(1,128)S(1)} %bitcast.78), channel_id=1, replica_groups=mesh['vol'=64,'src'=8] {'vol'}, dimensions={0} | all-to-all | bytes 65536 | tf_op jit(solution)/shard_map/all_to_all | solution.py:172
  875.8 3.1 collective-permute-done.17
  879.0 26.3 %collective-permute-done.16 = f32[32,1,16,128]{3,2,1,0:T(8,128)S(1)} collective-permute-done((f32[32,1,16,128]{3,2,1,0:T(8,128)S(1)}, f32[32,1,16,128]{3,2,1,0:T(8,128)S(1)}, u32[]{:S(2)}, u32[]{:S(2)}) %collective-permute-start.16) | collective-permute-done | bytes 262176 | tf_op jit(solution)/shard_map/ppermute | solution.py:25
  909.8 3.1 collective-permute-done.18
  916.9 3.2 collective-permute-done.21
  920.1 26.0 %collective-permute-done.20 = f32[32,1,16,128]{3,2,1,0:T(8,128)S(1)} collective-permute-done((f32[32,1,16,128]{3,2,1,0:T(8,128)S(1)}, f32[32,1,16,128]{3,2,1,0:T(8,128)S(1)}, u32[]{:S(2)}, u32[]{:S(2)}) %collective-permute-start.20) | collective-permute-done | bytes 262176 | tf_op jit(solution)/shard_map/ppermute | solution.py:25
  950.5 3.2 collective-permute-done.22
  (210 shorter events, 117.2 us)
Async XLA Ops:
  8.0 249.3 %copy-start.33 = (pred[256]{0:T(512)(128)(4,1)}, pred[256]{0:T(512)(128)(4,1)S(1)}, u32[]{:S(2)}) copy-start(pred[256]{0:T(512)(128)(4,1)S(1)} %compare_and_fusion) | copy-start | bytes 772
  8.7 248.6 %copy-start.16 = (f32[3,1024]{1,0:T(4,128)S(1)}, f32[3,1024]{1,0:T(4,128)}, u32[]{:S(2)}) copy-start(f32[3,1024]{1,0:T(4,128)} %param.24) | copy-start | bytes 36868
  14.7 32.7 %all-to-all-start = ((f32[64,1,128]{2,1,0:T(1,128)}), f32[64,1,128]{2,1,0:T(1,128)S(1)}, u32[]{:S(2)}, u32[]{:S(2)}) async-start(f32[64,1,128]{2,1,0:T(1,128)} %bitcast.14), calls=%async_computation | async-start | bytes 65536 | tf_op jit(solution)/shard_map/all_to_all | solution.py:132
  34.2 334.3 %all-reduce.7.cloned.1.call-start = ((), (), s32[]{:S(2)}) async-start(), calls=%async_computation.4 | async-start | bytes 262144 | tf_op jit(solution)/shard_map/psum | solution.py:161
  34.3 350.4 %collective-permute-start = (f32[32,1,16,128]{3,2,1,0:T(8,128)S(1)}, f32[32,1,16,128]{3,2,1,0:T(8,128)S(1)}, u32[]{:S(2)}, u32[]{:S(2)}) collective-permute-start(f32[32,1,16,128]{3,2,1,0:T(8,128)S(1)} %get-tuple-element.317), channel_id=1, source_target_pairs={{8,0},{16,8},{24,16},{32,24},{40,32},{48,40},{56,48},{64,56},{72,6... | collective-permute-start | bytes 786440 | tf_op jit(solution)/shard_map/ppermute | solution.py:25
  35.6 349.0 %collective-permute-start.1 = (f32[32,1,16,128]{3,2,1,0:T(8,128)S(1)}, f32[32,1,16,128]{3,2,1,0:T(8,128)S(1)}, u32[]{:S(2)}, u32[]{:S(2)}) collective-permute-start(f32[32,1,16,128]{3,2,1,0:T(8,128)S(1)} %get-tuple-element.318), channel_id=1, source_target_pairs={{0,8},{8,16},{16,24},{24,32},{32,40},{40,48},{48,56},{56,64},{64,7... | collective-permute-start | bytes 786440 | tf_op jit(solution)/shard_map/ppermute | solution.py:22
  370.2 27.5 %all-to-all-start.1 = ((f32[64,1,128]{2,1,0:T(1,128)}), f32[64,1,128]{2,1,0:T(1,128)S(1)}, u32[]{:S(2)}, u32[]{:S(2)}) async-start(f32[64,1,128]{2,1,0:T(1,128)} %bitcast.15), calls=%async_computation.1 | async-start | bytes 65536 | tf_op jit(solution)/shard_map/all_to_all | solution.py:172
  384.9 19.6 %collective-permute-start.3 = (f32[32,4,1,128]{3,2,1,0:T(1,128)S(1)}, f32[32,4,1,128]{3,2,1,0:T(1,128)S(1)}, u32[]{:S(2)}, u32[]{:S(2)}) collective-permute-start(f32[32,4,1,128]{3,2,1,0:T(1,128)S(1)} %get-tuple-element.293), channel_id=1, source_target_pairs={{0,1},{1,2},{2,3},{3,4},{4,5},{5,6},{6,7},{8,9},{9,10},{10,11},{11... | collective-permute-start | bytes 196616 | tf_op jit(solution)/shard_map/ppermute | solution.py:22
  386.8 17.7 %collective-permute-start.2 = (f32[32,4,1,128]{3,2,1,0:T(1,128)S(1)}, f32[32,4,1,128]{3,2,1,0:T(1,128)S(1)}, u32[]{:S(2)}, u32[]{:S(2)}) collective-permute-start(f32[32,4,1,128]{3,2,1,0:T(1,128)S(1)} %get-tuple-element.294), channel_id=1, source_target_pairs={{1,0},{2,1},{3,2},{4,3},{5,4},{6,5},{7,6},{9,8},{10,9},{11,10},{12... | collective-permute-start | bytes 196616 | tf_op jit(solution)/shard_map/ppermute | solution.py:25
  406.6 5.7 collective-permute-start.5
  409.0 30.5 %collective-permute-start.4 = (f32[32,1,16,128]{3,2,1,0:T(8,128)S(1)}, f32[32,1,16,128]{3,2,1,0:T(8,128)S(1)}, u32[]{:S(2)}, u32[]{:S(2)}) collective-permute-start(f32[32,1,16,128]{3,2,1,0:T(8,128)S(1)} %get-tuple-element.316), channel_id=1, source_target_pairs={{8,0},{16,8},{24,16},{32,24},{40,32},{48,40},{56,48},{64,56},{72,6... | collective-permute-start | bytes 786440 | tf_op jit(solution)/shard_map/ppermute | solution.py:25
  439.6 4.6 collective-permute-start.7
  441.5 5.6 collective-permute-start.6
  449.3 5.9 collective-permute-start.9
  450.8 30.5 %collective-permute-start.8 = (f32[32,1,16,128]{3,2,1,0:T(8,128)S(1)}, f32[32,1,16,128]{3,2,1,0:T(8,128)S(1)}, u32[]{:S(2)}, u32[]{:S(2)}) collective-permute-start(f32[32,1,16,128]{3,2,1,0:T(8,128)S(1)} %get-tuple-element.308), channel_id=1, source_target_pairs={{8,0},{16,8},{24,16},{32,24},{40,32},{48,40},{56,48},{64,56},{72,6... | collective-permute-start | bytes 786440 | tf_op jit(solution)/shard_map/ppermute | solution.py:25
  481.3 4.4 collective-permute-start.11
  483.3 5.6 collective-permute-start.10
  493.4 226.2 %copy-start.25 = (f32[32,1024]{1,0:T(8,128)S(1)}, f32[32,1024]{1,0:T(8,128)}, u32[]{:S(2)}) copy-start(f32[32,1024]{1,0:T(8,128)} %custom-call.1) | copy-start | bytes 393220
  495.6 19.2 %all-to-all-start.2 = ((f32[64,1,128]{2,1,0:T(1,128)}), f32[64,1,128]{2,1,0:T(1,128)S(1)}, u32[]{:S(2)}, u32[]{:S(2)}) async-start(f32[64,1,128]{2,1,0:T(1,128)} %bitcast.20), calls=%async_computation.2 | async-start | bytes 65536 | tf_op jit(solution)/shard_map/all_to_all | solution.py:132
  501.0 329.5 %all-reduce.9.cloned.1.call-start = ((), (), s32[]{:S(2)}) async-start(), calls=%async_computation.5 | async-start | bytes 262144 | tf_op jit(solution)/shard_map/psum | solution.py:161
  501.1 330.1 %collective-permute-start.13 = (f32[32,1,16,128]{3,2,1,0:T(8,128)S(1)}, f32[32,1,16,128]{3,2,1,0:T(8,128)S(1)}, u32[]{:S(2)}, u32[]{:S(2)}) collective-permute-start(f32[32,1,16,128]{3,2,1,0:T(8,128)S(1)} %get-tuple-element.305), channel_id=1, source_target_pairs={{0,8},{8,16},{16,24},{24,32},{32,40},{40,48},{48,56},{56,64},{64,7... | collective-permute-start | bytes 786440 | tf_op jit(solution)/shard_map/ppermute | solution.py:22
  508.0 323.3 %collective-permute-start.12 = (f32[32,1,16,128]{3,2,1,0:T(8,128)S(1)}, f32[32,1,16,128]{3,2,1,0:T(8,128)S(1)}, u32[]{:S(2)}, u32[]{:S(2)}) collective-permute-start(f32[32,1,16,128]{3,2,1,0:T(8,128)S(1)} %get-tuple-element.306), channel_id=1, source_target_pairs={{8,0},{16,8},{24,16},{32,24},{40,32},{48,40},{56,48},{64,56},{72,6... | collective-permute-start | bytes 786440 | tf_op jit(solution)/shard_map/ppermute | solution.py:25
  832.0 37.1 %collective-permute-start.15 = (f32[32,4,1,128]{3,2,1,0:T(1,128)}, f32[32,4,1,128]{3,2,1,0:T(1,128)S(1)}, u32[]{:S(2)}, u32[]{:S(2)}) collective-permute-start(f32[32,4,1,128]{3,2,1,0:T(1,128)} %get-tuple-element.287), channel_id=1, source_target_pairs={{0,1},{1,2},{2,3},{3,4},{4,5},{5,6},{6,7},{8,9},{9,10},{10,11},{11... | collective-permute-start | bytes 196616 | tf_op jit(solution)/shard_map/ppermute | solution.py:22
  835.3 33.8 %collective-permute-start.14 = (f32[32,4,1,128]{3,2,1,0:T(1,128)}, f32[32,4,1,128]{3,2,1,0:T(1,128)S(1)}, u32[]{:S(2)}, u32[]{:S(2)}) collective-permute-start(f32[32,4,1,128]{3,2,1,0:T(1,128)} %get-tuple-element.288), channel_id=1, source_target_pairs={{1,0},{2,1},{3,2},{4,3},{5,4},{6,5},{7,6},{9,8},{10,9},{11,10},{12... | collective-permute-start | bytes 196616 | tf_op jit(solution)/shard_map/ppermute | solution.py:25
  872.0 7.0 collective-permute-start.17
  874.3 31.0 %collective-permute-start.16 = (f32[32,1,16,128]{3,2,1,0:T(8,128)S(1)}, f32[32,1,16,128]{3,2,1,0:T(8,128)S(1)}, u32[]{:S(2)}, u32[]{:S(2)}) collective-permute-start(f32[32,1,16,128]{3,2,1,0:T(8,128)S(1)} %get-tuple-element.304), channel_id=1, source_target_pairs={{8,0},{16,8},{24,16},{32,24},{40,32},{48,40},{56,48},{64,56},{72,6... | collective-permute-start | bytes 786440 | tf_op jit(solution)/shard_map/ppermute | solution.py:25
  905.4 4.4 collective-permute-start.19
  907.3 5.6 collective-permute-start.18
  914.3 5.8 collective-permute-start.21
  915.6 30.5 %collective-permute-start.20 = (f32[32,1,16,128]{3,2,1,0:T(8,128)S(1)}, f32[32,1,16,128]{3,2,1,0:T(8,128)S(1)}, u32[]{:S(2)}, u32[]{:S(2)}) collective-permute-start(f32[32,1,16,128]{3,2,1,0:T(8,128)S(1)} %get-tuple-element.296), channel_id=1, source_target_pairs={{8,0},{16,8},{24,16},{32,24},{40,32},{48,40},{56,48},{64,56},{72,6... | collective-permute-start | bytes 786440 | tf_op jit(solution)/shard_map/ppermute | solution.py:25
  946.2 4.3 collective-permute-start.23
  948.1 5.6 collective-permute-start.22
  (34 other events, 937.4 us)
Sparse Core Ops, SparseCore 0:
  279.5 88.9 all-reduce.6
  741.8 88.6 all-reduce.8
where the time goes:
time: 967 us; the launch traced here: 965 us
  blocking collectives  437 us (45%)
  waiting for transfers between devices  324 us (34%)
  starting transfers between devices  98.3 us (10%)
  local copies, waits for them, and re-layouts  30.3 us (3%)
  other arithmetic  29.5 us (3%)
  matrix products  29.4 us (3%)
  between operations  15.1 us (2%)
    all_gather x2, blocking collectives, per_device(): block_piece = lax.all_gather(density, 'vol', axis=1, tiled=True)  412 us
    psum x2, waiting for transfers between devices, per_device(): whole_sum = lax.psum(partial_flux, 'src')  178 us
    ppermute x12, waiting for transfers between devices, extended(): lax.ppermute(lax.slice_in_dim(block, 0, width, axis=dim), axis, backward)  118 us
    ppermute x12, starting transfers between devices, extended(): lax.ppermute(lax.slice_in_dim(block, block.shape[dim] - width, None, axis...  35.1 us
    dot_general x16, matrix products, one_step(): jnp.einsum('en,tn->et', segment, kernel, preferred_element_type=jnp.float32)  27.6 us
    all_to_all x1, blocking collectives, per_device(): lax.all_to_all(per_slot.T.reshape(vol_count, capacity * exc_count), 'vol'...  25.7 us
    all_to_all x2, starting transfers between devices, per_device(): lax.all_to_all(outgoing, 'vol', split_axis=0, concat_axis=0, tiled=True)  25 us
    ppermute x12, starting transfers between devices, extended(): lax.ppermute(lax.slice_in_dim(block, 0, width, axis=dim), axis, backward)  23.6 us
  transfers between devices with their start and end apart: 29, of which 17 were waited for; matrix products, arithmetic and copies ran while one was open for 6% of the time, Pallas kernels for 0%

commit v1 on v0

v1 whole, which is shorter than its diff:
```python
import jax
import jax.numpy as jnp
from jax import lax
from jax.experimental import pallas as pl
from jax.experimental.pallas import tpu as pltpu
from jax.sharding import Mesh
from jax.sharding import PartitionSpec as P

P_SIZE = 65536
ITERS = 2
NU_BASE = (1.0, 0.05, 0.4)
NU_SATURATION = (0.0, 0.9, 0.3)
RELAXATION = 0.8
SOFTENING = 0.05

F32 = jnp.float32
BF16 = jnp.bfloat16
NXY = 32
EH = 16
LX, LY, LZ = 4, 16, 128
KERNEL_VMEM = 60 << 20
VM = pl.BlockSpec(memory_space=pltpu.VMEM)
SM = pl.BlockSpec(memory_space=pltpu.SMEM)
PLANE = ("x", "y")
ROW = ("z", "c")


def sds(shape, dtype=F32):
    return jax.ShapeDtypeStruct(shape, dtype)


def call(body, out_shape, args, smem=(), scratch=(), flops=2_000_000, nbytes=2_000_000):
    return pl.pallas_call(
        body,
        out_shape=out_shape,
        in_specs=[SM if i in smem else VM for i in range(len(args))],
        out_specs=jax.tree.map(lambda _: VM, out_shape),
        scratch_shapes=list(scratch),
        compiler_params=pltpu.CompilerParams(vmem_limit_bytes=8 << 20),
        cost_estimate=pl.CostEstimate(flops=flops, bytes_accessed=nbytes, transcendentals=0),
    )(*args)


def split3(value):
    one = value.astype(BF16).astype(F32)
    rest = value - one
    two = rest.astype(BF16).astype(F32)
    return one, two, rest - two


def augmented(points, is_target):
    length = points.shape[1]
    shifted = jnp.concatenate([points - 0.5, jnp.zeros((5, length), F32)])
    norm = jnp.sum(shifted * shifted, axis=0, keepdims=True)
    if is_target:
        norm = norm + SOFTENING * SOFTENING
    norms = split3(norm)
    parts = split3(shifted)
    index = lax.broadcasted_iota(jnp.int32, (8, length), 0)
    first = 0 if is_target else 3
    extra = jnp.where(index < 6, 1.0, 0.0)
    for i in range(3):
        extra = jnp.where(index == first + i, norms[i], extra)
    rows = []
    for i in range(3):
        for j in range(3):
            rows.append(-2.0 * parts[i] if is_target else parts[j])
    return jnp.concatenate(rows + [extra, jnp.zeros((48, length), F32)])


def kernel_matrix_body(t_ref, s_ref, out_ref, turned_ref, aug_ref):
    @pl.when(pl.program_id(0) == 0)
    def _():
        aug_ref[...] = augmented(t_ref[...], True).astype(BF16)

    sources = augmented(s_ref[...], False)
    for i in range(4):
        pieces = [sources[:, (2 * i + k) * 128 : (2 * i + k + 1) * 128].T for k in range(2)]
        turned = jnp.concatenate(pieces).astype(BF16)
        at = slice(i * 256, (i + 1) * 256)
        turned_ref[at, :] = turned
        dist_sq = jnp.dot(turned, aug_ref[...], preferred_element_type=F32)
        out_ref[at, :] = lax.rsqrt(dist_sq).astype(BF16)


def kernel_matrix(targets, sources):
    return pl.pallas_call(
        kernel_matrix_body,
        grid=(8,),
        out_shape=(sds((8192, 1024), BF16), sds((8192, 128), BF16)),
        in_specs=[
            pl.BlockSpec((3, 1024), lambda i: (0, 0)),
            pl.BlockSpec((3, 1024), lambda i: (0, i)),
        ],
        out_specs=(
            pl.BlockSpec((1024, 1024), lambda i: (i, 0)),
            pl.BlockSpec((1024, 128), lambda i: (i, 0)),
        ),
        scratch_shapes=[pltpu.VMEM((128, 1024), BF16)],
        compiler_params=pltpu.CompilerParams(vmem_limit_bytes=KERNEL_VMEM),
        cost_estimate=pl.CostEstimate(
            flops=2_000_000_000, bytes_accessed=20_000_000, transcendentals=8_400_000
        ),
    )(targets, sources)


def density_body(arr, owner_hot, msg):
    turned = arr[...].T
    dens = []
    for wl in range(2):
        total = jnp.zeros((EH, 128), F32)
        for vl in range(2):
            q = vl * 2 + wl
            rows = turned[q * EH : (q + 1) * EH]
            parts = jnp.concatenate(split3(rows)).astype(BF16)
            found = jnp.dot(
                parts, owner_hot[q * 128 : (q + 1) * 128, :], preferred_element_type=F32
            )
            total = total + found[:EH] + found[EH : 2 * EH] + found[2 * EH :]
        dens.append(total)
    out = jnp.concatenate(dens).astype(BF16)
    for peer in range(NXY):
        msg[peer] = out


def flux_body(arr, t_ref, k0_ref, turned_ref, out_ref, aug_ref, acc_ref):
    step = pl.program_id(0)

    @pl.when(step == 0)
    def _():
        aug_ref[...] = augmented(t_ref[...], True).astype(BF16)
        acc_ref[...] = jnp.zeros_like(acc_ref)

    totals = [acc_ref[0], acc_ref[1]]
    for i in range(4):
        at = slice(i * 256, (i + 1) * 256)
        dens = jnp.concatenate([arr[i, :EH], arr[i, EH:]], axis=1)
        dist_sq = jnp.dot(turned_ref[at, :], aug_ref[...], preferred_element_type=F32)
        k1 = lax.rsqrt(dist_sq).astype(BF16)
        totals[0] = totals[0] + jnp.dot(dens, k0_ref[at, :], preferred_element_type=F32)
        totals[1] = totals[1] + jnp.dot(dens, k1, preferred_element_type=F32)
    for half in range(2):
        acc_ref[half] = totals[half]

    @pl.when(step == 7)
    def _():
        for half in range(2):
            for part in range(8):
                out_ref[part, half] = acc_ref[half, :, part * 128 : (part + 1) * 128] * (
                    float(P_SIZE) ** (-0.5)
                )


def partial_flux(arrived, targets, k0, turned):
    return pl.pallas_call(
        flux_body,
        grid=(8,),
        out_shape=sds((8, 2, EH, 128)),
        in_specs=[
            pl.BlockSpec((4, 2 * EH, 128), lambda i: (i, 0, 0)),
            pl.BlockSpec((3, 1024), lambda i: (0, 0)),
            pl.BlockSpec((1024, 1024), lambda i: (i, 0)),
            pl.BlockSpec((1024, 128), lambda i: (i, 0)),
        ],
        out_specs=pl.BlockSpec((8, 2, EH, 128), lambda i: (0, 0, 0, 0)),
        scratch_shapes=[pltpu.VMEM((128, 1024), BF16), pltpu.VMEM((2, EH, 1024), F32)],
        compiler_params=pltpu.CompilerParams(vmem_limit_bytes=KERNEL_VMEM),
        cost_estimate=pl.CostEstimate(
            flops=4_000_000_000, bytes_accessed=20_000_000, transcendentals=8_400_000
        ),
    )(arrived, targets, k0, turned)


def owner_body(flags_ref, parts_ref, owner_hot, flux_ref, msg_ref):
    total = parts_ref[0]
    for part in range(1, 8):
        total = total + parts_ref[part]
    flux_ref[...] = total
    swapped = flags_ref[4] == 1
    blocks = (
        jnp.where(swapped, total[1], total[0]),
        jnp.where(swapped, total[0], total[1]),
    )
    nt = (((1,), (1,)), ((), ()))
    out = jnp.zeros((128, 128), F32)
    for q in range(4):
        above_rows = [jnp.zeros((EH * q, 128), F32)] if q else []
        rows = jnp.concatenate(
            above_rows + [blocks[q % 2], jnp.zeros((128 - EH * (q + 1), 128), F32)]
        )
        for piece in split3(rows):
            out = out + lax.dot_general(
                owner_hot[q * 128 : (q + 1) * 128, :],
                piece.astype(BF16),
                nt,
                preferred_element_type=F32,
            )
    msg_ref[...] = out


def lane_iota():
    return lax.broadcasted_iota(jnp.int32, (EH, LZ), 1)


def below(value, lane, edge):
    return jnp.where(lane == 0, edge, pltpu.roll(value, 1, 1))


def above(value, lane, edge):
    return jnp.where(lane == LZ - 1, edge, pltpu.roll(value, LZ - 1, 1))


def nu_body(
    flags_ref, pot, xl, xh, yl, yh, mo, mxl, mxh, myl, myh, pp, nu, scale
):
    pp[2:6, 2:18] = pot[...]
    pp[0:2, 2:18] = xl[...].astype(F32)
    pp[6:8, 2:18] = xh[...].astype(F32)
    pp[1:7, 0:2] = yl[...].astype(F32)
    pp[1:7, 18:20] = yh[...].astype(F32)
    lane = lane_iota()

    def nu_at(x, y, ids):
        center = pp[x, y]
        gx = pp[x + 1, y] - pp[x - 1, y]
        gy = pp[x, y + 1] - pp[x, y - 1]
        gz = above(center, lane, 0.0) - below(center, lane, 0.0)
        grad_sq = 0.25 * (gx * gx + gy * gy + gz * gz)
        base = jnp.where(ids == 0, NU_BASE[0], jnp.where(ids == 1, NU_BASE[1], NU_BASE[2]))
        slope = jnp.where(
            ids == 0, NU_SATURATION[0], jnp.where(ids == 1, NU_SATURATION[1], NU_SATURATION[2])
        )
        return base + slope * (grad_sq / (1.0 + grad_sq))

    def own_rows(y, carry):
        for x in range(LX):
            nu[x + 1, y + 1] = nu_at(x + 2, y + 2, mo[x, pl.ds(y, 1), :])
        nu[0, y + 1] = jnp.where(
            flags_ref[0] == 1, nu[1, y + 1], nu_at(1, y + 2, mxl[pl.ds(y, 1), :])
        )
        nu[5, y + 1] = jnp.where(
            flags_ref[1] == 1, nu[4, y + 1], nu_at(6, y + 2, mxh[pl.ds(y, 1), :])
        )
        return carry

    lax.fori_loop(0, LY, own_rows, 0)
    for x in range(LX):
        nu[x + 1, 0] = jnp.where(
            flags_ref[2] == 1, nu[x + 1, 1], nu_at(x + 2, 1, myl[x : x + 1, :])
        )
        nu[x + 1, 17] = jnp.where(
            flags_ref[3] == 1, nu[x + 1, 16], nu_at(x + 2, 18, myh[x : x + 1, :])
        )

    def scale_rows(y, carry):
        for x in range(LX):
            own = nu[x + 1, y + 1]
            total = (
                nu[x, y + 1]
                + nu[x + 2, y + 1]
                + nu[x + 1, y]
                + nu[x + 1, y + 2]
                + below(own, lane, own)
                + above(own, lane, own)
            )
            scale[x, y] = RELAXATION / (3.0 * own + 0.5 * total)
        return carry

    lax.fori_loop(0, LY, scale_rows, 0)


def relaxed(p, px, py, nu, scale, forcing, x, y, lane):
    center = p[x + px, y + py]
    own = nu[x + 1, y + 1]
    around = (
        (p[x + px - 1, y + py], nu[x, y + 1]),
        (p[x + px + 1, y + py], nu[x + 2, y + 1]),
        (p[x + px, y + py - 1], nu[x + 1, y]),
        (p[x + px, y + py + 1], nu[x + 1, y + 2]),
        (below(center, lane, 0.0), pltpu.roll(own, 1, 1)),
        (above(center, lane, 0.0), pltpu.roll(own, LZ - 1, 1)),
    )
    total = around[0][0] * (own + around[0][1])
    for value, other in around[1:]:
        total = total + value * (own + other)
    return (1.0 - RELAXATION) * center + scale[x, y] * (forcing + 0.5 * total)


def sweep_one_body(
    arr, hot, lanes_ref, exc, pp, nu, scale, pot, forcing, xlo, xhi, ylo, yhi
):
    turned = arr[...].T
    lane = lane_iota()
    slots = jnp.concatenate([turned[q * EH : (q + 1) * EH] for q in range(4)], axis=1)
    slots = slots * lanes_ref[1:2, :]
    hi = slots.astype(BF16).astype(F32)
    low = slots - hi
    cell_row = lanes_ref[0:1, :]
    for group in range(8):
        masks = [cell_row == float(group * 8 + i) for i in range(8)]
        surface = jnp.zeros((128, 128), F32)
        for piece in (hi, low):
            stacked = jnp.concatenate([jnp.where(m, piece, 0.0) for m in masks]).astype(BF16)
            surface = surface + jnp.dot(stacked, hot[...], preferred_element_type=F32)
        x = group // 2
        for i in range(8):
            y = (group % 2) * 8 + i
            forcing[x, y] = exc[x, y] + surface[i * EH : (i + 1) * EH]

    def rows(y, carry):
        for x in range(LX):
            pot[x, y] = relaxed(pp, 2, 2, nu, scale, forcing[x, y], x, y, lane)
        return carry

    lax.fori_loop(0, LY, rows, 0)
    xlo[...] = pot[0:1].astype(xlo.dtype)
    xhi[...] = pot[LX - 1 : LX].astype(xhi.dtype)
    ylo[...] = pot[:, 0:1].astype(ylo.dtype)
    yhi[...] = pot[:, LY - 1 : LY].astype(yhi.dtype)


def sweep_two_body(pot_in, xl, xh, yl, yh, nu, scale, forcing, pot, p):
    p[1:5, 1:17] = pot_in[...]
    p[0:1, 1:17] = xl[...].astype(F32)
    p[5:6, 1:17] = xh[...].astype(F32)
    p[1:5, 0:1] = yl[...].astype(F32)
    p[1:5, 17:18] = yh[...].astype(F32)
    lane = lane_iota()

    def rows(y, carry):
        for x in range(LX):
            pot[x, y] = relaxed(p, 1, 1, nu, scale, forcing[x, y], x, y, lane)
        return carry

    lax.fori_loop(0, LY, rows, 0)


def gather_traces(pot, hot, rows_ref, weight_ref, msg):
    nt = (((1,), (1,)), ((), ()))
    taken = jnp.zeros((512, 128), F32)
    for group in range(8):
        x, y = group // 2, (group % 2) * 8
        block = pot[x, y : y + 8].reshape(128, LZ)
        value = jnp.zeros((512, 128), F32)
        for piece in split3(block):
            value = value + lax.dot_general(
                hot[...], piece.astype(BF16), nt, preferred_element_type=F32
            )
        taken = jnp.where(rows_ref[...] == float(group * 8), value, taken)
    taken = taken * weight_ref[...]
    for shift_by in (64, 32, 16):
        taken = taken + pltpu.roll(taken, shift_by, 1)
    lane_group = lax.broadcasted_iota(jnp.int32, (128, 128), 1) // EH
    out = jnp.zeros((128, 128), F32)
    for q in range(4):
        out = jnp.where(lane_group == q, taken[q * 128 : (q + 1) * 128], out)
    msg[...] = out


def tables_gather_body(
    flags_ref, own, other, pot, msg, hot, rows_ref, weight_ref, owner_hot, lanes_ref
):
    swapped = flags_ref[4] == 1
    first = jnp.where(swapped, other[...], own[...])
    second = jnp.where(swapped, own[...], other[...])
    lane = lax.broadcasted_iota(jnp.int32, (128, 128), 1)
    lane_f = lane.astype(F32)
    group_f = (lane // EH).astype(F32)

    def column(row):
        return jnp.broadcast_to(row, (128, 128)).T

    for vl, table in enumerate((first, second)):
        for wl in range(2):
            q = vl * 2 + wl
            at = slice(q * 128, (q + 1) * 128)
            cell_row = jnp.floor(table[wl : wl + 1] * (1.0 / LZ))
            depth = table[wl : wl + 1] - cell_row * LZ
            cell_row = cell_row + 32.0 * vl
            lanes_ref[:, at] = jnp.concatenate(
                [cell_row, table[2 + wl : 3 + wl], jnp.zeros((6, 128), F32)]
            )
            hot[at, :] = jnp.where(column(depth) == lane_f, 1.0, 0.0).astype(BF16)
            rows_ref[at, :] = column(cell_row) - group_f
            weight_ref[at, :] = column(table[2 + wl : 3 + wl])
            owned = (first, second)[wl][4 + vl : 5 + vl]
            owner_hot[at, :] = jnp.where(column(owned) == lane_f, 1.0, 0.0).astype(BF16)
    gather_traces(pot, hot, rows_ref, weight_ref, msg)


def sweep_two_gather_body(
    pot_in, xl, xh, yl, yh, nu, scale, forcing, hot, rows_ref, weight_ref, pot, msg, p
):
    sweep_two_body(pot_in, xl, xh, yl, yh, nu, scale, forcing, pot, p)
    gather_traces(pot, hot, rows_ref, weight_ref, msg)


def shift(value, axes, count, step):
    pairs = [(i, i + step) for i in range(count) if 0 <= i + step < count]
    return lax.ppermute(value, axes, pairs)


def swap_h(value):
    return lax.ppermute(value, "h", [(0, 1), (1, 0)])


def by_h(h, own, other):
    return jnp.where(h == 0, jnp.concatenate([own, other]), jnp.concatenate([other, own]))


def halved(value, h):
    turned = value.transpose(1, 2, 0, 3)
    low, high = turned[:, :, :EH], turned[:, :, EH:]
    return jnp.where(h == 0, low, high), jnp.where(h == 0, high, low)


def per_device(
    excitation,
    start,
    material,
    face_cell,
    face_count,
    face_weight,
    slot_panel,
    target_points,
    source_points,
):
    h = lax.axis_index("h")
    plane = lax.axis_index(PLANE)
    row = lax.axis_index(ROW)
    flags = jnp.stack(
        [plane == 0, plane == NXY - 1, row == 0, row == 7, h == 1, h == 1, h == 1, h == 1]
    ).astype(jnp.int32)

    rank = jnp.arange(4, dtype=jnp.int32)[None, :]
    weight = jnp.where(
        rank < face_count.reshape(64, 1), face_weight.reshape(64, 4), 0.0
    ).reshape(256)
    tables = jnp.stack(
        [face_cell.reshape(256).astype(F32), weight, slot_panel.reshape(256).astype(F32)]
    )
    tables = tables.reshape(3, 32, 2, 4).transpose(0, 2, 1, 3).reshape(6, 128)
    tables = jnp.concatenate([tables, jnp.zeros((2, 128), F32)])
    keep, give = halved(start, h)
    got = swap_h(
        jnp.concatenate(
            [
                give.reshape(512, 128),
                tables,
                target_points.reshape(24, 128),
                material.reshape(32, 128).astype(F32),
            ]
        )
    )
    exc_keep, exc_give = halved(excitation, h)
    exc_got = swap_h(exc_give)
    k0, turned = kernel_matrix(target_points, source_points)

    pot = by_h(h, keep, got[:512].reshape(2, LY, EH, LZ))
    mats = by_h(h, material.astype(F32), got[544:576].reshape(2, LY, LZ))
    msg, hot, rows_col, weights_col, owner_hot, lanes = call(
        tables_gather_body,
        (
            sds((128, 128)),
            sds((512, 128), BF16),
            sds((512, 128)),
            sds((512, 128)),
            sds((512, 128), BF16),
            sds((8, 512)),
        ),
        (flags, tables, got[512:520], pot),
        smem=(0,),
    )
    their_targets = got[520:544].reshape(3, 1024)
    exc = by_h(h, exc_keep, exc_got)

    rims = None
    for outer_index in range(ITERS):
        arrived = lax.all_to_all(msg.reshape(NXY, 4, 128), PLANE, 0, 0, tiled=True)
        dens = call(
            density_body, sds((NXY, 2 * EH, 128), BF16), (arrived.reshape(128, 128), owner_hot)
        )
        dens = lax.all_to_all(dens, PLANE, 0, 0, tiled=True)

        coarse = pot.astype(BF16)
        up, down = coarse[2:4].reshape(512, 128), coarse[0:2].reshape(512, 128)
        if outer_index == 0:
            up = jnp.concatenate([up, mats[3].astype(BF16)])
            down = jnp.concatenate([down, mats[0].astype(BF16)])
        xl = shift(up, PLANE, NXY, 1)
        xh = shift(down, PLANE, NXY, -1)
        xl_pot = xl[:512].reshape(2, LY, EH, LZ)
        xh_pot = xh[:512].reshape(2, LY, EH, LZ)

        def side(part):
            rows = jnp.concatenate([xl_pot[1:2, part], coarse[:, part], xh_pot[0:1, part]])
            return rows.reshape(6 * 2 * EH, LZ)

        up, down = side(slice(14, 16)), side(slice(0, 2))
        if outer_index == 0:
            pad = jnp.zeros((12, 128), BF16)
            up = jnp.concatenate([up, mats[:, 15].astype(BF16), pad])
            down = jnp.concatenate([down, mats[:, 0].astype(BF16), pad])
        yl = shift(up, ROW, 8, 1)
        yh = shift(down, ROW, 8, -1)
        if outer_index == 0:
            rims = tuple(v.astype(F32) for v in (xl[512:], xh[512:], yl[192:], yh[192:]))
        padded, nu, scale = call(
            nu_body,
            (sds((8, 20, EH, LZ)), sds((6, 18, EH, LZ)), sds((LX, LY, EH, LZ))),
            (
                flags,
                pot,
                xl_pot,
                xh_pot,
                yl[:192].reshape(6, 2, EH, LZ),
                yh[:192].reshape(6, 2, EH, LZ),
                mats,
                *rims,
            ),
            smem=(0,),
        )

        parts = partial_flux(dens, their_targets, k0, turned)
        parts = lax.all_to_all(parts, ROW, 0, 0, tiled=True)
        flux, slots = call(
            owner_body, (sds((2, EH, 128)), sds((128, 128))), (flags, parts, owner_hot), smem=(0,)
        )
        back = lax.all_to_all(slots.reshape(NXY, 4, 128), PLANE, 0, 0, tiled=True)

        brick = (LX, LY, EH, LZ)
        pot, forcing, xlo, xhi, ylo, yhi = call(
            sweep_one_body,
            (
                sds(brick),
                sds(brick),
                sds((1, LY, EH, LZ), BF16),
                sds((1, LY, EH, LZ), BF16),
                sds((LX, 1, EH, LZ), BF16),
                sds((LX, 1, EH, LZ), BF16),
            ),
            (back.reshape(128, 128), hot, lanes, exc, padded, nu, scale),
        )
        xl1 = shift(xhi, PLANE, NXY, 1)
        xh1 = shift(xlo, PLANE, NXY, -1)
        yl1 = shift(yhi, ROW, 8, 1)
        yh1 = shift(ylo, ROW, 8, -1)
        operands = (pot, xl1, xh1, yl1, yh1, nu, scale, forcing)
        scratch = (pltpu.VMEM((6, 18, EH, LZ), F32),)
        if outer_index < ITERS - 1:
            pot, msg = call(
                sweep_two_gather_body,
                (sds(brick), sds((128, 128))),
                operands + (hot, rows_col, weights_col),
                scratch=scratch,
            )
        else:
            pot = call(sweep_two_body, sds(brick), operands, scratch=scratch)

    lower, upper = pot[0:2], pot[2:4]
    mine = jnp.where(h == 0, lower, upper)
    theirs = jnp.where(h == 0, upper, lower)
    final = swap_h(jnp.concatenate([theirs.reshape(512, 128), flux[1]]))
    theirs = final[:512].reshape(2, LY, EH, LZ)
    out = jnp.where(
        h == 0, jnp.concatenate([mine, theirs], axis=2), jnp.concatenate([theirs, mine], axis=2)
    )
    flux_out = by_h(h, flux[0], final[512:])
    return out.transpose(2, 0, 1, 3), flux_out


def solution(mesh):
    fine = Mesh(mesh.devices.reshape(4, 8, 2, 4, 2), ("x", "y", "h", "z", "c"))
    vol, src = ("x", "y", "h"), ("z", "c")
    return jax.shard_map(
        per_device,
        mesh=fine,
        in_specs=(
            P(None, vol, src, None),
            P(None, vol, src, None),
            P(vol, src, None),
            P(vol, src, None),
            P(vol, src, None),
            P(vol, src, None),
            P(vol, src, None),
            P(None, vol),
            P(None, src),
        ),
        out_specs=(P(None, vol, src, None), P(None, vol + src)),
        check_vma=False,
    )
```

time: 967 us -> 277 us (0.29)
  blocking collectives: 437 us -> 0 us
  waiting for transfers between devices: 324 us -> 72.5 us
  Pallas kernels: 0 us -> 65.3 us
  matrix products: 29.4 us -> 0 us
  other arithmetic: 29.5 us -> 3.85 us
  between operations: 15.1 us -> 1.48 us
  starting transfers between devices: 98.3 us -> 111 us
  local copies, waits for them, and re-layouts: 30.3 us -> 18.2 us
    all_gather x2 -> x0, blocking collectives: 412 us -> none  [per_device(): block_piece = lax.all_gather(density, 'vol', axis=1, tiled=True)]
    psum x2 -> x0, waiting for transfers between devices: 178 us -> none  [per_device(): whole_sum = lax.psum(partial_flux, 'src')]
    ppermute x24 -> x19, waiting for transfers between devices: 129 us -> 41.6 us  [the longest x3 27.7 us: swap_h(): return lax.ppermute(value, 'h', [(0, 1), (1, 0)])]
    pallas_call x0 -> x14, Pallas kernels: none -> 65.3 us  [the longest x2 28.7 us: partial_flux(): pl.pallas_call(flux_body, grid=(8,), out_shape=sds((8, 2, EH, 128)), in_s...]
    dot_general x20 -> x0, matrix products: 29.4 us -> none  [the longest x16 27.6 us: one_step(): jnp.einsum('en,tn->et', segment, kernel, preferred_element_type=jnp.float32)]
    all_to_all x1 -> x0, blocking collectives: 25.7 us -> none  [per_device(): lax.all_to_all(per_slot.T.reshape(vol_count, capacity * exc_count), 'vol'...]
    all_to_all x3 -> x8, starting transfers between devices: 39.4 us -> 53.7 us  [the longest x2 22.7 us: per_device(): arrived = lax.all_to_all(msg.reshape(NXY, 4, 128), PLANE, 0, 0, tiled=True)]
    slice x25 -> x19, local copies, waits for them, and re-layouts: 15.5 us -> 1.4 us  [the longest x1 0.63 us: per_device(): yh[:192].reshape(6, 2, EH, LZ)]
  transfers between devices with their start and end apart: 29 -> 27, of which waited for: 17 -> 14; matrix products, arithmetic and copies ran while one was open for 6% -> 3% of each run, Pallas kernels for 0% -> 19%
where the time goes in v1:
time: 277 us; the launch traced here: 272 us
  starting transfers between devices  111 us (40%)
  waiting for transfers between devices  72.5 us (26%)
  Pallas kernels  65.3 us (24%)
  local copies, waits for them, and re-layouts  18.2 us (7%)
  other arithmetic  3.85 us (1%)
    ppermute x16, starting transfers between devices, shift(): return lax.ppermute(value, axes, pairs)  41.5 us
    pallas_call x2, Pallas kernels, partial_flux(): pl.pallas_call(flux_body, grid=(8,), out_shape=sds((8, 2, EH, 128)), in_s...  28.7 us
    ppermute x3, waiting for transfers between devices, swap_h(): return lax.ppermute(value, 'h', [(0, 1), (1, 0)])  27.7 us
    pallas_call x11, Pallas kernels, call(): pl.pallas_call(body, out_shape=out_shape, in_specs=[SM if i in smem else...  26.5 us
    all_to_all x2, starting transfers between devices, per_device(): arrived = lax.all_to_all(msg.reshape(NXY, 4, 128), PLANE, 0, 0, tiled=True)  22.7 us
    all_to_all x2, waiting for transfers between devices, per_device(): arrived = lax.all_to_all(msg.reshape(NXY, 4, 128), PLANE, 0, 0, tiled=True)  17.7 us
    ppermute x3, starting transfers between devices, swap_h(): return lax.ppermute(value, 'h', [(0, 1), (1, 0)])  15.7 us
    unnamed x57, local copies, waits for them, and re-layouts  14.9 us
  transfers between devices with their start and end apart: 27, of which 14 were waited for; matrix products, arithmetic and copies ran while one was open for 3% of the time, Pallas kernels for 19%

profile of v1, /device:TPU:1, one launch (start us, length us, event | category | flops | bytes accessed | tf_op | source)
XLA Modules:
  0.0 272.3 jit_solution(2148514997029989189)
XLA Ops:
  2.2 11.5 %collective-permute-start.1 = (f32[2,16,16,128]{3,2,1,0:T(8,128)S(1)}, f32[2,16,16,128]{3,2,1,0:T(8,128)S(1)}, u32[]{:S(2)}, u32[]{:S(2)}) collective-permute-start(f32[2,16,16,128]{3,2,1,0:T(8,128)S(1)} %get-tuple-element.79), channel_id=1, source_target_pairs={{0,8},{8,0},{1,9},{9,1},{2,10},{10,2},{3,11},{11,3},{4,12},{12,4},... | collective-permute-start | bytes 786440 | tf_op jit(solution)/shard_map/ppermute | solution.py:404
  19.8 10.2 %shard_map.106 = (bf16[8192,1024]{1,0:T(8,128)(2,1)}, bf16[8192,128]{1,0:T(8,128)(2,1)}) custom-call(f32[3,1024]{1,0:T(4,128)} %t_ref.1, f32[3,8192]{1,0:T(4,128)} %s_ref.1), custom_call_target="tpu_custom_call" | custom-call | flops 2000000000 | bytes 20000000 | tf_op jit(solution)/shard_map/pallas_call | solution.py:87
  30.0 13.5 %collective-permute-done = f32[576,128]{1,0:T(8,128)S(1)} collective-permute-done((f32[576,128]{1,0:T(8,128)S(1)}, f32[576,128]{1,0:T(8,128)S(1)}, u32[]{:S(2)}, u32[]{:S(2)}) %collective-permute-start) | collective-permute-done | bytes 294944 | tf_op jit(solution)/shard_map/ppermute | solution.py:404
  44.5 3.1 %collective-permute-start.2 = (bf16[528,128]{1,0:T(8,128)(2,1)S(1)}, bf16[528,128]{1,0:T(8,128)(2,1)S(1)}, u32[]{:S(2)}, u32[]{:S(2)}) collective-permute-start(bf16[528,128]{1,0:T(8,128)(2,1)S(1)} %pad_maximum_fusion.1), channel_id=1, source_target_pairs={{0,16},{16,32},{32,48},{48,64},{64,80},{80,96},{96,112},{112,128},... | collective-permute-start | bytes 405512 | tf_op jit(solution)/shard_map/ppermute | solution.py:400
  52.6 11.7 %all-to-all-start = ((f32[32,4,128]{2,1,0:T(4,128)}), f32[32,4,128]{2,1,0:T(4,128)S(1)}, u32[]{:S(2)}, u32[]{:S(2)}) async-start(f32[32,4,128]{2,1,0:T(4,128)} %bitcast.10), calls=%async_computation | async-start | bytes 131072 | tf_op jit(solution)/shard_map/all_to_all | solution.py:479
  64.3 8.9 %all-to-all-done = f32[32,4,128]{2,1,0:T(4,128)S(1)} async-done(((f32[32,4,128]{2,1,0:T(4,128)}), f32[32,4,128]{2,1,0:T(4,128)S(1)}, u32[]{:S(2)}, u32[]{:S(2)}) %all-to-all-start) | async-done | bytes 65568 | tf_op jit(solution)/shard_map/all_to_all | solution.py:479
  74.1 3.9 %all-to-all-start.1 = ((bf16[32,32,128]{2,1,0:T(8,128)(2,1)}), bf16[32,32,128]{2,1,0:T(8,128)(2,1)S(1)}, u32[]{:S(2)}, u32[]{:S(2)}) async-start(bf16[32,32,128]{2,1,0:T(8,128)(2,1)} %shard_map.105), calls=%async_computation.1 | async-start | bytes 524288 | tf_op jit(solution)/shard_map/all_to_all | solution.py:483
  78.2 4.4 %collective-permute-start.5 = (bf16[208,128]{1,0:T(8,128)(2,1)S(1)}, bf16[208,128]{1,0:T(8,128)(2,1)S(1)}, u32[]{:S(2)}, u32[]{:S(2)}) collective-permute-start(bf16[208,128]{1,0:T(8,128)(2,1)S(1)} %get-tuple-element.104), channel_id=1, source_target_pairs={{1,0},{2,1},{3,2},{4,3},{5,4},{6,5},{7,6},{9,8},{10,9},{11,10},{12... | collective-permute-start | bytes 159752 | tf_op jit(solution)/shard_map/ppermute | solution.py:400
  84.5 3.1 %all-to-all-done.1.arr = bf16[32,32,128]{2,1,0:T(8,128)(2,1)S(1)} async-done(((bf16[32,32,128]{2,1,0:T(8,128)(2,1)}), bf16[32,32,128]{2,1,0:T(8,128)(2,1)S(1)}, u32[]{:S(2)}, u32[]{:S(2)}) %all-to-all-start.1) | async-done | bytes 262176 | tf_op jit(solution)/shard_map/all_to_all | solution.py:483
  88.3 14.3 %shard_map.107 = f32[8,2,16,128]{3,2,1,0:T(8,128)} custom-call(bf16[32,32,128]{2,1,0:T(8,128)(2,1)} %copy-done.16, f32[3,1024]{1,0:T(4,128)} %reshape.178.t_ref, bf16[8192,1024]{1,0:T(8,128)(2,1)} %get-tuple-element.35.k0_ref, bf16[8192,128]{1,0:T(8,128)(2,1)} %get-tuple-element.36.turned_ref), custom_call_target="tpu_custom_call" | custom-call | flops 4000000000 | bytes 20000000 | tf_op jit(solution)/shard_map/pallas_call | solution.py:155
  102.6 7.8 %all-to-all-start.2 = ((f32[8,2,16,128]{3,2,1,0:T(8,128)}), f32[8,2,16,128]{3,2,1,0:T(8,128)S(1)}, u32[]{:S(2)}, u32[]{:S(2)}) async-start(f32[8,2,16,128]{3,2,1,0:T(8,128)} %shard_map.107), calls=%async_computation.2 | async-start | bytes 262144 | tf_op jit(solution)/shard_map/all_to_all | solution.py:525
  112.3 4.0 %all-to-all-done.2.parts_ref = f32[8,2,16,128]{3,2,1,0:T(8,128)S(1)} async-done(((f32[8,2,16,128]{3,2,1,0:T(8,128)}), f32[8,2,16,128]{3,2,1,0:T(8,128)S(1)}, u32[]{:S(2)}, u32[]{:S(2)}) %all-to-all-start.2) | async-done | bytes 131104 | tf_op jit(solution)/shard_map/all_to_all | solution.py:525
  117.8 4.5 %all-to-all-start.3 = ((f32[32,4,128]{2,1,0:T(4,128)}), f32[32,4,128]{2,1,0:T(4,128)}, u32[]{:S(2)}, u32[]{:S(2)}) async-start(f32[32,4,128]{2,1,0:T(4,128)} %bitcast.12), calls=%async_computation.3 | async-start | bytes 131072 | tf_op jit(solution)/shard_map/all_to_all | solution.py:529
  125.3 3.9 %shard_map.109 = (f32[8,20,16,128]{3,2,1,0:T(8,128)S(1)}, f32[6,18,16,128]{3,2,1,0:T(8,128)S(1)}, f32[4,16,16,128]{3,2,1,0:T(8,128)S(1)}) custom-call(s32[8]{0:T(128)S(1)} %copy-done.14, f32[4,16,16,128]{3,2,1,0:T(8,128)S(1)} %get-tuple-element.73.pot, bf16[2,16,16,128]{3,2,1,0:T(8,128)(2,1)S(1)} %bitcast.62, bf16[2,16,16,128]{3,2,1,0:T(8,128)(2,1)S(1)} %bitcast.64, ...), custom_call_target="tpu_custom_call" | custom-call | flops 2000000 | bytes 2000000 | tf_op jit(solution)/shard_map/pallas_call | solution.py:33
  133.2 3.3 %shard_map.110 = (f32[4,16,16,128]{3,2,1,0:T(8,128)S(1)}, f32[4,16,16,128]{3,2,1,0:T(8,128)S(1)}, bf16[1,16,16,128]{3,2,1,0:T(8,128)(2,1)S(1)}, bf16[1,16,16,128...) custom-call(f32[128,128]{1,0:T(8,128)} %bitcast.13.arr, ...), custom_call_target="tpu_custom_call" | custom-call | flops 2000000 | bytes 2000000 | tf_op jit(solution)/shard_map/pallas_call | solution.py:33
  140.6 4.5 %collective-permute-start.8 = (bf16[4,1,16,128]{3,2,1,0:T(8,128)(2,1)S(1)}, bf16[4,1,16,128]{3,2,1,0:T(8,128)(2,1)S(1)}, u32[]{:S(2)}, u32[]{:S(2)}) collective-permute-start(bf16[4,1,16,128]{3,2,1,0:T(8,128)(2,1)S(1)} %get-tuple-element.46), channel_id=1, source_target_pairs={{0,1},{1,2},{2,3},{3,4},{4,5},{5,6},{6,7},{8,9},{9,10},{10,11},{11... | collective-permute-start | bytes 49160 | tf_op jit(solution)/shard_map/ppermute | solution.py:400
  147.1 3.1 %collective-permute-done.9.yh = bf16[4,1,16,128]{3,2,1,0:T(8,128)(2,1)S(1)} collective-permute-done((bf16[4,1,16,128]{3,2,1,0:T(8,128)(2,1)S(1)}, bf16[4,1,16,128]{3,2,1,0:T(8,128)(2,1)S(1)}, u32[]{:S(2)}, u32[]{:S(2)}) %collective-permute-start.9) | collective-permute-done | bytes 16416 | tf_op jit(solution)/shard_map/ppermute | solution.py:400
  150.2 3.6 %shard_map.111 = (f32[4,16,16,128]{3,2,1,0:T(8,128)S(1)}, f32[128,128]{1,0:T(8,128)}) custom-call(f32[4,16,16,128]{3,2,1,0:T(8,128)S(1)} %get-tuple-element.43.pot_in, bf16[1,16,16,128]{3,2,1,0:T(8,128)(2,1)S(1)} %collective-permute-done.6.xl, bf16[1,16,16,128]{3,2,1,0:T(8,128)(2,1)S(1)} %collective-permute-done.7.xh, ...), custom_call_target="tpu_custom_call" | custom-call | flops 2000000 | bytes 2000000 | tf_op jit(solution)/shard_map/pallas_call | solution.py:33
  153.8 11.0 %all-to-all-start.4 = ((f32[32,4,128]{2,1,0:T(4,128)}), f32[32,4,128]{2,1,0:T(4,128)S(1)}, u32[]{:S(2)}, u32[]{:S(2)}) async-start(f32[32,4,128]{2,1,0:T(4,128)} %bitcast.26), calls=%async_computation.4 | async-start | bytes 131072 | tf_op jit(solution)/shard_map/all_to_all | solution.py:479
  164.9 8.8 %all-to-all-done.4 = f32[32,4,128]{2,1,0:T(4,128)S(1)} async-done(((f32[32,4,128]{2,1,0:T(4,128)}), f32[32,4,128]{2,1,0:T(4,128)S(1)}, u32[]{:S(2)}, u32[]{:S(2)}) %all-to-all-start.4) | async-done | bytes 65568 | tf_op jit(solution)/shard_map/all_to_all | solution.py:479
  174.7 3.9 %all-to-all-start.5 = ((bf16[32,32,128]{2,1,0:T(8,128)(2,1)}), bf16[32,32,128]{2,1,0:T(8,128)(2,1)S(1)}, u32[]{:S(2)}, u32[]{:S(2)}) async-start(bf16[32,32,128]{2,1,0:T(8,128)(2,1)} %shard_map.112), calls=%async_computation.5 | async-start | bytes 524288 | tf_op jit(solution)/shard_map/all_to_all | solution.py:483
  178.6 3.0 %collective-permute-start.10 = (bf16[512,128]{1,0:T(8,128)(2,1)S(1)}, bf16[512,128]{1,0:T(8,128)(2,1)S(1)}, u32[]{:S(2)}, u32[]{:S(2)}) collective-permute-start(bf16[512,128]{1,0:T(8,128)(2,1)S(1)} %bitcast.88), channel_id=1, source_target_pairs={{0,16},{16,32},{32,48},{48,64},{64,80},{80,96},{96,112},{112,128},... | collective-permute-start | bytes 393224 | tf_op jit(solution)/shard_map/ppermute | solution.py:400
  183.1 3.7 %collective-permute-done.10 = bf16[512,128]{1,0:T(8,128)(2,1)S(1)} collective-permute-done((bf16[512,128]{1,0:T(8,128)(2,1)S(1)}, bf16[512,128]{1,0:T(8,128)(2,1)S(1)}, u32[]{:S(2)}, u32[]{:S(2)}) %collective-permute-start.10) | collective-permute-done | bytes 131104 | tf_op jit(solution)/shard_map/ppermute | solution.py:400
  186.8 3.7 %all-to-all-done.5.arr = bf16[32,32,128]{2,1,0:T(8,128)(2,1)S(1)} async-done(((bf16[32,32,128]{2,1,0:T(8,128)(2,1)}), bf16[32,32,128]{2,1,0:T(8,128)(2,1)S(1)}, u32[]{:S(2)}, u32[]{:S(2)}) %all-to-all-start.5) | async-done | bytes 262176 | tf_op jit(solution)/shard_map/all_to_all | solution.py:483
  191.2 14.3 %shard_map.113 = f32[8,2,16,128]{3,2,1,0:T(8,128)} custom-call(bf16[32,32,128]{2,1,0:T(8,128)(2,1)} %copy-done.17, f32[3,1024]{1,0:T(4,128)} %reshape.178.t_ref, bf16[8192,1024]{1,0:T(8,128)(2,1)} %get-tuple-element.35.k0_ref, bf16[8192,128]{1,0:T(8,128)(2,1)} %get-tuple-element.36.turned_ref), custom_call_target="tpu_custom_call" | custom-call | flops 4000000000 | bytes 20000000 | tf_op jit(solution)/shard_map/pallas_call | solution.py:155
  205.5 4.3 %all-to-all-start.6 = ((f32[8,2,16,128]{3,2,1,0:T(8,128)}), f32[8,2,16,128]{3,2,1,0:T(8,128)S(1)}, u32[]{:S(2)}, u32[]{:S(2)}) async-start(f32[8,2,16,128]{3,2,1,0:T(8,128)} %shard_map.113), calls=%async_computation.6 | async-start | bytes 262144 | tf_op jit(solution)/shard_map/all_to_all | solution.py:525
  209.9 3.6 %collective-permute-start.12 = (bf16[192,128]{1,0:T(8,128)(2,1)S(1)}, bf16[192,128]{1,0:T(8,128)(2,1)S(1)}, u32[]{:S(2)}, u32[]{:S(2)}) collective-permute-start(bf16[192,128]{1,0:T(8,128)(2,1)S(1)} %bitcast.90), channel_id=1, source_target_pairs={{0,1},{1,2},{2,3},{3,4},{4,5},{5,6},{6,7},{8,9},{9,10},{10,11},{11... | collective-permute-start | bytes 147464 | tf_op jit(solution)/shard_map/ppermute | solution.py:400
  217.1 6.6 %all-to-all-start.7 = ((f32[32,4,128]{2,1,0:T(4,128)}), f32[32,4,128]{2,1,0:T(4,128)S(1)}, u32[]{:S(2)}, u32[]{:S(2)}) async-start(f32[32,4,128]{2,1,0:T(4,128)} %bitcast.28), calls=%async_computation.7 | async-start | bytes 131072 | tf_op jit(solution)/shard_map/all_to_all | solution.py:529
  223.8 3.2 %collective-permute-start.13 = (bf16[192,128]{1,0:T(8,128)(2,1)S(1)}, bf16[192,128]{1,0:T(8,128)(2,1)S(1)}, u32[]{:S(2)}, u32[]{:S(2)}) collective-permute-start(bf16[192,128]{1,0:T(8,128)(2,1)S(1)} %bitcast.91), channel_id=1, source_target_pairs={{1,0},{2,1},{3,2},{4,3},{5,4},{6,5},{7,6},{9,8},{10,9},{11,10},{12... | collective-permute-start | bytes 147464 | tf_op jit(solution)/shard_map/ppermute | solution.py:400
  229.5 4.0 %shard_map.115 = (f32[8,20,16,128]{3,2,1,0:T(8,128)S(1)}, f32[6,18,16,128]{3,2,1,0:T(8,128)S(1)}, f32[4,16,16,128]{3,2,1,0:T(8,128)S(1)}) custom-call(s32[8]{0:T(128)S(1)} %copy-done.15, f32[4,16,16,128]{3,2,1,0:T(8,128)S(1)} %get-tuple-element.53.pot, bf16[2,16,16,128]{3,2,1,0:T(8,128)(2,1)S(1)} %bitcast.71, bf16[2,16,16,128]{3,2,1,0:T(8,128)(2,1)S(1)} %bitcast.73, ...), custom_call_target="tpu_custom_call" | custom-call | flops 2000000 | bytes 2000000 | tf_op jit(solution)/shard_map/pallas_call | solution.py:33
  248.0 4.1 %collective-permute-done.15.xh = bf16[1,16,16,128]{3,2,1,0:T(8,128)(2,1)S(1)} collective-permute-done((bf16[1,16,16,128]{3,2,1,0:T(8,128)(2,1)S(1)}, bf16[1,16,16,128]{3,2,1,0:T(8,128)(2,1)S(1)}, u32[]{:S(2)}, u32[]{:S(2)}) %collective-permute-start.15) | collective-permute-done | bytes 65568 | tf_op jit(solution)/shard_map/ppermute | solution.py:400
  256.3 14.2 %collective-permute-done.18 = f32[528,128]{1,0:T(8,128)S(1)} collective-permute-done((f32[528,128]{1,0:T(8,128)S(1)}, f32[528,128]{1,0:T(8,128)S(1)}, u32[]{:S(2)}, u32[]{:S(2)}) %collective-permute-start.18) | collective-permute-done | bytes 270368 | tf_op jit(solution)/shard_map/ppermute | solution.py:404
  (162 shorter events, 63.1 us)
Async XLA Ops:
  2.2 27.8 %collective-permute-start.1 = (f32[2,16,16,128]{3,2,1,0:T(8,128)S(1)}, f32[2,16,16,128]{3,2,1,0:T(8,128)S(1)}, u32[]{:S(2)}, u32[]{:S(2)}) collective-permute-start(f32[2,16,16,128]{3,2,1,0:T(8,128)S(1)} %get-tuple-element.79), channel_id=1, source_target_pairs={{0,8},{8,0},{1,9},{9,1},{2,10},{10,2},{3,11},{11,3},{4,12},{12,4},... | collective-permute-start | bytes 786440 | tf_op jit(solution)/shard_map/ppermute | solution.py:404
  17.6 26.0 %collective-permute-start = (f32[576,128]{1,0:T(8,128)S(1)}, f32[576,128]{1,0:T(8,128)S(1)}, u32[]{:S(2)}, u32[]{:S(2)}) collective-permute-start(f32[576,128]{1,0:T(8,128)S(1)} %concatenate.66), channel_id=1, source_target_pairs={{0,8},{8,0},{1,9},{9,1},{2,10},{10,2},{3,11},{11,3},{4,12},{12,4},... | collective-permute-start | bytes 884744 | tf_op jit(solution)/shard_map/ppermute | solution.py:404
  19.7 96.6 %copy-start.13 = (s32[8]{0:T(128)}, s32[8]{0:T(128)S(1)}, u32[]{:S(2)}) copy-start(s32[8]{0:T(128)S(1)} %convert_element_type.72.flags_ref) | copy-start | bytes 100
  44.5 33.5 %collective-permute-start.2 = (bf16[528,128]{1,0:T(8,128)(2,1)S(1)}, bf16[528,128]{1,0:T(8,128)(2,1)S(1)}, u32[]{:S(2)}, u32[]{:S(2)}) collective-permute-start(bf16[528,128]{1,0:T(8,128)(2,1)S(1)} %pad_maximum_fusion.1), channel_id=1, source_target_pairs={{0,16},{16,32},{32,48},{48,64},{64,80},{80,96},{96,112},{112,128},... | collective-permute-start | bytes 405512 | tf_op jit(solution)/shard_map/ppermute | solution.py:400
  48.3 29.7 %collective-permute-start.3 = (bf16[528,128]{1,0:T(8,128)(2,1)}, bf16[528,128]{1,0:T(8,128)(2,1)S(1)}, u32[]{:S(2)}, u32[]{:S(2)}) collective-permute-start(bf16[528,128]{1,0:T(8,128)(2,1)} %pad_maximum_fusion.2), channel_id=1, source_target_pairs={{16,0},{32,16},{48,32},{64,48},{80,64},{96,80},{112,96},{128,112},... | collective-permute-start | bytes 405512 | tf_op jit(solution)/shard_map/ppermute | solution.py:400
  52.6 20.5 %all-to-all-start = ((f32[32,4,128]{2,1,0:T(4,128)}), f32[32,4,128]{2,1,0:T(4,128)S(1)}, u32[]{:S(2)}, u32[]{:S(2)}) async-start(f32[32,4,128]{2,1,0:T(4,128)} %bitcast.10), calls=%async_computation | async-start | bytes 131072 | tf_op jit(solution)/shard_map/all_to_all | solution.py:479
  74.1 13.5 %all-to-all-start.1 = ((bf16[32,32,128]{2,1,0:T(8,128)(2,1)}), bf16[32,32,128]{2,1,0:T(8,128)(2,1)S(1)}, u32[]{:S(2)}, u32[]{:S(2)}) async-start(bf16[32,32,128]{2,1,0:T(8,128)(2,1)} %shard_map.105), calls=%async_computation.1 | async-start | bytes 524288 | tf_op jit(solution)/shard_map/all_to_all | solution.py:483
  78.2 32.3 %collective-permute-start.5 = (bf16[208,128]{1,0:T(8,128)(2,1)S(1)}, bf16[208,128]{1,0:T(8,128)(2,1)S(1)}, u32[]{:S(2)}, u32[]{:S(2)}) collective-permute-start(bf16[208,128]{1,0:T(8,128)(2,1)S(1)} %get-tuple-element.104), channel_id=1, source_target_pairs={{1,0},{2,1},{3,2},{4,3},{5,4},{6,5},{7,6},{9,8},{10,9},{11,10},{12... | collective-permute-start | bytes 159752 | tf_op jit(solution)/shard_map/ppermute | solution.py:400
  82.6 28.5 %collective-permute-start.4 = (bf16[208,128]{1,0:T(8,128)(2,1)S(1)}, bf16[208,128]{1,0:T(8,128)(2,1)S(1)}, u32[]{:S(2)}, u32[]{:S(2)}) collective-permute-start(bf16[208,128]{1,0:T(8,128)(2,1)S(1)} %get-tuple-element.105), channel_id=1, source_target_pairs={{0,1},{1,2},{2,3},{3,4},{4,5},{5,6},{6,7},{8,9},{9,10},{10,11},{11... | collective-permute-start | bytes 159752 | tf_op jit(solution)/shard_map/ppermute | solution.py:400
  102.6 13.6 %all-to-all-start.2 = ((f32[8,2,16,128]{3,2,1,0:T(8,128)}), f32[8,2,16,128]{3,2,1,0:T(8,128)S(1)}, u32[]{:S(2)}, u32[]{:S(2)}) async-start(f32[8,2,16,128]{3,2,1,0:T(8,128)} %shard_map.107), calls=%async_computation.2 | async-start | bytes 262144 | tf_op jit(solution)/shard_map/all_to_all | solution.py:525
  117.8 13.4 %all-to-all-start.3 = ((f32[32,4,128]{2,1,0:T(4,128)}), f32[32,4,128]{2,1,0:T(4,128)}, u32[]{:S(2)}, u32[]{:S(2)}) async-start(f32[32,4,128]{2,1,0:T(4,128)} %bitcast.12), calls=%async_computation.3 | async-start | bytes 131072 | tf_op jit(solution)/shard_map/all_to_all | solution.py:529
  136.5 13.7 %collective-permute-start.6 = (bf16[1,16,16,128]{3,2,1,0:T(8,128)(2,1)S(1)}, bf16[1,16,16,128]{3,2,1,0:T(8,128)(2,1)S(1)}, u32[]{:S(2)}, u32[]{:S(2)}) collective-permute-start(bf16[1,16,16,128]{3,2,1,0:T(8,128)(2,1)S(1)} %get-tuple-element.44), channel_id=1, source_target_pairs={{0,16},{16,32},{32,48},{48,64},{64,80},{80,96},{96,112},{112,128},... | collective-permute-start | bytes 196616 | tf_op jit(solution)/shard_map/ppermute | solution.py:400
  139.3 10.9 %collective-permute-start.7 = (bf16[1,16,16,128]{3,2,1,0:T(8,128)(2,1)S(1)}, bf16[1,16,16,128]{3,2,1,0:T(8,128)(2,1)S(1)}, u32[]{:S(2)}, u32[]{:S(2)}) collective-permute-start(bf16[1,16,16,128]{3,2,1,0:T(8,128)(2,1)S(1)} %get-tuple-element.45), channel_id=1, source_target_pairs={{16,0},{32,16},{48,32},{64,48},{80,64},{96,80},{112,96},{128,112},... | collective-permute-start | bytes 196616 | tf_op jit(solution)/shard_map/ppermute | solution.py:400
  140.6 6.5 %collective-permute-start.8 = (bf16[4,1,16,128]{3,2,1,0:T(8,128)(2,1)S(1)}, bf16[4,1,16,128]{3,2,1,0:T(8,128)(2,1)S(1)}, u32[]{:S(2)}, u32[]{:S(2)}) collective-permute-start(bf16[4,1,16,128]{3,2,1,0:T(8,128)(2,1)S(1)} %get-tuple-element.46), channel_id=1, source_target_pairs={{0,1},{1,2},{2,3},{3,4},{4,5},{5,6},{6,7},{8,9},{9,10},{10,11},{11... | collective-permute-start | bytes 49160 | tf_op jit(solution)/shard_map/ppermute | solution.py:400
  145.2 5.1 %collective-permute-start.9 = (bf16[4,1,16,128]{3,2,1,0:T(8,128)(2,1)S(1)}, bf16[4,1,16,128]{3,2,1,0:T(8,128)(2,1)S(1)}, u32[]{:S(2)}, u32[]{:S(2)}) collective-permute-start(bf16[4,1,16,128]{3,2,1,0:T(8,128)(2,1)S(1)} %get-tuple-element.47), channel_id=1, source_target_pairs={{1,0},{2,1},{3,2},{4,3},{5,4},{6,5},{7,6},{9,8},{10,9},{11,10},{12... | collective-permute-start | bytes 49160 | tf_op jit(solution)/shard_map/ppermute | solution.py:400
  153.8 19.9 %all-to-all-start.4 = ((f32[32,4,128]{2,1,0:T(4,128)}), f32[32,4,128]{2,1,0:T(4,128)S(1)}, u32[]{:S(2)}, u32[]{:S(2)}) async-start(f32[32,4,128]{2,1,0:T(4,128)} %bitcast.26), calls=%async_computation.4 | async-start | bytes 131072 | tf_op jit(solution)/shard_map/all_to_all | solution.py:479
  174.7 15.8 %all-to-all-start.5 = ((bf16[32,32,128]{2,1,0:T(8,128)(2,1)}), bf16[32,32,128]{2,1,0:T(8,128)(2,1)S(1)}, u32[]{:S(2)}, u32[]{:S(2)}) async-start(bf16[32,32,128]{2,1,0:T(8,128)(2,1)} %shard_map.112), calls=%async_computation.5 | async-start | bytes 524288 | tf_op jit(solution)/shard_map/all_to_all | solution.py:483
  178.6 8.2 %collective-permute-start.10 = (bf16[512,128]{1,0:T(8,128)(2,1)S(1)}, bf16[512,128]{1,0:T(8,128)(2,1)S(1)}, u32[]{:S(2)}, u32[]{:S(2)}) collective-permute-start(bf16[512,128]{1,0:T(8,128)(2,1)S(1)} %bitcast.88), channel_id=1, source_target_pairs={{0,16},{16,32},{32,48},{48,64},{64,80},{80,96},{96,112},{112,128},... | collective-permute-start | bytes 393224 | tf_op jit(solution)/shard_map/ppermute | solution.py:400
  181.6 28.2 %collective-permute-start.11 = (bf16[512,128]{1,0:T(8,128)(2,1)S(1)}, bf16[512,128]{1,0:T(8,128)(2,1)S(1)}, u32[]{:S(2)}, u32[]{:S(2)}) collective-permute-start(bf16[512,128]{1,0:T(8,128)(2,1)S(1)} %bitcast.87), channel_id=1, source_target_pairs={{16,0},{32,16},{48,32},{64,48},{80,64},{96,80},{112,96},{128,112},... | collective-permute-start | bytes 393224 | tf_op jit(solution)/shard_map/ppermute | solution.py:400
  186.8 28.8 %copy-start.15 = (s32[8]{0:T(128)S(1)}, s32[8]{0:T(128)}, u32[]{:S(2)}) copy-start(s32[8]{0:T(128)} %copy-done.13) | copy-start | bytes 100
  186.8 42.7 %copy-start.7 = (f32[16,128]{1,0:T(8,128)S(1)}, f32[16,128]{1,0:T(8,128)}, u32[]{:S(2)}) copy-start(f32[16,128]{1,0:T(8,128)} %slice_convert_fusion.myh) | copy-start | bytes 24580
  186.8 42.7 %copy-start.9 = (f32[16,128]{1,0:T(8,128)S(1)}, f32[16,128]{1,0:T(8,128)}, u32[]{:S(2)}) copy-start(f32[16,128]{1,0:T(8,128)} %copy-done.8) | copy-start | bytes 24580
  186.8 47.8 %copy-start.12 = (f32[8,512]{1,0:T(8,128)S(1)}, f32[8,512]{1,0:T(8,128)}, u32[]{:S(2)}) copy-start(f32[8,512]{1,0:T(8,128)} %copy-done.10) | copy-start | bytes 49156
  205.5 10.1 %all-to-all-start.6 = ((f32[8,2,16,128]{3,2,1,0:T(8,128)}), f32[8,2,16,128]{3,2,1,0:T(8,128)S(1)}, u32[]{:S(2)}, u32[]{:S(2)}) async-start(f32[8,2,16,128]{3,2,1,0:T(8,128)} %shard_map.113), calls=%async_computation.6 | async-start | bytes 262144 | tf_op jit(solution)/shard_map/all_to_all | solution.py:525
  209.9 17.1 %collective-permute-start.12 = (bf16[192,128]{1,0:T(8,128)(2,1)S(1)}, bf16[192,128]{1,0:T(8,128)(2,1)S(1)}, u32[]{:S(2)}, u32[]{:S(2)}) collective-permute-start(bf16[192,128]{1,0:T(8,128)(2,1)S(1)} %bitcast.90), channel_id=1, source_target_pairs={{0,1},{1,2},{2,3},{3,4},{4,5},{5,6},{6,7},{8,9},{9,10},{10,11},{11... | collective-permute-start | bytes 147464 | tf_op jit(solution)/shard_map/ppermute | solution.py:400
  217.1 17.4 %all-to-all-start.7 = ((f32[32,4,128]{2,1,0:T(4,128)}), f32[32,4,128]{2,1,0:T(4,128)S(1)}, u32[]{:S(2)}, u32[]{:S(2)}) async-start(f32[32,4,128]{2,1,0:T(4,128)} %bitcast.28), calls=%async_computation.7 | async-start | bytes 131072 | tf_op jit(solution)/shard_map/all_to_all | solution.py:529
  223.8 5.7 %collective-permute-start.13 = (bf16[192,128]{1,0:T(8,128)(2,1)S(1)}, bf16[192,128]{1,0:T(8,128)(2,1)S(1)}, u32[]{:S(2)}, u32[]{:S(2)}) collective-permute-start(bf16[192,128]{1,0:T(8,128)(2,1)S(1)} %bitcast.91), channel_id=1, source_target_pairs={{1,0},{2,1},{3,2},{4,3},{5,4},{6,5},{7,6},{9,8},{10,9},{11,10},{12... | collective-permute-start | bytes 147464 | tf_op jit(solution)/shard_map/ppermute | solution.py:400
  238.4 9.1 %collective-permute-start.16 = (bf16[4,1,16,128]{3,2,1,0:T(8,128)(2,1)S(1)}, bf16[4,1,16,128]{3,2,1,0:T(8,128)(2,1)S(1)}, u32[]{:S(2)}, u32[]{:S(2)}) collective-permute-start(bf16[4,1,16,128]{3,2,1,0:T(8,128)(2,1)S(1)} %get-tuple-element.60), channel_id=1, source_target_pairs={{0,1},{1,2},{2,3},{3,4},{4,5},{5,6},{6,7},{8,9},{9,10},{10,11},{11... | collective-permute-start | bytes 49160 | tf_op jit(solution)/shard_map/ppermute | solution.py:400
  241.3 6.2 %collective-permute-start.17 = (bf16[4,1,16,128]{3,2,1,0:T(8,128)(2,1)S(1)}, bf16[4,1,16,128]{3,2,1,0:T(8,128)(2,1)S(1)}, u32[]{:S(2)}, u32[]{:S(2)}) collective-permute-start(bf16[4,1,16,128]{3,2,1,0:T(8,128)(2,1)S(1)} %get-tuple-element.61), channel_id=1, source_target_pairs={{1,0},{2,1},{3,2},{4,3},{5,4},{6,5},{7,6},{9,8},{10,9},{11,10},{12... | collective-permute-start | bytes 49160 | tf_op jit(solution)/shard_map/ppermute | solution.py:400
  243.3 4.7 %collective-permute-start.14 = (bf16[1,16,16,128]{3,2,1,0:T(8,128)(2,1)S(1)}, bf16[1,16,16,128]{3,2,1,0:T(8,128)(2,1)S(1)}, u32[]{:S(2)}, u32[]{:S(2)}) collective-permute-start(bf16[1,16,16,128]{3,2,1,0:T(8,128)(2,1)S(1)} %get-tuple-element.58), channel_id=1, source_target_pairs={{0,16},{16,32},{32,48},{48,64},{64,80},{80,96},{96,112},{112,128},... | collective-permute-start | bytes 196616 | tf_op jit(solution)/shard_map/ppermute | solution.py:400
  246.2 5.9 %collective-permute-start.15 = (bf16[1,16,16,128]{3,2,1,0:T(8,128)(2,1)S(1)}, bf16[1,16,16,128]{3,2,1,0:T(8,128)(2,1)S(1)}, u32[]{:S(2)}, u32[]{:S(2)}) collective-permute-start(bf16[1,16,16,128]{3,2,1,0:T(8,128)(2,1)S(1)} %get-tuple-element.59), channel_id=1, source_target_pairs={{16,0},{32,16},{48,32},{64,48},{80,64},{96,80},{112,96},{128,112},... | collective-permute-start | bytes 196616 | tf_op jit(solution)/shard_map/ppermute | solution.py:400
  253.9 16.5 %collective-permute-start.18 = (f32[528,128]{1,0:T(8,128)S(1)}, f32[528,128]{1,0:T(8,128)S(1)}, u32[]{:S(2)}, u32[]{:S(2)}) collective-permute-start(f32[528,128]{1,0:T(8,128)S(1)} %pad_maximum_fusion), channel_id=1, source_target_pairs={{0,8},{8,0},{1,9},{9,1},{2,10},{10,2},{3,11},{11,3},{4,12},{12,4},... | collective-permute-start | bytes 811016 | tf_op jit(solution)/shard_map/ppermute | solution.py:404
  (20 other events, 111.8 us)

commit v2 on v1

--- a/solution.py
+++ b/solution.py
@@ -123,7 +123,11 @@
         msg[peer] = out
 
 
-def flux_body(arr, t_ref, k0_ref, turned_ref, out_ref, aug_ref, acc_ref):
+FLUX_STEPS = 4
+FLUX_ROWS = 8192 // FLUX_STEPS
+
+
+def flux_body(arr, t_ref, ka, kb, kc, kd, turned_ref, out_ref, aug_ref, acc_ref):
     step = pl.program_id(0)
 
     @pl.when(step == 0)
@@ -131,18 +135,26 @@
         aug_ref[...] = augmented(t_ref[...], True).astype(BF16)
         acc_ref[...] = jnp.zeros_like(acc_ref)
 
-    totals = [acc_ref[0], acc_ref[1]]
-    for i in range(4):
-        at = slice(i * 256, (i + 1) * 256)
-        dens = jnp.concatenate([arr[i, :EH], arr[i, EH:]], axis=1)
-        dist_sq = jnp.dot(turned_ref[at, :], aug_ref[...], preferred_element_type=F32)
+    pieces = []
+    for i in range(FLUX_ROWS // 256):
+        pieces += [arr[i, :EH], arr[i, EH:]]
+    dens = jnp.concatenate(pieces, axis=1)
+    depth = FLUX_ROWS // 4
+    for c in range(2):
+        at = slice(c * 512, (c + 1) * 512)
+        dist_sq = jnp.dot(turned_ref[...], aug_ref[:, at], preferred_element_type=F32)
         k1 = lax.rsqrt(dist_sq).astype(BF16)
-        totals[0] = totals[0] + jnp.dot(dens, k0_ref[at, :], preferred_element_type=F32)
-        totals[1] = totals[1] + jnp.dot(dens, k1, preferred_element_type=F32)
-    for half in range(2):
-        acc_ref[half] = totals[half]
-
-    @pl.when(step == 7)
+        acc_ref[1, :, at] += jnp.dot(dens, k1, preferred_element_type=F32)
+        total = acc_ref[0, :, at]
+        for part, k_ref in enumerate((ka, kb, kc, kd)):
+            total = total + jnp.dot(
+                dens[:, part * depth : (part + 1) * depth],
+                k_ref[:, at],
+                preferred_element_type=F32,
+            )
+        acc_ref[0, :, at] = total
+
+    @pl.when(step == FLUX_STEPS - 1)
     def _():
         for half in range(2):
             for part in range(8):
@@ -151,16 +163,20 @@
                 )
 
 
+def stored_part(part):
+    return pl.BlockSpec((FLUX_ROWS // 4, 1024), lambda i: (i * 4 + part, 0))
+
+
 def partial_flux(arrived, targets, k0, turned):
     return pl.pallas_call(
         flux_body,
-        grid=(8,),
+        grid=(FLUX_STEPS,),
         out_shape=sds((8, 2, EH, 128)),
         in_specs=[
-            pl.BlockSpec((4, 2 * EH, 128), lambda i: (i, 0, 0)),
+            pl.BlockSpec((FLUX_ROWS // 256, 2 * EH, 128), lambda i: (i, 0, 0)),
             pl.BlockSpec((3, 1024), lambda i: (0, 0)),
-            pl.BlockSpec((1024, 1024), lambda i: (i, 0)),
-            pl.BlockSpec((1024, 128), lambda i: (i, 0)),
+            *[stored_part(part) for part in range(4)],
+            pl.BlockSpec((FLUX_ROWS, 128), lambda i: (i, 0)),
         ],
         out_specs=pl.BlockSpec((8, 2, EH, 128), lambda i: (0, 0, 0, 0)),
         scratch_shapes=[pltpu.VMEM((128, 1024), BF16), pltpu.VMEM((2, EH, 1024), F32)],
@@ -168,7 +184,7 @@
         cost_estimate=pl.CostEstimate(
             flops=4_000_000_000, bytes_accessed=20_000_000, transcendentals=8_400_000
         ),
-    )(arrived, targets, k0, turned)
+    )(arrived, targets, k0, k0, k0, k0, turned)
 
 
 def owner_body(flags_ref, parts_ref, owner_hot, flux_ref, msg_ref):
@@ -211,7 +227,7 @@
 
 
 def nu_body(
-    flags_ref, pot, xl, xh, yl, yh, mo, mxl, mxh, myl, myh, pp, nu, scale
+    flags_ref, pot, xl, xh, yl, yh, mo, mxl, mxh, myl, myh, nu, scale, pp
 ):
     pp[2:6, 2:18] = pot[...]
     pp[0:2, 2:18] = xl[...].astype(F32)
@@ -287,10 +303,16 @@
 
 
 def sweep_one_body(
-    arr, hot, lanes_ref, exc, pp, nu, scale, pot, forcing, xlo, xhi, ylo, yhi
+    arr, hot, lanes_ref, exc, pot_in, xl, xh, yl, yh, nu, scale,
+    pot, forcing, xlo, xhi, ylo, yhi, p,
 ):
     turned = arr[...].T
     lane = lane_iota()
+    p[1:5, 1:17] = pot_in[...]
+    p[0:1, 1:17] = xl[1:2].astype(F32)
+    p[5:6, 1:17] = xh[0:1].astype(F32)
+    p[1:5, 0:1] = yl[1:5, 1:2].astype(F32)
+    p[1:5, 17:18] = yh[1:5, 0:1].astype(F32)
     slots = jnp.concatenate([turned[q * EH : (q + 1) * EH] for q in range(4)], axis=1)
     slots = slots * lanes_ref[1:2, :]
     hi = slots.astype(BF16).astype(F32)
@@ -309,7 +331,7 @@
 
     def rows(y, carry):
         for x in range(LX):
-            pot[x, y] = relaxed(pp, 2, 2, nu, scale, forcing[x, y], x, y, lane)
+            pot[x, y] = relaxed(p, 1, 1, nu, scale, forcing[x, y], x, y, lane)
         return carry
 
     lax.fori_loop(0, LY, rows, 0)
@@ -452,8 +474,6 @@
             ]
         )
     )
-    exc_keep, exc_give = halved(excitation, h)
-    exc_got = swap_h(exc_give)
     k0, turned = kernel_matrix(target_points, source_points)
 
     pot = by_h(h, keep, got[:512].reshape(2, LY, EH, LZ))
@@ -472,17 +492,21 @@
         smem=(0,),
     )
     their_targets = got[520:544].reshape(3, 1024)
-    exc = by_h(h, exc_keep, exc_got)
 
     rims = None
     for outer_index in range(ITERS):
+        msg, coarse = lax.optimization_barrier((msg, pot))
+        coarse = coarse.astype(BF16)
         arrived = lax.all_to_all(msg.reshape(NXY, 4, 128), PLANE, 0, 0, tiled=True)
         dens = call(
             density_body, sds((NXY, 2 * EH, 128), BF16), (arrived.reshape(128, 128), owner_hot)
         )
+        if outer_index == 0:
+            dens, late = lax.optimization_barrier((dens, excitation))
+            exc_keep, exc_give = halved(late, h)
+            exc = by_h(h, exc_keep, swap_h(exc_give))
         dens = lax.all_to_all(dens, PLANE, 0, 0, tiled=True)
 
-        coarse = pot.astype(BF16)
         up, down = coarse[2:4].reshape(512, 128), coarse[0:2].reshape(512, 128)
         if outer_index == 0:
             up = jnp.concatenate([up, mats[3].astype(BF16)])
@@ -505,20 +529,19 @@
         yh = shift(down, ROW, 8, -1)
         if outer_index == 0:
             rims = tuple(v.astype(F32) for v in (xl[512:], xh[512:], yl[192:], yh[192:]))
-        padded, nu, scale = call(
+        scratch = (pltpu.VMEM((6, 18, EH, LZ), F32),)
+        halos = (
+            xl_pot,
+            xh_pot,
+            yl[:192].reshape(6, 2, EH, LZ),
+            yh[:192].reshape(6, 2, EH, LZ),
+        )
+        nu, scale = call(
             nu_body,
-            (sds((8, 20, EH, LZ)), sds((6, 18, EH, LZ)), sds((LX, LY, EH, LZ))),
-            (
-                flags,
-                pot,
-                xl_pot,
-                xh_pot,
-                yl[:192].reshape(6, 2, EH, LZ),
-                yh[:192].reshape(6, 2, EH, LZ),
-                mats,
-                *rims,
-            ),
+            (sds((6, 18, EH, LZ)), sds((LX, LY, EH, LZ))),
+            (flags, pot, *halos, mats, *rims),
             smem=(0,),
+            scratch=(pltpu.VMEM((8, 20, EH, LZ), F32),),
         )
 
         parts = partial_flux(dens, their_targets, k0, turned)
@@ -539,14 +562,14 @@
                 sds((LX, 1, EH, LZ), BF16),
                 sds((LX, 1, EH, LZ), BF16),
             ),
-            (back.reshape(128, 128), hot, lanes, exc, padded, nu, scale),
+            (back.reshape(128, 128), hot, lanes, exc, pot, *halos, nu, scale),
+            scratch=scratch,
         )
         xl1 = shift(xhi, PLANE, NXY, 1)
         xh1 = shift(xlo, PLANE, NXY, -1)
         yl1 = shift(yhi, ROW, 8, 1)
         yh1 = shift(ylo, ROW, 8, -1)
         operands = (pot, xl1, xh1, yl1, yh1, nu, scale, forcing)
-        scratch = (pltpu.VMEM((6, 18, EH, LZ), F32),)
         if outer_index < ITERS - 1:
             pot, msg = call(
                 sweep_two_gather_body,
@@ -560,12 +583,21 @@
     lower, upper = pot[0:2], pot[2:4]
     mine = jnp.where(h == 0, lower, upper)
     theirs = jnp.where(h == 0, upper, lower)
-    final = swap_h(jnp.concatenate([theirs.reshape(512, 128), flux[1]]))
+    hi = lax.reduce_precision(flux[1], 8, 7)
+    final = swap_h(
+        jnp.concatenate(
+            [
+                theirs.reshape(512, 128).astype(BF16),
+                hi.astype(BF16),
+                (flux[1] - hi).astype(BF16),
+            ]
+        )
+    ).astype(F32)
     theirs = final[:512].reshape(2, LY, EH, LZ)
     out = jnp.where(
         h == 0, jnp.concatenate([mine, theirs], axis=2), jnp.concatenate([theirs, mine], axis=2)
     )
-    flux_out = by_h(h, flux[0], final[512:])
+    flux_out = by_h(h, flux[0], final[512:528] + final[528:544])
     return out.transpose(2, 0, 1, 3), flux_out
 
 

time: 277 us -> 258 us (0.931)
  waiting for transfers between devices: 72.5 us -> 57.5 us
  local copies, waits for them, and re-layouts: 18.2 us -> 9.64 us
  starting transfers between devices: 111 us -> 118 us
  Pallas kernels: 65.3 us -> 61.2 us
  other arithmetic: 3.85 us -> 7.37 us
    ppermute x3, waiting for transfers between devices: 27.7 us -> 9.37 us  [swap_h(): return lax.ppermute(value, 'h', [(0, 1), (1, 0)])]
    all_to_all x2, waiting for transfers between devices: 0.25 us -> 12.4 us  [per_device(): back = lax.all_to_all(slots.reshape(NXY, 4, 128), PLANE, 0, 0, tiled=True)]
    unnamed x57 -> x16, local copies, waits for them, and re-layouts: 14.9 us -> 6.55 us
    all_to_all x2, waiting for transfers between devices: 17.7 us -> 10 us  [per_device(): arrived = lax.all_to_all(msg.reshape(NXY, 4, 128), PLANE, 0, 0, tiled=True)]
    ppermute x16, starting transfers between devices: 41.5 us -> 48.9 us  [shift(): return lax.ppermute(value, axes, pairs)]
    all_to_all x2, waiting for transfers between devices: 6.78 us -> 0.7 us  [per_device(): dens = lax.all_to_all(dens, PLANE, 0, 0, tiled=True)]
    ppermute x16, waiting for transfers between devices: 13.9 us -> 19.6 us  [shift(): return lax.ppermute(value, axes, pairs)]
    all_to_all x2, starting transfers between devices: 11.2 us -> 16.8 us  [per_device(): back = lax.all_to_all(slots.reshape(NXY, 4, 128), PLANE, 0, 0, tiled=True)]
  transfers between devices with their start and end apart: 27 -> 27, of which waited for: 14 -> 11; matrix products, arithmetic and copies ran while one was open for 3% -> 1% of each run, Pallas kernels for 19% -> 13%
where the time goes in v2:
time: 258 us; the launch traced here: 255 us
  starting transfers between devices  118 us (46%)
  Pallas kernels  61.2 us (24%)
  waiting for transfers between devices  57.5 us (22%)
  local copies, waits for them, and re-layouts  9.64 us (4%)
  other arithmetic  7.37 us (3%)
    ppermute x16, starting transfers between devices, shift(): return lax.ppermute(value, axes, pairs)  48.9 us
    pallas_call x11, Pallas kernels, call(): pl.pallas_call(body, out_shape=out_shape, in_specs=[SM if i in smem else...  25.7 us
    pallas_call x2, Pallas kernels, partial_flux(): pl.pallas_call(flux_body, grid=(FLUX_STEPS,), out_shape=sds((8, 2, EH, 12...  25.3 us
    ppermute x16, waiting for transfers between devices, shift(): return lax.ppermute(value, axes, pairs)  19.6 us
    all_to_all x2, starting transfers between devices, per_device(): arrived = lax.all_to_all(msg.reshape(NXY, 4, 128), PLANE, 0, 0, tiled=True)  17.5 us
    ppermute x3, starting transfers between devices, swap_h(): return lax.ppermute(value, 'h', [(0, 1), (1, 0)])  17.1 us
    all_to_all x2, starting transfers between devices, per_device(): back = lax.all_to_all(slots.reshape(NXY, 4, 128), PLANE, 0, 0, tiled=True)  16.8 us
    all_to_all x2, waiting for transfers between devices, per_device(): back = lax.all_to_all(slots.reshape(NXY, 4, 128), PLANE, 0, 0, tiled=True)  12.4 us
  transfers between devices with their start and end apart: 27, of which 11 were waited for; matrix products, arithmetic and copies ran while one was open for 1% of the time, Pallas kernels for 13%

profile of v2, /device:TPU:1, one launch (start us, length us, event | category | flops | bytes accessed | tf_op | source)
XLA Modules:
  0.0 255.5 jit_solution(5096369579975463760)
XLA Ops:
  9.1 11.4 %collective-permute-start = (f32[576,128]{1,0:T(8,128)S(1)}, f32[576,128]{1,0:T(8,128)S(1)}, u32[]{:S(2)}, u32[]{:S(2)}) collective-permute-start(f32[576,128]{1,0:T(8,128)S(1)} %concatenate.66), channel_id=1, source_target_pairs={{0,8},{8,0},{1,9},{9,1},{2,10},{10,2},{3,11},{11,3},{4,12},{12,4},... | collective-permute-start | bytes 884744 | tf_op jit(solution)/shard_map/ppermute | solution.py:426
  20.8 10.2 %shard_map.106 = (bf16[8192,1024]{1,0:T(8,128)(2,1)}, bf16[8192,128]{1,0:T(8,128)(2,1)}) custom-call(f32[3,1024]{1,0:T(4,128)} %t_ref.1, f32[3,8192]{1,0:T(4,128)} %s_ref.1), custom_call_target="tpu_custom_call" | custom-call | flops 2000000000 | bytes 20000000 | tf_op jit(solution)/shard_map/pallas_call | solution.py:87
  35.1 9.7 %all-to-all-start = ((f32[32,4,128]{2,1,0:T(4,128)}), f32[32,4,128]{2,1,0:T(4,128)S(1)}, u32[]{:S(2)}, u32[]{:S(2)}) async-start(f32[32,4,128]{2,1,0:T(4,128)} %bitcast.10), calls=%async_computation | async-start | bytes 131072 | tf_op jit(solution)/shard_map/all_to_all | solution.py:500
  44.8 3.1 %collective-permute-start.2 = (bf16[528,128]{1,0:T(8,128)(2,1)S(1)}, bf16[528,128]{1,0:T(8,128)(2,1)S(1)}, u32[]{:S(2)}, u32[]{:S(2)}) collective-permute-start(bf16[528,128]{1,0:T(8,128)(2,1)S(1)} %pad_maximum_fusion.1), channel_id=1, source_target_pairs={{0,16},{16,32},{32,48},{48,64},{64,80},{80,96},{96,112},{112,128},... | collective-permute-start | bytes 405512 | tf_op jit(solution)/shard_map/ppermute | solution.py:422
  49.3 4.4 %all-to-all-done = f32[32,4,128]{2,1,0:T(4,128)S(1)} async-done(((f32[32,4,128]{2,1,0:T(4,128)}), f32[32,4,128]{2,1,0:T(4,128)S(1)}, u32[]{:S(2)}, u32[]{:S(2)}) %all-to-all-start) | async-done | bytes 65568 | tf_op jit(solution)/shard_map/all_to_all | solution.py:500
  54.6 6.9 %all-to-all-start.1 = ((bf16[32,32,128]{2,1,0:T(8,128)(2,1)}), bf16[32,32,128]{2,1,0:T(8,128)(2,1)S(1)}, u32[]{:S(2)}, u32[]{:S(2)}) async-start(bf16[32,32,128]{2,1,0:T(8,128)(2,1)} %shard_map.105), calls=%async_computation.1 | async-start | bytes 524288 | tf_op jit(solution)/shard_map/all_to_all | solution.py:508
  62.6 3.4 %collective-permute-start.1 = (f32[2,16,16,128]{3,2,1,0:T(8,128)S(1)}, f32[2,16,16,128]{3,2,1,0:T(8,128)}, u32[]{:S(2)}, u32[]{:S(2)}) collective-permute-start(f32[2,16,16,128]{3,2,1,0:T(8,128)S(1)} %get-tuple-element.83), channel_id=1, source_target_pairs={{0,8},{8,0},{1,9},{9,1},{2,10},{10,2},{3,11},{11,3},{4,12},{12,4},... | collective-permute-start | bytes 786440 | tf_op jit(solution)/shard_map/ppermute | solution.py:426
  66.3 11.2 %collective-permute-start.5 = (bf16[208,128]{1,0:T(8,128)(2,1)S(1)}, bf16[208,128]{1,0:T(8,128)(2,1)S(1)}, u32[]{:S(2)}, u32[]{:S(2)}) collective-permute-start(bf16[208,128]{1,0:T(8,128)(2,1)S(1)} %get-tuple-element.108), channel_id=1, source_target_pairs={{1,0},{2,1},{3,2},{4,3},{5,4},{6,5},{7,6},{9,8},{10,9},{11,10},{12... | collective-permute-start | bytes 159752 | tf_op jit(solution)/shard_map/ppermute | solution.py:422
  81.1 12.7 %shard_map.107 = f32[8,2,16,128]{3,2,1,0:T(8,128)} custom-call(bf16[32,32,128]{2,1,0:T(8,128)(2,1)} %copy-done.2, f32[3,1024]{1,0:T(4,128)} %reshape.177.t_ref, bf16[8192,1024]{1,0:T(8,128)(2,1)} %get-tuple-element.41.ka.kb.kc.kd, bf16[8192,1024]{1,0:T(8,128)(2,1)} %get-tuple-element.41.ka.kb.kc.kd, bf16[8192,1024]{1,0:T(8,128)(2,1)} %get-tuple-element.41.ka.kb.kc.kd, ...), custom_call_target="tpu_custom_call" | custom-call | flops 4000000000 | bytes 20000000 | tf_op jit(solution)/shard_map/pallas_call | solution.py:171
  93.8 3.3 %all-to-all-start.2 = ((f32[8,2,16,128]{3,2,1,0:T(8,128)}), f32[8,2,16,128]{3,2,1,0:T(8,128)S(1)}, u32[]{:S(2)}, u32[]{:S(2)}) async-start(f32[8,2,16,128]{3,2,1,0:T(8,128)} %shard_map.107), calls=%async_computation.2 | async-start | bytes 262144 | tf_op jit(solution)/shard_map/all_to_all | solution.py:548
  97.2 5.4 %all-to-all-done.2.parts_ref = f32[8,2,16,128]{3,2,1,0:T(8,128)S(1)} async-done(((f32[8,2,16,128]{3,2,1,0:T(8,128)}), f32[8,2,16,128]{3,2,1,0:T(8,128)S(1)}, u32[]{:S(2)}, u32[]{:S(2)}) %all-to-all-start.2) | async-done | bytes 131104 | tf_op jit(solution)/shard_map/all_to_all | solution.py:548
  104.1 9.5 %all-to-all-start.3 = ((f32[32,4,128]{2,1,0:T(4,128)}), f32[32,4,128]{2,1,0:T(4,128)S(1)}, u32[]{:S(2)}, u32[]{:S(2)}) async-start(f32[32,4,128]{2,1,0:T(4,128)} %bitcast.12), calls=%async_computation.3 | async-start | bytes 131072 | tf_op jit(solution)/shard_map/all_to_all | solution.py:552
  113.7 4.0 %shard_map.109 = (f32[6,18,16,128]{3,2,1,0:T(8,128)S(1)}, f32[4,16,16,128]{3,2,1,0:T(8,128)S(1)}) custom-call(s32[8]{0:T(128)S(1)} %convert_element_type.87.flags_ref, f32[4,16,16,128]{3,2,1,0:T(8,128)S(1)} %maximum_select_fusion.pot.pot_in, bf16[2,16,16,128]{3,2,1,0:T(8,128)(2,1)S(1)} %bitcast.63, bf16[2,16,16,128]{3,2,1,0:T(8,128)(2,1)S(1)} %bitcast.66, ...), custom_call_target="tpu_custom_call" | custom-call | flops 2000000 | bytes 2000000 | tf_op jit(solution)/shard_map/pallas_call | solution.py:33
  118.9 3.5 %all-to-all-done.3 = f32[32,4,128]{2,1,0:T(4,128)S(1)} async-done(((f32[32,4,128]{2,1,0:T(4,128)}), f32[32,4,128]{2,1,0:T(4,128)S(1)}, u32[]{:S(2)}, u32[]{:S(2)}) %all-to-all-start.3) | async-done | bytes 65568 | tf_op jit(solution)/shard_map/all_to_all | solution.py:552
  128.8 5.1 %collective-permute-start.8 = (bf16[4,1,16,128]{3,2,1,0:T(8,128)(2,1)S(1)}, bf16[4,1,16,128]{3,2,1,0:T(8,128)(2,1)S(1)}, u32[]{:S(2)}, u32[]{:S(2)}) collective-permute-start(bf16[4,1,16,128]{3,2,1,0:T(8,128)(2,1)S(1)} %get-tuple-element.53), channel_id=1, source_target_pairs={{0,1},{1,2},{2,3},{3,4},{4,5},{5,6},{6,7},{8,9},{9,10},{10,11},{11... | collective-permute-start | bytes 49160 | tf_op jit(solution)/shard_map/ppermute | solution.py:422
  135.9 3.1 %collective-permute-done.9.yh = bf16[4,1,16,128]{3,2,1,0:T(8,128)(2,1)S(1)} collective-permute-done((bf16[4,1,16,128]{3,2,1,0:T(8,128)(2,1)S(1)}, bf16[4,1,16,128]{3,2,1,0:T(8,128)(2,1)S(1)}, u32[]{:S(2)}, u32[]{:S(2)}) %collective-permute-start.9) | collective-permute-done | bytes 16416 | tf_op jit(solution)/shard_map/ppermute | solution.py:422
  139.9 3.6 %shard_map.111 = (f32[4,16,16,128]{3,2,1,0:T(8,128)S(1)}, f32[128,128]{1,0:T(8,128)}) custom-call(f32[4,16,16,128]{3,2,1,0:T(8,128)S(1)} %get-tuple-element.50.pot_in, bf16[1,16,16,128]{3,2,1,0:T(8,128)(2,1)S(1)} %collective-permute-done.6.xl, bf16[1,16,16,128]{3,2,1,0:T(8,128)(2,1)S(1)} %collective-permute-done.7.xh, ...), custom_call_target="tpu_custom_call" | custom-call | flops 2000000 | bytes 2000000 | tf_op jit(solution)/shard_map/pallas_call | solution.py:33
  143.6 7.8 %all-to-all-start.4 = ((f32[32,4,128]{2,1,0:T(4,128)}), f32[32,4,128]{2,1,0:T(4,128)S(1)}, u32[]{:S(2)}, u32[]{:S(2)}) async-start(f32[32,4,128]{2,1,0:T(4,128)} %bitcast.26), calls=%async_computation.4 | async-start | bytes 131072 | tf_op jit(solution)/shard_map/all_to_all | solution.py:500
  151.5 3.1 %collective-permute-start.10 = (bf16[512,128]{1,0:T(8,128)(2,1)S(1)}, bf16[512,128]{1,0:T(8,128)(2,1)S(1)}, u32[]{:S(2)}, u32[]{:S(2)}) collective-permute-start(bf16[512,128]{1,0:T(8,128)(2,1)S(1)} %bitcast.98), channel_id=1, source_target_pairs={{0,16},{16,32},{32,48},{48,64},{64,80},{80,96},{96,112},{112,128},... | collective-permute-start | bytes 393224 | tf_op jit(solution)/shard_map/ppermute | solution.py:422
  154.6 5.6 %all-to-all-done.4 = f32[32,4,128]{2,1,0:T(4,128)S(1)} async-done(((f32[32,4,128]{2,1,0:T(4,128)}), f32[32,4,128]{2,1,0:T(4,128)S(1)}, u32[]{:S(2)}, u32[]{:S(2)}) %all-to-all-start.4) | async-done | bytes 65568 | tf_op jit(solution)/shard_map/all_to_all | solution.py:500
  161.2 3.9 %all-to-all-start.5 = ((bf16[32,32,128]{2,1,0:T(8,128)(2,1)}), bf16[32,32,128]{2,1,0:T(8,128)(2,1)S(1)}, u32[]{:S(2)}, u32[]{:S(2)}) async-start(bf16[32,32,128]{2,1,0:T(8,128)(2,1)} %shard_map.112), calls=%async_computation.5 | async-start | bytes 524288 | tf_op jit(solution)/shard_map/all_to_all | solution.py:508
  166.6 9.3 %collective-permute-done.11 = bf16[512,128]{1,0:T(8,128)(2,1)S(1)} collective-permute-done((bf16[512,128]{1,0:T(8,128)(2,1)S(1)}, bf16[512,128]{1,0:T(8,128)(2,1)S(1)}, u32[]{:S(2)}, u32[]{:S(2)}) %collective-permute-start.11) | collective-permute-done | bytes 131104 | tf_op jit(solution)/shard_map/ppermute | solution.py:422
  177.3 12.7 %shard_map.113 = f32[8,2,16,128]{3,2,1,0:T(8,128)} custom-call(bf16[32,32,128]{2,1,0:T(8,128)(2,1)} %copy-done.3, f32[3,1024]{1,0:T(4,128)} %reshape.177.t_ref, bf16[8192,1024]{1,0:T(8,128)(2,1)} %get-tuple-element.41.ka.kb.kc.kd, bf16[8192,1024]{1,0:T(8,128)(2,1)} %get-tuple-element.41.ka.kb.kc.kd, bf16[8192,1024]{1,0:T(8,128)(2,1)} %get-tuple-element.41.ka.kb.kc.kd, ...), custom_call_target="tpu_custom_call" | custom-call | flops 4000000000 | bytes 20000000 | tf_op jit(solution)/shard_map/pallas_call | solution.py:171
  190.0 4.0 %all-to-all-start.6 = ((f32[8,2,16,128]{3,2,1,0:T(8,128)}), f32[8,2,16,128]{3,2,1,0:T(8,128)S(1)}, u32[]{:S(2)}, u32[]{:S(2)}) async-start(f32[8,2,16,128]{3,2,1,0:T(8,128)} %shard_map.113), calls=%async_computation.6 | async-start | bytes 262144 | tf_op jit(solution)/shard_map/all_to_all | solution.py:548
  193.9 3.6 %collective-permute-start.12 = (bf16[192,128]{1,0:T(8,128)(2,1)S(1)}, bf16[192,128]{1,0:T(8,128)(2,1)S(1)}, u32[]{:S(2)}, u32[]{:S(2)}) collective-permute-start(bf16[192,128]{1,0:T(8,128)(2,1)S(1)} %bitcast.100), channel_id=1, source_target_pairs={{0,1},{1,2},{2,3},{3,4},{4,5},{5,6},{6,7},{8,9},{9,10},{10,11},{11... | collective-permute-start | bytes 147464 | tf_op jit(solution)/shard_map/ppermute | solution.py:422
  199.5 3.5 %collective-permute-done.13 = bf16[192,128]{1,0:T(8,128)(2,1)S(1)} collective-permute-done((bf16[192,128]{1,0:T(8,128)(2,1)S(1)}, bf16[192,128]{1,0:T(8,128)(2,1)S(1)}, u32[]{:S(2)}, u32[]{:S(2)}) %collective-permute-start.13) | collective-permute-done | bytes 49184 | tf_op jit(solution)/shard_map/ppermute | solution.py:422
  202.9 4.0 %shard_map.115 = (f32[6,18,16,128]{3,2,1,0:T(8,128)S(1)}, f32[4,16,16,128]{3,2,1,0:T(8,128)S(1)}) custom-call(s32[8]{0:T(128)S(1)} %convert_element_type.87.flags_ref, f32[4,16,16,128]{3,2,1,0:T(8,128)S(1)} %get-tuple-element.62.pot.pot_in, bf16[2,16,16,128]{3,2,1,0:T(8,128)(2,1)S(1)} %bitcast.69, bf16[2,16,16,128]{3,2,1,0:T(8,128)(2,1)S(1)} %bitcast.72, ...), custom_call_target="tpu_custom_call" | custom-call | flops 2000000 | bytes 2000000 | tf_op jit(solution)/shard_map/pallas_call | solution.py:33
  208.4 7.3 %all-to-all-start.7 = ((f32[32,4,128]{2,1,0:T(4,128)}), f32[32,4,128]{2,1,0:T(4,128)S(1)}, u32[]{:S(2)}, u32[]{:S(2)}) async-start(f32[32,4,128]{2,1,0:T(4,128)} %bitcast.28), calls=%async_computation.7 | async-start | bytes 131072 | tf_op jit(solution)/shard_map/all_to_all | solution.py:552
  215.7 8.9 %all-to-all-done.7 = f32[32,4,128]{2,1,0:T(4,128)S(1)} async-done(((f32[32,4,128]{2,1,0:T(4,128)}), f32[32,4,128]{2,1,0:T(4,128)S(1)}, u32[]{:S(2)}, u32[]{:S(2)}) %all-to-all-start.7) | async-done | bytes 65568 | tf_op jit(solution)/shard_map/all_to_all | solution.py:552
  227.1 3.3 %collective-permute-start.16 = (bf16[4,1,16,128]{3,2,1,0:T(8,128)(2,1)S(1)}, bf16[4,1,16,128]{3,2,1,0:T(8,128)(2,1)S(1)}, u32[]{:S(2)}, u32[]{:S(2)}) collective-permute-start(bf16[4,1,16,128]{3,2,1,0:T(8,128)(2,1)S(1)} %get-tuple-element.68), channel_id=1, source_target_pairs={{0,1},{1,2},{2,3},{3,4},{4,5},{5,6},{6,7},{8,9},{9,10},{10,11},{11... | collective-permute-start | bytes 49160 | tf_op jit(solution)/shard_map/ppermute | solution.py:422
  236.5 3.7 %collective-permute-done.15.xh = bf16[1,16,16,128]{3,2,1,0:T(8,128)(2,1)S(1)} collective-permute-done((bf16[1,16,16,128]{3,2,1,0:T(8,128)(2,1)S(1)}, bf16[1,16,16,128]{3,2,1,0:T(8,128)(2,1)S(1)}, u32[]{:S(2)}, u32[]{:S(2)}) %collective-permute-start.15) | collective-permute-done | bytes 65568 | tf_op jit(solution)/shard_map/ppermute | solution.py:422
  244.3 9.4 %collective-permute-done.18 = bf16[544,128]{1,0:T(8,128)(2,1)S(1)} collective-permute-done((bf16[544,128]{1,0:T(8,128)(2,1)S(1)}, bf16[544,128]{1,0:T(8,128)(2,1)S(1)}, u32[]{:S(2)}, u32[]{:S(2)}) %collective-permute-start.18) | collective-permute-done | bytes 139296 | tf_op jit(solution)/shard_map/ppermute | solution.py:426
  (126 shorter events, 53.5 us)
Async XLA Ops:
  0.6 60.9 %copy-start.4 = (f32[32,2,16,128]{3,2,1,0:T(8,128)S(1)}, f32[32,2,16,128]{3,2,1,0:T(8,128)}, u32[]{:S(2)}) copy-start(f32[32,2,16,128]{3,2,1,0:T(8,128)} %param.9) | copy-start | bytes 1572868
  9.1 21.9 %collective-permute-start = (f32[576,128]{1,0:T(8,128)S(1)}, f32[576,128]{1,0:T(8,128)S(1)}, u32[]{:S(2)}, u32[]{:S(2)}) collective-permute-start(f32[576,128]{1,0:T(8,128)S(1)} %concatenate.66), channel_id=1, source_target_pairs={{0,8},{8,0},{1,9},{9,1},{2,10},{10,2},{3,11},{11,3},{4,12},{12,4},... | collective-permute-start | bytes 884744 | tf_op jit(solution)/shard_map/ppermute | solution.py:426
  33.6 0.7 copy-start
  35.1 18.6 %all-to-all-start = ((f32[32,4,128]{2,1,0:T(4,128)}), f32[32,4,128]{2,1,0:T(4,128)S(1)}, u32[]{:S(2)}, u32[]{:S(2)}) async-start(f32[32,4,128]{2,1,0:T(4,128)} %bitcast.10), calls=%async_computation | async-start | bytes 131072 | tf_op jit(solution)/shard_map/all_to_all | solution.py:500
  44.8 21.2 %collective-permute-start.2 = (bf16[528,128]{1,0:T(8,128)(2,1)S(1)}, bf16[528,128]{1,0:T(8,128)(2,1)S(1)}, u32[]{:S(2)}, u32[]{:S(2)}) collective-permute-start(bf16[528,128]{1,0:T(8,128)(2,1)S(1)} %pad_maximum_fusion.1), channel_id=1, source_target_pairs={{0,16},{16,32},{32,48},{48,64},{64,80},{80,96},{96,112},{112,128},... | collective-permute-start | bytes 405512 | tf_op jit(solution)/shard_map/ppermute | solution.py:422
  48.0 18.1 %collective-permute-start.3 = (bf16[528,128]{1,0:T(8,128)(2,1)S(1)}, bf16[528,128]{1,0:T(8,128)(2,1)S(1)}, u32[]{:S(2)}, u32[]{:S(2)}) collective-permute-start(bf16[528,128]{1,0:T(8,128)(2,1)S(1)} %pad_maximum_fusion.2), channel_id=1, source_target_pairs={{16,0},{32,16},{48,32},{64,48},{80,64},{96,80},{112,96},{128,112},... | collective-permute-start | bytes 405512 | tf_op jit(solution)/shard_map/ppermute | solution.py:422
  54.6 25.8 %all-to-all-start.1 = ((bf16[32,32,128]{2,1,0:T(8,128)(2,1)}), bf16[32,32,128]{2,1,0:T(8,128)(2,1)S(1)}, u32[]{:S(2)}, u32[]{:S(2)}) async-start(bf16[32,32,128]{2,1,0:T(8,128)(2,1)} %shard_map.105), calls=%async_computation.1 | async-start | bytes 524288 | tf_op jit(solution)/shard_map/all_to_all | solution.py:508
  62.6 55.0 %collective-permute-start.1 = (f32[2,16,16,128]{3,2,1,0:T(8,128)S(1)}, f32[2,16,16,128]{3,2,1,0:T(8,128)}, u32[]{:S(2)}, u32[]{:S(2)}) collective-permute-start(f32[2,16,16,128]{3,2,1,0:T(8,128)S(1)} %get-tuple-element.83), channel_id=1, source_target_pairs={{0,8},{8,0},{1,9},{9,1},{2,10},{10,2},{3,11},{11,3},{4,12},{12,4},... | collective-permute-start | bytes 786440 | tf_op jit(solution)/shard_map/ppermute | solution.py:426
  66.3 30.9 %collective-permute-start.5 = (bf16[208,128]{1,0:T(8,128)(2,1)S(1)}, bf16[208,128]{1,0:T(8,128)(2,1)S(1)}, u32[]{:S(2)}, u32[]{:S(2)}) collective-permute-start(bf16[208,128]{1,0:T(8,128)(2,1)S(1)} %get-tuple-element.108), channel_id=1, source_target_pairs={{1,0},{2,1},{3,2},{4,3},{5,4},{6,5},{7,6},{9,8},{10,9},{11,10},{12... | collective-permute-start | bytes 159752 | tf_op jit(solution)/shard_map/ppermute | solution.py:422
  77.5 36.1 %collective-permute-start.4 = (bf16[208,128]{1,0:T(8,128)(2,1)S(1)}, bf16[208,128]{1,0:T(8,128)(2,1)S(1)}, u32[]{:S(2)}, u32[]{:S(2)}) collective-permute-start(bf16[208,128]{1,0:T(8,128)(2,1)S(1)} %get-tuple-element.109), channel_id=1, source_target_pairs={{0,1},{1,2},{2,3},{3,4},{4,5},{5,6},{6,7},{8,9},{9,10},{10,11},{11... | collective-permute-start | bytes 159752 | tf_op jit(solution)/shard_map/ppermute | solution.py:422
  80.4 0.7 copy-start.2
  93.8 8.8 %all-to-all-start.2 = ((f32[8,2,16,128]{3,2,1,0:T(8,128)}), f32[8,2,16,128]{3,2,1,0:T(8,128)S(1)}, u32[]{:S(2)}, u32[]{:S(2)}) async-start(f32[8,2,16,128]{3,2,1,0:T(8,128)} %shard_map.107), calls=%async_computation.2 | async-start | bytes 262144 | tf_op jit(solution)/shard_map/all_to_all | solution.py:548
  104.1 18.4 %all-to-all-start.3 = ((f32[32,4,128]{2,1,0:T(4,128)}), f32[32,4,128]{2,1,0:T(4,128)S(1)}, u32[]{:S(2)}, u32[]{:S(2)}) async-start(f32[32,4,128]{2,1,0:T(4,128)} %bitcast.12), calls=%async_computation.3 | async-start | bytes 131072 | tf_op jit(solution)/shard_map/all_to_all | solution.py:552
  125.0 14.0 %collective-permute-start.6 = (bf16[1,16,16,128]{3,2,1,0:T(8,128)(2,1)S(1)}, bf16[1,16,16,128]{3,2,1,0:T(8,128)(2,1)S(1)}, u32[]{:S(2)}, u32[]{:S(2)}) collective-permute-start(bf16[1,16,16,128]{3,2,1,0:T(8,128)(2,1)S(1)} %get-tuple-element.51), channel_id=1, source_target_pairs={{0,16},{16,32},{32,48},{48,64},{64,80},{80,96},{96,112},{112,128},... | collective-permute-start | bytes 196616 | tf_op jit(solution)/shard_map/ppermute | solution.py:422
  127.5 11.5 %collective-permute-start.7 = (bf16[1,16,16,128]{3,2,1,0:T(8,128)(2,1)S(1)}, bf16[1,16,16,128]{3,2,1,0:T(8,128)(2,1)S(1)}, u32[]{:S(2)}, u32[]{:S(2)}) collective-permute-start(bf16[1,16,16,128]{3,2,1,0:T(8,128)(2,1)S(1)} %get-tuple-element.52), channel_id=1, source_target_pairs={{16,0},{32,16},{48,32},{64,48},{80,64},{96,80},{112,96},{128,112},... | collective-permute-start | bytes 196616 | tf_op jit(solution)/shard_map/ppermute | solution.py:422
  128.8 7.1 %collective-permute-start.8 = (bf16[4,1,16,128]{3,2,1,0:T(8,128)(2,1)S(1)}, bf16[4,1,16,128]{3,2,1,0:T(8,128)(2,1)S(1)}, u32[]{:S(2)}, u32[]{:S(2)}) collective-permute-start(bf16[4,1,16,128]{3,2,1,0:T(8,128)(2,1)S(1)} %get-tuple-element.53), channel_id=1, source_target_pairs={{0,1},{1,2},{2,3},{3,4},{4,5},{5,6},{6,7},{8,9},{9,10},{10,11},{11... | collective-permute-start | bytes 49160 | tf_op jit(solution)/shard_map/ppermute | solution.py:422
  133.9 5.1 %collective-permute-start.9 = (bf16[4,1,16,128]{3,2,1,0:T(8,128)(2,1)S(1)}, bf16[4,1,16,128]{3,2,1,0:T(8,128)(2,1)S(1)}, u32[]{:S(2)}, u32[]{:S(2)}) collective-permute-start(bf16[4,1,16,128]{3,2,1,0:T(8,128)(2,1)S(1)} %get-tuple-element.54), channel_id=1, source_target_pairs={{1,0},{2,1},{3,2},{4,3},{5,4},{6,5},{7,6},{9,8},{10,9},{11,10},{12... | collective-permute-start | bytes 49160 | tf_op jit(solution)/shard_map/ppermute | solution.py:422
  139.0 1.0 copy-start.1
  143.6 16.7 %all-to-all-start.4 = ((f32[32,4,128]{2,1,0:T(4,128)}), f32[32,4,128]{2,1,0:T(4,128)S(1)}, u32[]{:S(2)}, u32[]{:S(2)}) async-start(f32[32,4,128]{2,1,0:T(4,128)} %bitcast.26), calls=%async_computation.4 | async-start | bytes 131072 | tf_op jit(solution)/shard_map/all_to_all | solution.py:500
  151.5 15.1 %collective-permute-start.10 = (bf16[512,128]{1,0:T(8,128)(2,1)S(1)}, bf16[512,128]{1,0:T(8,128)(2,1)S(1)}, u32[]{:S(2)}, u32[]{:S(2)}) collective-permute-start(bf16[512,128]{1,0:T(8,128)(2,1)S(1)} %bitcast.98), channel_id=1, source_target_pairs={{0,16},{16,32},{32,48},{48,64},{64,80},{80,96},{96,112},{112,128},... | collective-permute-start | bytes 393224 | tf_op jit(solution)/shard_map/ppermute | solution.py:422
  161.2 15.4 %all-to-all-start.5 = ((bf16[32,32,128]{2,1,0:T(8,128)(2,1)}), bf16[32,32,128]{2,1,0:T(8,128)(2,1)S(1)}, u32[]{:S(2)}, u32[]{:S(2)}) async-start(bf16[32,32,128]{2,1,0:T(8,128)(2,1)} %shard_map.112), calls=%async_computation.5 | async-start | bytes 524288 | tf_op jit(solution)/shard_map/all_to_all | solution.py:508
  165.1 10.8 %collective-permute-start.11 = (bf16[512,128]{1,0:T(8,128)(2,1)S(1)}, bf16[512,128]{1,0:T(8,128)(2,1)S(1)}, u32[]{:S(2)}, u32[]{:S(2)}) collective-permute-start(bf16[512,128]{1,0:T(8,128)(2,1)S(1)} %bitcast.97), channel_id=1, source_target_pairs={{16,0},{32,16},{48,32},{64,48},{80,64},{96,80},{112,96},{128,112},... | collective-permute-start | bytes 393224 | tf_op jit(solution)/shard_map/ppermute | solution.py:422
  176.6 0.7 copy-start.3
  190.0 16.9 %all-to-all-start.6 = ((f32[8,2,16,128]{3,2,1,0:T(8,128)}), f32[8,2,16,128]{3,2,1,0:T(8,128)S(1)}, u32[]{:S(2)}, u32[]{:S(2)}) async-start(f32[8,2,16,128]{3,2,1,0:T(8,128)} %shard_map.113), calls=%async_computation.6 | async-start | bytes 262144 | tf_op jit(solution)/shard_map/all_to_all | solution.py:548
  193.9 5.5 %collective-permute-start.12 = (bf16[192,128]{1,0:T(8,128)(2,1)S(1)}, bf16[192,128]{1,0:T(8,128)(2,1)S(1)}, u32[]{:S(2)}, u32[]{:S(2)}) collective-permute-start(bf16[192,128]{1,0:T(8,128)(2,1)S(1)} %bitcast.100), channel_id=1, source_target_pairs={{0,1},{1,2},{2,3},{3,4},{4,5},{5,6},{6,7},{8,9},{9,10},{10,11},{11... | collective-permute-start | bytes 147464 | tf_op jit(solution)/shard_map/ppermute | solution.py:422
  197.5 5.4 %collective-permute-start.13 = (bf16[192,128]{1,0:T(8,128)(2,1)S(1)}, bf16[192,128]{1,0:T(8,128)(2,1)S(1)}, u32[]{:S(2)}, u32[]{:S(2)}) collective-permute-start(bf16[192,128]{1,0:T(8,128)(2,1)S(1)} %bitcast.101), channel_id=1, source_target_pairs={{1,0},{2,1},{3,2},{4,3},{5,4},{6,5},{7,6},{9,8},{10,9},{11,10},{12... | collective-permute-start | bytes 147464 | tf_op jit(solution)/shard_map/ppermute | solution.py:422
  208.4 16.2 %all-to-all-start.7 = ((f32[32,4,128]{2,1,0:T(4,128)}), f32[32,4,128]{2,1,0:T(4,128)S(1)}, u32[]{:S(2)}, u32[]{:S(2)}) async-start(f32[32,4,128]{2,1,0:T(4,128)} %bitcast.28), calls=%async_computation.7 | async-start | bytes 131072 | tf_op jit(solution)/shard_map/all_to_all | solution.py:552
  227.1 9.4 %collective-permute-start.16 = (bf16[4,1,16,128]{3,2,1,0:T(8,128)(2,1)S(1)}, bf16[4,1,16,128]{3,2,1,0:T(8,128)(2,1)S(1)}, u32[]{:S(2)}, u32[]{:S(2)}) collective-permute-start(bf16[4,1,16,128]{3,2,1,0:T(8,128)(2,1)S(1)} %get-tuple-element.68), channel_id=1, source_target_pairs={{0,1},{1,2},{2,3},{3,4},{4,5},{5,6},{6,7},{8,9},{9,10},{10,11},{11... | collective-permute-start | bytes 49160 | tf_op jit(solution)/shard_map/ppermute | solution.py:422
  230.4 6.1 %collective-permute-start.17 = (bf16[4,1,16,128]{3,2,1,0:T(8,128)(2,1)S(1)}, bf16[4,1,16,128]{3,2,1,0:T(8,128)(2,1)S(1)}, u32[]{:S(2)}, u32[]{:S(2)}) collective-permute-start(bf16[4,1,16,128]{3,2,1,0:T(8,128)(2,1)S(1)} %get-tuple-element.69), channel_id=1, source_target_pairs={{1,0},{2,1},{3,2},{4,3},{5,4},{6,5},{7,6},{9,8},{10,9},{11,10},{12... | collective-permute-start | bytes 49160 | tf_op jit(solution)/shard_map/ppermute | solution.py:422
  232.3 4.2 %collective-permute-start.14 = (bf16[1,16,16,128]{3,2,1,0:T(8,128)(2,1)S(1)}, bf16[1,16,16,128]{3,2,1,0:T(8,128)(2,1)S(1)}, u32[]{:S(2)}, u32[]{:S(2)}) collective-permute-start(bf16[1,16,16,128]{3,2,1,0:T(8,128)(2,1)S(1)} %get-tuple-element.66), channel_id=1, source_target_pairs={{0,16},{16,32},{32,48},{48,64},{64,80},{80,96},{96,112},{112,128},... | collective-permute-start | bytes 196616 | tf_op jit(solution)/shard_map/ppermute | solution.py:422
  235.2 5.0 %collective-permute-start.15 = (bf16[1,16,16,128]{3,2,1,0:T(8,128)(2,1)S(1)}, bf16[1,16,16,128]{3,2,1,0:T(8,128)(2,1)S(1)}, u32[]{:S(2)}, u32[]{:S(2)}) collective-permute-start(bf16[1,16,16,128]{3,2,1,0:T(8,128)(2,1)S(1)} %get-tuple-element.67), channel_id=1, source_target_pairs={{16,0},{32,16},{48,32},{64,48},{80,64},{96,80},{112,96},{128,112},... | collective-permute-start | bytes 196616 | tf_op jit(solution)/shard_map/ppermute | solution.py:422
  242.1 11.6 %collective-permute-start.18 = (bf16[544,128]{1,0:T(8,128)(2,1)S(1)}, bf16[544,128]{1,0:T(8,128)(2,1)S(1)}, u32[]{:S(2)}, u32[]{:S(2)}) collective-permute-start(bf16[544,128]{1,0:T(8,128)(2,1)S(1)} %pad_maximum_fusion), channel_id=1, source_target_pairs={{0,8},{8,0},{1,9},{9,1},{2,10},{10,2},{3,11},{11,3},{4,12},{12,4},... | collective-permute-start | bytes 417800 | tf_op jit(solution)/shard_map/ppermute | solution.py:426

commit v3 on v2

--- a/solution.py
+++ b/solution.py
@@ -379,6 +379,40 @@
     msg[...] = out
 
 
+def tables_body(cell, count, weight, panel, points, material, out):
+    lane = lax.broadcasted_iota(jnp.int32, (256, 128), 1)
+    index = lax.broadcasted_iota(jnp.int32, (256, 128), 0)
+    rows = jnp.concatenate(
+        [
+            cell[0].astype(F32),
+            weight[0],
+            panel[0].astype(F32),
+            jnp.zeros((5, 256), F32),
+        ]
+    )
+    parts = jnp.concatenate(split3(rows)).astype(BF16)
+    counts = jnp.broadcast_to(count[0].astype(F32), (16, 64)).astype(BF16)
+    rank = (lax.broadcasted_iota(jnp.int32, (1, 128), 1) % 4).astype(F32)
+    picked = []
+    for b in range(2):
+        take = jnp.where(index == (lane // 4) * 8 + b * 4 + lane % 4, 1.0, 0.0).astype(BF16)
+        found = jnp.dot(parts, take, preferred_element_type=F32)
+        found = found[:8] + found[8:16] + found[16:]
+        spread = jnp.where(index == (lane // 4) * 2 + b, 1.0, 0.0)[:64].astype(BF16)
+        live = jnp.dot(counts, spread, preferred_element_type=F32)[0:1]
+        picked.append((found[0:1], jnp.where(rank < live, found[1:2], 0.0), found[2:3]))
+    for kind in range(3):
+        for b in range(2):
+            out[kind * 2 + b : kind * 2 + b + 1, :] = picked[b][kind]
+    out[6:8, :] = jnp.zeros((2, 128), F32)
+    for component in range(3):
+        for j in range(8):
+            row = 8 + component * 8 + j
+            out[row : row + 1, :] = points[component : component + 1, j * 128 : (j + 1) * 128]
+    for x in range(2):
+        out[32 + x * LY : 32 + (x + 1) * LY, :] = material[x].astype(F32)
+
+
 def tables_gather_body(
     flags_ref, own, other, pot, msg, hot, rows_ref, weight_ref, owner_hot, lanes_ref
 ):
@@ -454,30 +488,18 @@
         [plane == 0, plane == NXY - 1, row == 0, row == 7, h == 1, h == 1, h == 1, h == 1]
     ).astype(jnp.int32)
 
-    rank = jnp.arange(4, dtype=jnp.int32)[None, :]
-    weight = jnp.where(
-        rank < face_count.reshape(64, 1), face_weight.reshape(64, 4), 0.0
-    ).reshape(256)
-    tables = jnp.stack(
-        [face_cell.reshape(256).astype(F32), weight, slot_panel.reshape(256).astype(F32)]
+    block = call(
+        tables_body,
+        sds((64, 128)),
+        (face_cell, face_count, face_weight, slot_panel, target_points, material),
     )
-    tables = tables.reshape(3, 32, 2, 4).transpose(0, 2, 1, 3).reshape(6, 128)
-    tables = jnp.concatenate([tables, jnp.zeros((2, 128), F32)])
+    tables = block[:8]
     keep, give = halved(start, h)
-    got = swap_h(
-        jnp.concatenate(
-            [
-                give.reshape(512, 128),
-                tables,
-                target_points.reshape(24, 128),
-                material.reshape(32, 128).astype(F32),
-            ]
-        )
-    )
+    got = swap_h(jnp.concatenate([give.reshape(512, 128), block]))
     k0, turned = kernel_matrix(target_points, source_points)
 
     pot = by_h(h, keep, got[:512].reshape(2, LY, EH, LZ))
-    mats = by_h(h, material.astype(F32), got[544:576].reshape(2, LY, LZ))
+    mats = by_h(h, block[32:64].reshape(2, LY, LZ), got[544:576].reshape(2, LY, LZ))
     msg, hot, rows_col, weights_col, owner_hot, lanes = call(
         tables_gather_body,
         (
@@ -495,16 +517,17 @@
 
     rims = None
     for outer_index in range(ITERS):
-        msg, coarse = lax.optimization_barrier((msg, pot))
+        if outer_index == 0:
+            msg, coarse, late = lax.optimization_barrier((msg, pot, excitation))
+            exc_keep, exc_give = halved(late, h)
+            exc = by_h(h, exc_keep, swap_h(exc_give.astype(BF16)).astype(F32))
+        else:
+            msg, coarse = lax.optimization_barrier((msg, pot))
         coarse = coarse.astype(BF16)
         arrived = lax.all_to_all(msg.reshape(NXY, 4, 128), PLANE, 0, 0, tiled=True)
         dens = call(
             density_body, sds((NXY, 2 * EH, 128), BF16), (arrived.reshape(128, 128), owner_hot)
         )
-        if outer_index == 0:
-            dens, late = lax.optimization_barrier((dens, excitation))
-            exc_keep, exc_give = halved(late, h)
-            exc = by_h(h, exc_keep, swap_h(exc_give))
         dens = lax.all_to_all(dens, PLANE, 0, 0, tiled=True)
 
         up, down = coarse[2:4].reshape(512, 128), coarse[0:2].reshape(512, 128)
@@ -513,6 +536,8 @@
             down = jnp.concatenate([down, mats[0].astype(BF16)])
         xl = shift(up, PLANE, NXY, 1)
         xh = shift(down, PLANE, NXY, -1)
+        parts = partial_flux(dens, their_targets, k0, turned)
+        xl, xh, parts = lax.optimization_barrier((xl, xh, parts))
         xl_pot = xl[:512].reshape(2, LY, EH, LZ)
         xh_pot = xh[:512].reshape(2, LY, EH, LZ)
 
@@ -527,6 +552,12 @@
             down = jnp.concatenate([down, mats[:, 0].astype(BF16), pad])
         yl = shift(up, ROW, 8, 1)
         yh = shift(down, ROW, 8, -1)
+        parts = lax.all_to_all(parts, ROW, 0, 0, tiled=True)
+        flux, slots = call(
+            owner_body, (sds((2, EH, 128)), sds((128, 128))), (flags, parts, owner_hot), smem=(0,)
+        )
+        yl, yh, slots = lax.optimization_barrier((yl, yh, slots))
+        back = lax.all_to_all(slots.reshape(NXY, 4, 128), PLANE, 0, 0, tiled=True)
         if outer_index == 0:
             rims = tuple(v.astype(F32) for v in (xl[512:], xh[512:], yl[192:], yh[192:]))
         scratch = (pltpu.VMEM((6, 18, EH, LZ), F32),)
@@ -543,13 +574,6 @@
             smem=(0,),
             scratch=(pltpu.VMEM((8, 20, EH, LZ), F32),),
         )
-
-        parts = partial_flux(dens, their_targets, k0, turned)
-        parts = lax.all_to_all(parts, ROW, 0, 0, tiled=True)
-        flux, slots = call(
-            owner_body, (sds((2, EH, 128)), sds((128, 128))), (flags, parts, owner_hot), smem=(0,)
-        )
-        back = lax.all_to_all(slots.reshape(NXY, 4, 128), PLANE, 0, 0, tiled=True)
 
         brick = (LX, LY, EH, LZ)
         pot, forcing, xlo, xhi, ylo, yhi = call(

time: 258 us -> 248 us (0.961)
  blocking collectives: 0 us -> 15.3 us
  waiting for transfers between devices: 57.5 us -> 45.4 us
  starting transfers between devices: 118 us -> 110 us
  other arithmetic: 7.37 us -> 1.27 us
    all_to_all x2, waiting for transfers between devices: 0.7 us -> 16.9 us  [per_device(): dens = lax.all_to_all(dens, PLANE, 0, 0, tiled=True)]
    all_to_all x0 -> x1, blocking collectives: none -> 15.3 us  [per_device(): arrived = lax.all_to_all(msg.reshape(NXY, 4, 128), PLANE, 0, 0, tiled=True)]
    all_to_all x2, starting transfers between devices: 7.27 us -> 20.1 us  [per_device(): parts = lax.all_to_all(parts, ROW, 0, 0, tiled=True)]
    ppermute x16, waiting for transfers between devices: 19.6 us -> 8.94 us  [shift(): return lax.ppermute(value, axes, pairs)]
    all_to_all x2 -> x1, waiting for transfers between devices: 10 us -> 0.41 us  [per_device(): arrived = lax.all_to_all(msg.reshape(NXY, 4, 128), PLANE, 0, 0, tiled=True)]
    ppermute x16, starting transfers between devices: 48.9 us -> 40.1 us  [shift(): return lax.ppermute(value, axes, pairs)]
    all_to_all x2, starting transfers between devices: 16.8 us -> 8.59 us  [per_device(): back = lax.all_to_all(slots.reshape(NXY, 4, 128), PLANE, 0, 0, tiled=True)]
    all_to_all x2 -> x1, starting transfers between devices: 17.5 us -> 9.67 us  [per_device(): arrived = lax.all_to_all(msg.reshape(NXY, 4, 128), PLANE, 0, 0, tiled=True)]
  transfers between devices with their start and end apart: 27 -> 26, of which waited for: 11 -> 10; matrix products, arithmetic and copies ran while one was open for 1% -> 0% of each run, Pallas kernels for 13% -> 19%
where the time goes in v3:
time: 248 us; the launch traced here: 245 us
  starting transfers between devices  110 us (44%)
  Pallas kernels  60.8 us (25%)
  waiting for transfers between devices  45.4 us (18%)
  blocking collectives  15.3 us (6%)
  local copies, waits for them, and re-layouts  11 us (4%)
    ppermute x16, starting transfers between devices, shift(): return lax.ppermute(value, axes, pairs)  40.1 us
    pallas_call x2, Pallas kernels, partial_flux(): pl.pallas_call(flux_body, grid=(FLUX_STEPS,), out_shape=sds((8, 2, EH, 12...  25.4 us
    pallas_call x12, Pallas kernels, call(): pl.pallas_call(body, out_shape=out_shape, in_specs=[SM if i in smem else...  25.2 us
    all_to_all x2, starting transfers between devices, per_device(): parts = lax.all_to_all(parts, ROW, 0, 0, tiled=True)  20.1 us
    ppermute x3, starting transfers between devices, swap_h(): return lax.ppermute(value, 'h', [(0, 1), (1, 0)])  17 us
    all_to_all x2, waiting for transfers between devices, per_device(): dens = lax.all_to_all(dens, PLANE, 0, 0, tiled=True)  16.9 us
    all_to_all x1, blocking collectives, per_device(): arrived = lax.all_to_all(msg.reshape(NXY, 4, 128), PLANE, 0, 0, tiled=True)  15.3 us
    all_to_all x2, starting transfers between devices, per_device(): dens = lax.all_to_all(dens, PLANE, 0, 0, tiled=True)  14.8 us
  transfers between devices with their start and end apart: 26, of which 10 were waited for; matrix products, arithmetic and copies ran while one was open for 0% of the time, Pallas kernels for 19%

profile of v3, /device:TPU:1, one launch (start us, length us, event | category | flops | bytes accessed | tf_op | source)
XLA Modules:
  0.0 245.3 jit_solution(8118187052801351499)
XLA Ops:
  6.4 11.5 %collective-permute-start = (f32[576,128]{1,0:T(8,128)S(1)}, f32[576,128]{1,0:T(8,128)S(1)}, u32[]{:S(2)}, u32[]{:S(2)}) collective-permute-start(f32[576,128]{1,0:T(8,128)S(1)} %pad_maximum_fusion), channel_id=1, source_target_pairs={{0,8},{8,0},{1,9},{9,1},{2,10},{10,2},{3,11},{11,3},{4,12},{12,4},... | collective-permute-start | bytes 884744 | tf_op jit(solution)/shard_map/ppermute | solution.py:460
  18.2 10.1 %shard_map.107 = (bf16[8192,1024]{1,0:T(8,128)(2,1)}, bf16[8192,128]{1,0:T(8,128)(2,1)}) custom-call(f32[3,1024]{1,0:T(4,128)} %t_ref.1, f32[3,8192]{1,0:T(4,128)} %s_ref.1), custom_call_target="tpu_custom_call" | custom-call | flops 2000000000 | bytes 20000000 | tf_op jit(solution)/shard_map/pallas_call | solution.py:87
  32.3 9.7 %all-to-all-start = ((f32[32,4,128]{2,1,0:T(4,128)}), f32[32,4,128]{2,1,0:T(4,128)S(1)}, u32[]{:S(2)}, u32[]{:S(2)}) async-start(f32[32,4,128]{2,1,0:T(4,128)} %bitcast.12), calls=%async_computation | async-start | bytes 131072 | tf_op jit(solution)/shard_map/all_to_all | solution.py:527
  42.1 3.1 %collective-permute-start.1 = (bf16[528,128]{1,0:T(8,128)(2,1)S(1)}, bf16[528,128]{1,0:T(8,128)(2,1)S(1)}, u32[]{:S(2)}, u32[]{:S(2)}) collective-permute-start(bf16[528,128]{1,0:T(8,128)(2,1)S(1)} %pad_maximum_fusion.2), channel_id=1, source_target_pairs={{0,16},{16,32},{32,48},{48,64},{64,80},{80,96},{96,112},{112,128},... | collective-permute-start | bytes 405512 | tf_op jit(solution)/shard_map/ppermute | solution.py:456
  46.9 3.5 %collective-permute-start.5 = (bf16[2,16,16,128]{3,2,1,0:T(8,128)(2,1)S(1)}, bf16[2,16,16,128]{3,2,1,0:T(8,128)(2,1)S(1)}, u32[]{:S(2)}, u32[]{:S(2)}) collective-permute-start(bf16[2,16,16,128]{3,2,1,0:T(8,128)(2,1)S(1)} %select_convert_fusion.1), channel_id=1, source_target_pairs={{0,8},{8,0},{1,9},{9,1},{2,10},{10,2},{3,11},{11,3},{4,12},{12,4},... | collective-permute-start | bytes 393224 | tf_op jit(solution)/shard_map/ppermute | solution.py:460
  51.8 10.9 %all-to-all-start.1 = ((bf16[32,32,128]{2,1,0:T(8,128)(2,1)}), bf16[32,32,128]{2,1,0:T(8,128)(2,1)S(1)}, u32[]{:S(2)}, u32[]{:S(2)}) async-start(bf16[32,32,128]{2,1,0:T(8,128)(2,1)} %shard_map.106), calls=%async_computation.1 | async-start | bytes 524288 | tf_op jit(solution)/shard_map/all_to_all | solution.py:531
  62.8 9.5 %all-to-all-done.1.arr = bf16[32,32,128]{2,1,0:T(8,128)(2,1)S(1)} async-done(((bf16[32,32,128]{2,1,0:T(8,128)(2,1)}), bf16[32,32,128]{2,1,0:T(8,128)(2,1)S(1)}, u32[]{:S(2)}, u32[]{:S(2)}) %all-to-all-start.1) | async-done | bytes 262176 | tf_op jit(solution)/shard_map/all_to_all | solution.py:531
  73.0 12.7 %shard_map.108 = f32[8,2,16,128]{3,2,1,0:T(8,128)} custom-call(bf16[32,32,128]{2,1,0:T(8,128)(2,1)} %copy-done.9, f32[3,1024]{1,0:T(4,128)} %reshape.108.t_ref, bf16[8192,1024]{1,0:T(8,128)(2,1)} %get-tuple-element.52.ka.kb.kc.kd, bf16[8192,1024]{1,0:T(8,128)(2,1)} %get-tuple-element.52.ka.kb.kc.kd, bf16[8192,1024]{1,0:T(8,128)(2,1)} %get-tuple-element.52.ka.kb.kc.kd, ...), custom_call_target="tpu_custom_call" | custom-call | flops 4000000000 | bytes 20000000 | tf_op jit(solution)/shard_map/pallas_call | solution.py:171
  85.7 14.5 %all-to-all-start.2 = ((f32[8,2,16,128]{3,2,1,0:T(8,128)}), f32[8,2,16,128]{3,2,1,0:T(8,128)S(1)}, u32[]{:S(2)}, u32[]{:S(2)}) async-start(f32[8,2,16,128]{3,2,1,0:T(8,128)} %shard_map.108), calls=%async_computation.2 | async-start | bytes 262144 | tf_op jit(solution)/shard_map/all_to_all | solution.py:555
  102.3 3.6 %collective-permute-start.3 = (bf16[208,128]{1,0:T(8,128)(2,1)S(1)}, bf16[208,128]{1,0:T(8,128)(2,1)S(1)}, u32[]{:S(2)}, u32[]{:S(2)}) collective-permute-start(bf16[208,128]{1,0:T(8,128)(2,1)S(1)} %get-tuple-element.125), channel_id=1, source_target_pairs={{0,1},{1,2},{2,3},{3,4},{4,5},{5,6},{6,7},{8,9},{9,10},{10,11},{11... | collective-permute-start | bytes 159752 | tf_op jit(solution)/shard_map/ppermute | solution.py:456
  107.5 4.1 %all-to-all-start.3 = ((f32[32,4,128]{2,1,0:T(4,128)}), f32[32,4,128]{2,1,0:T(4,128)S(1)}, u32[]{:S(2)}, u32[]{:S(2)}) async-start(f32[32,4,128]{2,1,0:T(4,128)} %bitcast.20), calls=%async_computation.3 | async-start | bytes 131072 | tf_op jit(solution)/shard_map/all_to_all | solution.py:560
  111.6 4.0 %shard_map.110 = (f32[6,18,16,128]{3,2,1,0:T(8,128)S(1)}, f32[4,16,16,128]{3,2,1,0:T(8,128)S(1)}) custom-call(s32[8]{0:T(128)S(1)} %convert_element_type.58.flags_ref, f32[4,16,16,128]{3,2,1,0:T(8,128)S(1)} %maximum_select_fusion.pot.pot_in, bf16[2,16,16,128]{3,2,1,0:T(8,128)(2,1)S(1)} %bitcast.59, bf16[2,16,16,128]{3,2,1,0:T(8,128)(2,1)S(1)} %bitcast.62, ...), custom_call_target="tpu_custom_call" | custom-call | flops 2000000 | bytes 2000000 | tf_op jit(solution)/shard_map/pallas_call | solution.py:33
  115.5 4.9 %all-to-all-done.3 = f32[32,4,128]{2,1,0:T(4,128)S(1)} async-done(((f32[32,4,128]{2,1,0:T(4,128)}), f32[32,4,128]{2,1,0:T(4,128)S(1)}, u32[]{:S(2)}, u32[]{:S(2)}) %all-to-all-start.3) | async-done | bytes 65568 | tf_op jit(solution)/shard_map/all_to_all | solution.py:560
  120.4 2.5 %shard_map.111 = (f32[4,16,16,128]{3,2,1,0:T(8,128)S(1)}, f32[4,16,16,128]{3,2,1,0:T(8,128)S(1)}, bf16[1,16,16,128]{3,2,1,0:T(8,128)(2,1)S(1)}, bf16[1,16,16,128...) custom-call(f32[128,128]{1,0:T(8,128)S(1)} %bitcast.76, ...), custom_call_target="tpu_custom_call" | custom-call | flops 2000000 | bytes 2000000 | tf_op jit(solution)/shard_map/pallas_call | solution.py:33
  126.8 5.6 %collective-permute-start.8 = (bf16[4,1,16,128]{3,2,1,0:T(8,128)(2,1)S(1)}, bf16[4,1,16,128]{3,2,1,0:T(8,128)(2,1)S(1)}, u32[]{:S(2)}, u32[]{:S(2)}) collective-permute-start(bf16[4,1,16,128]{3,2,1,0:T(8,128)(2,1)S(1)} %get-tuple-element.69), channel_id=1, source_target_pairs={{0,1},{1,2},{2,3},{3,4},{4,5},{5,6},{6,7},{8,9},{9,10},{10,11},{11... | collective-permute-start | bytes 49160 | tf_op jit(solution)/shard_map/ppermute | solution.py:456
  134.3 3.1 %collective-permute-done.9.yh = bf16[4,1,16,128]{3,2,1,0:T(8,128)(2,1)S(1)} collective-permute-done((bf16[4,1,16,128]{3,2,1,0:T(8,128)(2,1)S(1)}, bf16[4,1,16,128]{3,2,1,0:T(8,128)(2,1)S(1)}, u32[]{:S(2)}, u32[]{:S(2)}) %collective-permute-start.9) | collective-permute-done | bytes 16416 | tf_op jit(solution)/shard_map/ppermute | solution.py:456
  138.4 3.0 %shard_map.112 = (f32[4,16,16,128]{3,2,1,0:T(8,128)S(1)}, f32[128,128]{1,0:T(8,128)S(1)}) custom-call(f32[4,16,16,128]{3,2,1,0:T(8,128)S(1)} %get-tuple-element.66.pot_in, bf16[1,16,16,128]{3,2,1,0:T(8,128)(2,1)S(1)} %collective-permute-done.6.xl, bf16[1,16,16,128]{3,2,1,0:T(8,128)(2,1)S(1)} %collective-permute-done.7.xh, ...), custom_call_target="tpu_custom_call" | custom-call | flops 2000000 | bytes 2000000 | tf_op jit(solution)/shard_map/pallas_call | solution.py:33
  141.4 15.3 %all_to_all.40 = f32[32,4,128]{2,1,0:T(4,128)S(1)} all-to-all(f32[32,4,128]{2,1,0:T(4,128)S(1)} %bitcast.82), channel_id=1, replica_groups=mesh['x'=4,'y'=8,'h'=2,'z'=4,'c'=2] {'x','y'}, dimensions={0} | all-to-all | bytes 131072 | tf_op jit(solution)/shard_map/all_to_all | solution.py:527
  157.6 3.9 %all-to-all-start.5 = ((bf16[32,32,128]{2,1,0:T(8,128)(2,1)}), bf16[32,32,128]{2,1,0:T(8,128)(2,1)S(1)}, u32[]{:S(2)}, u32[]{:S(2)}) async-start(bf16[32,32,128]{2,1,0:T(8,128)(2,1)} %shard_map.113), calls=%async_computation.5 | async-start | bytes 524288 | tf_op jit(solution)/shard_map/all_to_all | solution.py:531
  161.6 3.0 %collective-permute-start.10 = (bf16[512,128]{1,0:T(8,128)(2,1)S(1)}, bf16[512,128]{1,0:T(8,128)(2,1)S(1)}, u32[]{:S(2)}, u32[]{:S(2)}) collective-permute-start(bf16[512,128]{1,0:T(8,128)(2,1)S(1)} %bitcast.95), channel_id=1, source_target_pairs={{0,16},{16,32},{32,48},{48,64},{64,80},{80,96},{96,112},{112,128},... | collective-permute-start | bytes 393224 | tf_op jit(solution)/shard_map/ppermute | solution.py:456
  166.1 7.3 %all-to-all-done.5.arr = bf16[32,32,128]{2,1,0:T(8,128)(2,1)S(1)} async-done(((bf16[32,32,128]{2,1,0:T(8,128)(2,1)}), bf16[32,32,128]{2,1,0:T(8,128)(2,1)S(1)}, u32[]{:S(2)}, u32[]{:S(2)}) %all-to-all-start.5) | async-done | bytes 262176 | tf_op jit(solution)/shard_map/all_to_all | solution.py:531
  174.1 12.7 %shard_map.114 = f32[8,2,16,128]{3,2,1,0:T(8,128)} custom-call(bf16[32,32,128]{2,1,0:T(8,128)(2,1)} %copy-done.8, f32[3,1024]{1,0:T(4,128)} %reshape.108.t_ref, bf16[8192,1024]{1,0:T(8,128)(2,1)} %get-tuple-element.52.ka.kb.kc.kd, bf16[8192,1024]{1,0:T(8,128)(2,1)} %get-tuple-element.52.ka.kb.kc.kd, bf16[8192,1024]{1,0:T(8,128)(2,1)} %get-tuple-element.52.ka.kb.kc.kd, ...), custom_call_target="tpu_custom_call" | custom-call | flops 4000000000 | bytes 20000000 | tf_op jit(solution)/shard_map/pallas_call | solution.py:171
  186.8 5.6 %all-to-all-start.6 = ((f32[8,2,16,128]{3,2,1,0:T(8,128)}), f32[8,2,16,128]{3,2,1,0:T(8,128)S(1)}, u32[]{:S(2)}, u32[]{:S(2)}) async-start(f32[8,2,16,128]{3,2,1,0:T(8,128)} %shard_map.114), calls=%async_computation.6 | async-start | bytes 262144 | tf_op jit(solution)/shard_map/all_to_all | solution.py:555
  192.5 3.5 %collective-permute-start.12 = (bf16[192,128]{1,0:T(8,128)(2,1)S(1)}, bf16[192,128]{1,0:T(8,128)(2,1)S(1)}, u32[]{:S(2)}, u32[]{:S(2)}) collective-permute-start(bf16[192,128]{1,0:T(8,128)(2,1)S(1)} %bitcast.98), channel_id=1, source_target_pairs={{0,1},{1,2},{2,3},{3,4},{4,5},{5,6},{6,7},{8,9},{9,10},{10,11},{11... | collective-permute-start | bytes 147464 | tf_op jit(solution)/shard_map/ppermute | solution.py:456
  201.4 4.5 %all-to-all-start.7 = ((f32[32,4,128]{2,1,0:T(4,128)}), f32[32,4,128]{2,1,0:T(4,128)S(1)}, u32[]{:S(2)}, u32[]{:S(2)}) async-start(f32[32,4,128]{2,1,0:T(4,128)} %bitcast.33), calls=%async_computation.7 | async-start | bytes 131072 | tf_op jit(solution)/shard_map/all_to_all | solution.py:560
  206.0 4.0 %shard_map.116 = (f32[6,18,16,128]{3,2,1,0:T(8,128)S(1)}, f32[4,16,16,128]{3,2,1,0:T(8,128)S(1)}) custom-call(s32[8]{0:T(128)S(1)} %convert_element_type.58.flags_ref, f32[4,16,16,128]{3,2,1,0:T(8,128)S(1)} %get-tuple-element.76.pot.pot_in, bf16[2,16,16,128]{3,2,1,0:T(8,128)(2,1)S(1)} %bitcast.65, bf16[2,16,16,128]{3,2,1,0:T(8,128)(2,1)S(1)} %bitcast.68, ...), custom_call_target="tpu_custom_call" | custom-call | flops 2000000 | bytes 2000000 | tf_op jit(solution)/shard_map/pallas_call | solution.py:33
  209.9 5.5 %all-to-all-done.7 = f32[32,4,128]{2,1,0:T(4,128)S(1)} async-done(((f32[32,4,128]{2,1,0:T(4,128)}), f32[32,4,128]{2,1,0:T(4,128)S(1)}, u32[]{:S(2)}, u32[]{:S(2)}) %all-to-all-start.7) | async-done | bytes 65568 | tf_op jit(solution)/shard_map/all_to_all | solution.py:560
  215.4 2.5 %shard_map.117 = (f32[4,16,16,128]{3,2,1,0:T(8,128)S(1)}, f32[4,16,16,128]{3,2,1,0:T(8,128)S(1)}, bf16[1,16,16,128]{3,2,1,0:T(8,128)(2,1)S(1)}, bf16[1,16,16,128...) custom-call(f32[128,128]{1,0:T(8,128)S(1)} %bitcast.75, ...), custom_call_target="tpu_custom_call" | custom-call | flops 2000000 | bytes 2000000 | tf_op jit(solution)/shard_map/pallas_call | solution.py:33
  217.9 2.8 %collective-permute-start.16 = (bf16[4,1,16,128]{3,2,1,0:T(8,128)(2,1)S(1)}, bf16[4,1,16,128]{3,2,1,0:T(8,128)(2,1)S(1)}, u32[]{:S(2)}, u32[]{:S(2)}) collective-permute-start(bf16[4,1,16,128]{3,2,1,0:T(8,128)(2,1)S(1)} %get-tuple-element.90), channel_id=1, source_target_pairs={{0,1},{1,2},{2,3},{3,4},{4,5},{5,6},{6,7},{8,9},{9,10},{10,11},{11... | collective-permute-start | bytes 49160 | tf_op jit(solution)/shard_map/ppermute | solution.py:456
  222.6 2.9 %collective-permute-start.14 = (bf16[1,16,16,128]{3,2,1,0:T(8,128)(2,1)S(1)}, bf16[1,16,16,128]{3,2,1,0:T(8,128)(2,1)S(1)}, u32[]{:S(2)}, u32[]{:S(2)}) collective-permute-start(bf16[1,16,16,128]{3,2,1,0:T(8,128)(2,1)S(1)} %get-tuple-element.88), channel_id=1, source_target_pairs={{0,16},{16,32},{32,48},{48,64},{64,80},{80,96},{96,112},{112,128},... | collective-permute-start | bytes 196616 | tf_op jit(solution)/shard_map/ppermute | solution.py:456
  226.8 4.1 %collective-permute-done.15.xh = bf16[1,16,16,128]{3,2,1,0:T(8,128)(2,1)S(1)} collective-permute-done((bf16[1,16,16,128]{3,2,1,0:T(8,128)(2,1)S(1)}, bf16[1,16,16,128]{3,2,1,0:T(8,128)(2,1)S(1)}, u32[]{:S(2)}, u32[]{:S(2)}) %collective-permute-start.15) | collective-permute-done | bytes 65568 | tf_op jit(solution)/shard_map/ppermute | solution.py:456
  234.9 8.5 %collective-permute-done.18 = bf16[544,128]{1,0:T(8,128)(2,1)S(1)} collective-permute-done((bf16[544,128]{1,0:T(8,128)(2,1)S(1)}, bf16[544,128]{1,0:T(8,128)(2,1)S(1)}, u32[]{:S(2)}, u32[]{:S(2)}) %collective-permute-start.18) | collective-permute-done | bytes 139296 | tf_op jit(solution)/shard_map/ppermute | solution.py:460
  (120 shorter events, 41.6 us)
Async XLA Ops:
  0.6 45.9 %copy-start.10 = (f32[32,2,16,128]{3,2,1,0:T(8,128)S(1)}, f32[32,2,16,128]{3,2,1,0:T(8,128)}, u32[]{:S(2)}) copy-start(f32[32,2,16,128]{3,2,1,0:T(8,128)} %param.9) | copy-start | bytes 1572868
  2.1 0.7 copy-start.2
  2.8 0.7 copy-start.3
  6.4 21.9 %collective-permute-start = (f32[576,128]{1,0:T(8,128)S(1)}, f32[576,128]{1,0:T(8,128)S(1)}, u32[]{:S(2)}, u32[]{:S(2)}) collective-permute-start(f32[576,128]{1,0:T(8,128)S(1)} %pad_maximum_fusion), channel_id=1, source_target_pairs={{0,8},{8,0},{1,9},{9,1},{2,10},{10,2},{3,11},{11,3},{4,12},{12,4},... | collective-permute-start | bytes 884744 | tf_op jit(solution)/shard_map/ppermute | solution.py:460
  32.3 18.5 %all-to-all-start = ((f32[32,4,128]{2,1,0:T(4,128)}), f32[32,4,128]{2,1,0:T(4,128)S(1)}, u32[]{:S(2)}, u32[]{:S(2)}) async-start(f32[32,4,128]{2,1,0:T(4,128)} %bitcast.12), calls=%async_computation | async-start | bytes 131072 | tf_op jit(solution)/shard_map/all_to_all | solution.py:527
  42.1 43.7 %collective-permute-start.1 = (bf16[528,128]{1,0:T(8,128)(2,1)S(1)}, bf16[528,128]{1,0:T(8,128)(2,1)S(1)}, u32[]{:S(2)}, u32[]{:S(2)}) collective-permute-start(bf16[528,128]{1,0:T(8,128)(2,1)S(1)} %pad_maximum_fusion.2), channel_id=1, source_target_pairs={{0,16},{16,32},{32,48},{48,64},{64,80},{80,96},{96,112},{112,128},... | collective-permute-start | bytes 405512 | tf_op jit(solution)/shard_map/ppermute | solution.py:456
  45.2 40.5 %collective-permute-start.2 = (bf16[528,128]{1,0:T(8,128)(2,1)S(1)}, bf16[528,128]{1,0:T(8,128)(2,1)S(1)}, u32[]{:S(2)}, u32[]{:S(2)}) collective-permute-start(bf16[528,128]{1,0:T(8,128)(2,1)S(1)} %pad_maximum_fusion.3), channel_id=1, source_target_pairs={{16,0},{32,16},{48,32},{64,48},{80,64},{96,80},{112,96},{128,112},... | collective-permute-start | bytes 405512 | tf_op jit(solution)/shard_map/ppermute | solution.py:456
  46.9 15.8 %collective-permute-start.5 = (bf16[2,16,16,128]{3,2,1,0:T(8,128)(2,1)S(1)}, bf16[2,16,16,128]{3,2,1,0:T(8,128)(2,1)S(1)}, u32[]{:S(2)}, u32[]{:S(2)}) collective-permute-start(bf16[2,16,16,128]{3,2,1,0:T(8,128)(2,1)S(1)} %select_convert_fusion.1), channel_id=1, source_target_pairs={{0,8},{8,0},{1,9},{9,1},{2,10},{10,2},{3,11},{11,3},{4,12},{12,4},... | collective-permute-start | bytes 393224 | tf_op jit(solution)/shard_map/ppermute | solution.py:460
  51.8 20.5 %all-to-all-start.1 = ((bf16[32,32,128]{2,1,0:T(8,128)(2,1)}), bf16[32,32,128]{2,1,0:T(8,128)(2,1)S(1)}, u32[]{:S(2)}, u32[]{:S(2)}) async-start(bf16[32,32,128]{2,1,0:T(8,128)(2,1)} %shard_map.106), calls=%async_computation.1 | async-start | bytes 524288 | tf_op jit(solution)/shard_map/all_to_all | solution.py:531
  72.3 0.7 copy-start.9
  85.7 20.2 %all-to-all-start.2 = ((f32[8,2,16,128]{3,2,1,0:T(8,128)}), f32[8,2,16,128]{3,2,1,0:T(8,128)S(1)}, u32[]{:S(2)}, u32[]{:S(2)}) async-start(f32[8,2,16,128]{3,2,1,0:T(8,128)} %shard_map.108), calls=%async_computation.2 | async-start | bytes 262144 | tf_op jit(solution)/shard_map/all_to_all | solution.py:555
  100.4 7.1 %collective-permute-start.4 = (bf16[208,128]{1,0:T(8,128)(2,1)S(1)}, bf16[208,128]{1,0:T(8,128)(2,1)S(1)}, u32[]{:S(2)}, u32[]{:S(2)}) collective-permute-start(bf16[208,128]{1,0:T(8,128)(2,1)S(1)} %get-tuple-element.124), channel_id=1, source_target_pairs={{1,0},{2,1},{3,2},{4,3},{5,4},{6,5},{7,6},{9,8},{10,9},{11,10},{12... | collective-permute-start | bytes 159752 | tf_op jit(solution)/shard_map/ppermute | solution.py:456
  102.3 5.2 %collective-permute-start.3 = (bf16[208,128]{1,0:T(8,128)(2,1)S(1)}, bf16[208,128]{1,0:T(8,128)(2,1)S(1)}, u32[]{:S(2)}, u32[]{:S(2)}) collective-permute-start(bf16[208,128]{1,0:T(8,128)(2,1)S(1)} %get-tuple-element.125), channel_id=1, source_target_pairs={{0,1},{1,2},{2,3},{3,4},{4,5},{5,6},{6,7},{8,9},{9,10},{10,11},{11... | collective-permute-start | bytes 159752 | tf_op jit(solution)/shard_map/ppermute | solution.py:456
  107.5 12.9 %all-to-all-start.3 = ((f32[32,4,128]{2,1,0:T(4,128)}), f32[32,4,128]{2,1,0:T(4,128)S(1)}, u32[]{:S(2)}, u32[]{:S(2)}) async-start(f32[32,4,128]{2,1,0:T(4,128)} %bitcast.20), calls=%async_computation.3 | async-start | bytes 131072 | tf_op jit(solution)/shard_map/all_to_all | solution.py:560
  123.0 14.5 %collective-permute-start.6 = (bf16[1,16,16,128]{3,2,1,0:T(8,128)(2,1)S(1)}, bf16[1,16,16,128]{3,2,1,0:T(8,128)(2,1)S(1)}, u32[]{:S(2)}, u32[]{:S(2)}) collective-permute-start(bf16[1,16,16,128]{3,2,1,0:T(8,128)(2,1)S(1)} %get-tuple-element.67), channel_id=1, source_target_pairs={{0,16},{16,32},{32,48},{48,64},{64,80},{80,96},{96,112},{112,128},... | collective-permute-start | bytes 196616 | tf_op jit(solution)/shard_map/ppermute | solution.py:456
  125.5 12.0 %collective-permute-start.7 = (bf16[1,16,16,128]{3,2,1,0:T(8,128)(2,1)S(1)}, bf16[1,16,16,128]{3,2,1,0:T(8,128)(2,1)S(1)}, u32[]{:S(2)}, u32[]{:S(2)}) collective-permute-start(bf16[1,16,16,128]{3,2,1,0:T(8,128)(2,1)S(1)} %get-tuple-element.68), channel_id=1, source_target_pairs={{16,0},{32,16},{48,32},{64,48},{80,64},{96,80},{112,96},{128,112},... | collective-permute-start | bytes 196616 | tf_op jit(solution)/shard_map/ppermute | solution.py:456
  126.8 7.5 %collective-permute-start.8 = (bf16[4,1,16,128]{3,2,1,0:T(8,128)(2,1)S(1)}, bf16[4,1,16,128]{3,2,1,0:T(8,128)(2,1)S(1)}, u32[]{:S(2)}, u32[]{:S(2)}) collective-permute-start(bf16[4,1,16,128]{3,2,1,0:T(8,128)(2,1)S(1)} %get-tuple-element.69), channel_id=1, source_target_pairs={{0,1},{1,2},{2,3},{3,4},{4,5},{5,6},{6,7},{8,9},{9,10},{10,11},{11... | collective-permute-start | bytes 49160 | tf_op jit(solution)/shard_map/ppermute | solution.py:456
  132.4 5.1 %collective-permute-start.9 = (bf16[4,1,16,128]{3,2,1,0:T(8,128)(2,1)S(1)}, bf16[4,1,16,128]{3,2,1,0:T(8,128)(2,1)S(1)}, u32[]{:S(2)}, u32[]{:S(2)}) collective-permute-start(bf16[4,1,16,128]{3,2,1,0:T(8,128)(2,1)S(1)} %get-tuple-element.70), channel_id=1, source_target_pairs={{1,0},{2,1},{3,2},{4,3},{5,4},{6,5},{7,6},{9,8},{10,9},{11,10},{12... | collective-permute-start | bytes 49160 | tf_op jit(solution)/shard_map/ppermute | solution.py:456
  137.5 1.0 copy-start.1
  157.6 15.8 %all-to-all-start.5 = ((bf16[32,32,128]{2,1,0:T(8,128)(2,1)}), bf16[32,32,128]{2,1,0:T(8,128)(2,1)S(1)}, u32[]{:S(2)}, u32[]{:S(2)}) async-start(bf16[32,32,128]{2,1,0:T(8,128)(2,1)} %shard_map.113), calls=%async_computation.5 | async-start | bytes 524288 | tf_op jit(solution)/shard_map/all_to_all | solution.py:531
  161.6 25.3 %collective-permute-start.10 = (bf16[512,128]{1,0:T(8,128)(2,1)S(1)}, bf16[512,128]{1,0:T(8,128)(2,1)S(1)}, u32[]{:S(2)}, u32[]{:S(2)}) collective-permute-start(bf16[512,128]{1,0:T(8,128)(2,1)S(1)} %bitcast.95), channel_id=1, source_target_pairs={{0,16},{16,32},{32,48},{48,64},{64,80},{80,96},{96,112},{112,128},... | collective-permute-start | bytes 393224 | tf_op jit(solution)/shard_map/ppermute | solution.py:456
  164.6 22.2 %collective-permute-start.11 = (bf16[512,128]{1,0:T(8,128)(2,1)S(1)}, bf16[512,128]{1,0:T(8,128)(2,1)S(1)}, u32[]{:S(2)}, u32[]{:S(2)}) collective-permute-start(bf16[512,128]{1,0:T(8,128)(2,1)S(1)} %bitcast.94), channel_id=1, source_target_pairs={{16,0},{32,16},{48,32},{64,48},{80,64},{96,80},{112,96},{128,112},... | collective-permute-start | bytes 393224 | tf_op jit(solution)/shard_map/ppermute | solution.py:456
  173.4 0.7 copy-start.8
  186.8 11.4 %all-to-all-start.6 = ((f32[8,2,16,128]{3,2,1,0:T(8,128)}), f32[8,2,16,128]{3,2,1,0:T(8,128)S(1)}, u32[]{:S(2)}, u32[]{:S(2)}) async-start(f32[8,2,16,128]{3,2,1,0:T(8,128)} %shard_map.114), calls=%async_computation.6 | async-start | bytes 262144 | tf_op jit(solution)/shard_map/all_to_all | solution.py:555
  192.5 7.3 %collective-permute-start.12 = (bf16[192,128]{1,0:T(8,128)(2,1)S(1)}, bf16[192,128]{1,0:T(8,128)(2,1)S(1)}, u32[]{:S(2)}, u32[]{:S(2)}) collective-permute-start(bf16[192,128]{1,0:T(8,128)(2,1)S(1)} %bitcast.98), channel_id=1, source_target_pairs={{0,1},{1,2},{2,3},{3,4},{4,5},{5,6},{6,7},{8,9},{9,10},{10,11},{11... | collective-permute-start | bytes 147464 | tf_op jit(solution)/shard_map/ppermute | solution.py:456
  196.0 5.4 %collective-permute-start.13 = (bf16[192,128]{1,0:T(8,128)(2,1)S(1)}, bf16[192,128]{1,0:T(8,128)(2,1)S(1)}, u32[]{:S(2)}, u32[]{:S(2)}) collective-permute-start(bf16[192,128]{1,0:T(8,128)(2,1)S(1)} %bitcast.99), channel_id=1, source_target_pairs={{1,0},{2,1},{3,2},{4,3},{5,4},{6,5},{7,6},{9,8},{10,9},{11,10},{12... | collective-permute-start | bytes 147464 | tf_op jit(solution)/shard_map/ppermute | solution.py:456
  201.4 14.0 %all-to-all-start.7 = ((f32[32,4,128]{2,1,0:T(4,128)}), f32[32,4,128]{2,1,0:T(4,128)S(1)}, u32[]{:S(2)}, u32[]{:S(2)}) async-start(f32[32,4,128]{2,1,0:T(4,128)} %bitcast.33), calls=%async_computation.7 | async-start | bytes 131072 | tf_op jit(solution)/shard_map/all_to_all | solution.py:560
  217.9 8.9 %collective-permute-start.16 = (bf16[4,1,16,128]{3,2,1,0:T(8,128)(2,1)S(1)}, bf16[4,1,16,128]{3,2,1,0:T(8,128)(2,1)S(1)}, u32[]{:S(2)}, u32[]{:S(2)}) collective-permute-start(bf16[4,1,16,128]{3,2,1,0:T(8,128)(2,1)S(1)} %get-tuple-element.90), channel_id=1, source_target_pairs={{0,1},{1,2},{2,3},{3,4},{4,5},{5,6},{6,7},{8,9},{9,10},{10,11},{11... | collective-permute-start | bytes 49160 | tf_op jit(solution)/shard_map/ppermute | solution.py:456
  220.7 6.1 %collective-permute-start.17 = (bf16[4,1,16,128]{3,2,1,0:T(8,128)(2,1)S(1)}, bf16[4,1,16,128]{3,2,1,0:T(8,128)(2,1)S(1)}, u32[]{:S(2)}, u32[]{:S(2)}) collective-permute-start(bf16[4,1,16,128]{3,2,1,0:T(8,128)(2,1)S(1)} %get-tuple-element.91), channel_id=1, source_target_pairs={{1,0},{2,1},{3,2},{4,3},{5,4},{6,5},{7,6},{9,8},{10,9},{11,10},{12... | collective-permute-start | bytes 49160 | tf_op jit(solution)/shard_map/ppermute | solution.py:456
  222.6 4.2 %collective-permute-start.14 = (bf16[1,16,16,128]{3,2,1,0:T(8,128)(2,1)S(1)}, bf16[1,16,16,128]{3,2,1,0:T(8,128)(2,1)S(1)}, u32[]{:S(2)}, u32[]{:S(2)}) collective-permute-start(bf16[1,16,16,128]{3,2,1,0:T(8,128)(2,1)S(1)} %get-tuple-element.88), channel_id=1, source_target_pairs={{0,16},{16,32},{32,48},{48,64},{64,80},{80,96},{96,112},{112,128},... | collective-permute-start | bytes 196616 | tf_op jit(solution)/shard_map/ppermute | solution.py:456
  225.5 5.4 %collective-permute-start.15 = (bf16[1,16,16,128]{3,2,1,0:T(8,128)(2,1)S(1)}, bf16[1,16,16,128]{3,2,1,0:T(8,128)(2,1)S(1)}, u32[]{:S(2)}, u32[]{:S(2)}) collective-permute-start(bf16[1,16,16,128]{3,2,1,0:T(8,128)(2,1)S(1)} %get-tuple-element.89), channel_id=1, source_target_pairs={{16,0},{32,16},{48,32},{64,48},{80,64},{96,80},{112,96},{128,112},... | collective-permute-start | bytes 196616 | tf_op jit(solution)/shard_map/ppermute | solution.py:456
  232.8 10.7 %collective-permute-start.18 = (bf16[544,128]{1,0:T(8,128)(2,1)S(1)}, bf16[544,128]{1,0:T(8,128)(2,1)S(1)}, u32[]{:S(2)}, u32[]{:S(2)}) collective-permute-start(bf16[544,128]{1,0:T(8,128)(2,1)S(1)} %pad_maximum_fusion.1), channel_id=1, source_target_pairs={{0,8},{8,0},{1,9},{9,1},{2,10},{10,2},{3,11},{11,3},{4,12},{12,4},... | collective-permute-start | bytes 417800 | tf_op jit(solution)/shard_map/ppermute | solution.py:460
  (5 other events, 3.4 us)

commit v4 on v3

--- a/solution.py
+++ b/solution.py
@@ -29,14 +29,14 @@
     return jax.ShapeDtypeStruct(shape, dtype)
 
 
-def call(body, out_shape, args, smem=(), scratch=(), flops=2_000_000, nbytes=2_000_000):
+def call(body, out_shape, args, smem=(), scratch=(), flops=2_000_000, nbytes=2_000_000, room=8 << 20):
     return pl.pallas_call(
         body,
         out_shape=out_shape,
         in_specs=[SM if i in smem else VM for i in range(len(args))],
         out_specs=jax.tree.map(lambda _: VM, out_shape),
         scratch_shapes=list(scratch),
-        compiler_params=pltpu.CompilerParams(vmem_limit_bytes=8 << 20),
+        compiler_params=pltpu.CompilerParams(vmem_limit_bytes=room),
         cost_estimate=pl.CostEstimate(flops=flops, bytes_accessed=nbytes, transcendentals=0),
     )(*args)
 
@@ -492,10 +492,13 @@
         tables_body,
         sds((64, 128)),
         (face_cell, face_count, face_weight, slot_panel, target_points, material),
+        room=KERNEL_VMEM,
     )
     tables = block[:8]
     keep, give = halved(start, h)
     got = swap_h(jnp.concatenate([give.reshape(512, 128), block]))
+    exc_keep, exc_give = halved(excitation, h)
+    exc_got = swap_h(exc_give.astype(BF16))
     k0, turned = kernel_matrix(target_points, source_points)
 
     pot = by_h(h, keep, got[:512].reshape(2, LY, EH, LZ))
@@ -514,20 +517,16 @@
         smem=(0,),
     )
     their_targets = got[520:544].reshape(3, 1024)
+    exc = by_h(h, exc_keep, exc_got.astype(F32))
 
     rims = None
     for outer_index in range(ITERS):
-        if outer_index == 0:
-            msg, coarse, late = lax.optimization_barrier((msg, pot, excitation))
-            exc_keep, exc_give = halved(late, h)
-            exc = by_h(h, exc_keep, swap_h(exc_give.astype(BF16)).astype(F32))
-        else:
-            msg, coarse = lax.optimization_barrier((msg, pot))
-        coarse = coarse.astype(BF16)
         arrived = lax.all_to_all(msg.reshape(NXY, 4, 128), PLANE, 0, 0, tiled=True)
         dens = call(
             density_body, sds((NXY, 2 * EH, 128), BF16), (arrived.reshape(128, 128), owner_hot)
         )
+        dens, coarse = lax.optimization_barrier((dens, pot))
+        coarse = coarse.astype(BF16)
         dens = lax.all_to_all(dens, PLANE, 0, 0, tiled=True)
 
         up, down = coarse[2:4].reshape(512, 128), coarse[0:2].reshape(512, 128)

time: 248 us -> 245 us (0.988)
  starting transfers between devices: 110 us -> 103 us
  waiting for transfers between devices: 45.4 us -> 49.5 us
    all_to_all x1, waiting for transfers between devices: 0.41 us -> 8.85 us  [per_device(): arrived = lax.all_to_all(msg.reshape(NXY, 4, 128), PLANE, 0, 0, tiled=True)]
    all_to_all x2, starting transfers between devices: 14.8 us -> 7.74 us  [per_device(): dens = lax.all_to_all(dens, PLANE, 0, 0, tiled=True)]
    all_to_all x2, waiting for transfers between devices: 16.9 us -> 12.5 us  [per_device(): dens = lax.all_to_all(dens, PLANE, 0, 0, tiled=True)]
    unnamed x26 -> x13, local copies, waits for them, and re-layouts: 9.69 us -> 6.88 us
  transfers between devices with their start and end apart: 26 -> 26, of which waited for: 10 -> 10; matrix products, arithmetic and copies ran while one was open for 0% -> 2% of each run, Pallas kernels for 19% -> 20%
where the time goes in v4:
time: 245 us; the launch traced here: 242 us
  starting transfers between devices  103 us (42%)
  Pallas kernels  62.1 us (25%)
  waiting for transfers between devices  49.5 us (20%)
  blocking collectives  15.3 us (6%)
  local copies, waits for them, and re-layouts  9.29 us (4%)
    ppermute x16, starting transfers between devices, shift(): return lax.ppermute(value, axes, pairs)  40 us
    pallas_call x12, Pallas kernels, call(): pl.pallas_call(body, out_shape=out_shape, in_specs=[SM if i in smem else...  26.7 us
    pallas_call x2, Pallas kernels, partial_flux(): pl.pallas_call(flux_body, grid=(FLUX_STEPS,), out_shape=sds((8, 2, EH, 12...  25.3 us
    all_to_all x2, starting transfers between devices, per_device(): parts = lax.all_to_all(parts, ROW, 0, 0, tiled=True)  21.4 us
    ppermute x3, starting transfers between devices, swap_h(): return lax.ppermute(value, 'h', [(0, 1), (1, 0)])  15.5 us
    all_to_all x1, blocking collectives, per_device(): arrived = lax.all_to_all(msg.reshape(NXY, 4, 128), PLANE, 0, 0, tiled=True)  15.3 us
    all_to_all x2, waiting for transfers between devices, per_device(): dens = lax.all_to_all(dens, PLANE, 0, 0, tiled=True)  12.5 us
    all_to_all x2, waiting for transfers between devices, per_device(): back = lax.all_to_all(slots.reshape(NXY, 4, 128), PLANE, 0, 0, tiled=True)  10.4 us
  transfers between devices with their start and end apart: 26, of which 10 were waited for; matrix products, arithmetic and copies ran while one was open for 2% of the time, Pallas kernels for 20%

profile of v4, /device:TPU:1, one launch (start us, length us, event | category | flops | bytes accessed | tf_op | source)
XLA Modules:
  0.0 242.3 jit_solution(141849283558701616)
XLA Ops:
  2.0 11.5 %collective-permute-start.5 = (bf16[2,16,16,128]{3,2,1,0:T(8,128)(2,1)S(1)}, bf16[2,16,16,128]{3,2,1,0:T(8,128)(2,1)S(1)}, u32[]{:S(2)}, u32[]{:S(2)}) collective-permute-start(bf16[2,16,16,128]{3,2,1,0:T(8,128)(2,1)S(1)} %select_convert_fusion.1), channel_id=1, source_target_pairs={{0,8},{8,0},{1,9},{9,1},{2,10},{10,2},{3,11},{11,3},{4,12},{12,4},... | collective-permute-start | bytes 393224 | tf_op jit(solution)/shard_map/ppermute | solution.py:460
  20.9 10.2 %shard_map.107 = (bf16[8192,1024]{1,0:T(8,128)(2,1)}, bf16[8192,128]{1,0:T(8,128)(2,1)}) custom-call(f32[3,1024]{1,0:T(4,128)} %t_ref.1, f32[3,8192]{1,0:T(4,128)} %s_ref.1), custom_call_target="tpu_custom_call" | custom-call | flops 2000000000 | bytes 20000000 | tf_op jit(solution)/shard_map/pallas_call | solution.py:87
  35.1 9.7 %all-to-all-start = ((f32[32,4,128]{2,1,0:T(4,128)}), f32[32,4,128]{2,1,0:T(4,128)S(1)}, u32[]{:S(2)}, u32[]{:S(2)}) async-start(f32[32,4,128]{2,1,0:T(4,128)} %bitcast.8), calls=%async_computation | async-start | bytes 131072 | tf_op jit(solution)/shard_map/all_to_all | solution.py:524
  44.8 8.8 %all-to-all-done = f32[32,4,128]{2,1,0:T(4,128)S(1)} async-done(((f32[32,4,128]{2,1,0:T(4,128)}), f32[32,4,128]{2,1,0:T(4,128)S(1)}, u32[]{:S(2)}, u32[]{:S(2)}) %all-to-all-start) | async-done | bytes 65568 | tf_op jit(solution)/shard_map/all_to_all | solution.py:524
  54.6 3.9 %all-to-all-start.1 = ((bf16[32,32,128]{2,1,0:T(8,128)(2,1)}), bf16[32,32,128]{2,1,0:T(8,128)(2,1)S(1)}, u32[]{:S(2)}, u32[]{:S(2)}) async-start(bf16[32,32,128]{2,1,0:T(8,128)(2,1)} %shard_map.106), calls=%async_computation.1 | async-start | bytes 524288 | tf_op jit(solution)/shard_map/all_to_all | solution.py:530
  58.6 3.0 %collective-permute-start.1 = (bf16[528,128]{1,0:T(8,128)(2,1)S(1)}, bf16[528,128]{1,0:T(8,128)(2,1)S(1)}, u32[]{:S(2)}, u32[]{:S(2)}) collective-permute-start(bf16[528,128]{1,0:T(8,128)(2,1)S(1)} %pad_maximum_fusion.2), channel_id=1, source_target_pairs={{0,16},{16,32},{32,48},{48,64},{64,80},{80,96},{96,112},{112,128},... | collective-permute-start | bytes 405512 | tf_op jit(solution)/shard_map/ppermute | solution.py:456
  62.9 5.2 %all-to-all-done.1.arr = bf16[32,32,128]{2,1,0:T(8,128)(2,1)S(1)} async-done(((bf16[32,32,128]{2,1,0:T(8,128)(2,1)}), bf16[32,32,128]{2,1,0:T(8,128)(2,1)S(1)}, u32[]{:S(2)}, u32[]{:S(2)}) %all-to-all-start.1) | async-done | bytes 262176 | tf_op jit(solution)/shard_map/all_to_all | solution.py:530
  68.8 12.7 %shard_map.108 = f32[8,2,16,128]{3,2,1,0:T(8,128)} custom-call(bf16[32,32,128]{2,1,0:T(8,128)(2,1)} %copy-done.2, f32[3,1024]{1,0:T(4,128)} %reshape.108.t_ref, bf16[8192,1024]{1,0:T(8,128)(2,1)} %get-tuple-element.51.ka.kb.kc.kd, bf16[8192,1024]{1,0:T(8,128)(2,1)} %get-tuple-element.51.ka.kb.kc.kd, bf16[8192,1024]{1,0:T(8,128)(2,1)} %get-tuple-element.51.ka.kb.kc.kd, ...), custom_call_target="tpu_custom_call" | custom-call | flops 4000000000 | bytes 20000000 | tf_op jit(solution)/shard_map/pallas_call | solution.py:171
  81.5 15.8 %all-to-all-start.2 = ((f32[8,2,16,128]{3,2,1,0:T(8,128)}), f32[8,2,16,128]{3,2,1,0:T(8,128)S(1)}, u32[]{:S(2)}, u32[]{:S(2)}) async-start(f32[8,2,16,128]{3,2,1,0:T(8,128)} %shard_map.108), calls=%async_computation.2 | async-start | bytes 262144 | tf_op jit(solution)/shard_map/all_to_all | solution.py:554
  99.5 3.6 %collective-permute-start.3 = (bf16[208,128]{1,0:T(8,128)(2,1)S(1)}, bf16[208,128]{1,0:T(8,128)(2,1)S(1)}, u32[]{:S(2)}, u32[]{:S(2)}) collective-permute-start(bf16[208,128]{1,0:T(8,128)(2,1)S(1)} %get-tuple-element.123), channel_id=1, source_target_pairs={{0,1},{1,2},{2,3},{3,4},{4,5},{5,6},{6,7},{8,9},{9,10},{10,11},{11... | collective-permute-start | bytes 159752 | tf_op jit(solution)/shard_map/ppermute | solution.py:456
  104.7 3.9 %all-to-all-start.3 = ((f32[32,4,128]{2,1,0:T(4,128)}), f32[32,4,128]{2,1,0:T(4,128)S(1)}, u32[]{:S(2)}, u32[]{:S(2)}) async-start(f32[32,4,128]{2,1,0:T(4,128)} %bitcast.20), calls=%async_computation.3 | async-start | bytes 131072 | tf_op jit(solution)/shard_map/all_to_all | solution.py:559
  108.6 4.0 %shard_map.110 = (f32[6,18,16,128]{3,2,1,0:T(8,128)S(1)}, f32[4,16,16,128]{3,2,1,0:T(8,128)S(1)}) custom-call(s32[8]{0:T(128)S(1)} %convert_element_type.58.flags_ref, f32[4,16,16,128]{3,2,1,0:T(8,128)S(1)} %maximum_select_fusion.pot.pot_in, bf16[2,16,16,128]{3,2,1,0:T(8,128)(2,1)S(1)} %bitcast.59, bf16[2,16,16,128]{3,2,1,0:T(8,128)(2,1)S(1)} %bitcast.62, ...), custom_call_target="tpu_custom_call" | custom-call | flops 2000000 | bytes 2000000 | tf_op jit(solution)/shard_map/pallas_call | solution.py:33
  112.5 4.9 %all-to-all-done.3 = f32[32,4,128]{2,1,0:T(4,128)S(1)} async-done(((f32[32,4,128]{2,1,0:T(4,128)}), f32[32,4,128]{2,1,0:T(4,128)S(1)}, u32[]{:S(2)}, u32[]{:S(2)}) %all-to-all-start.3) | async-done | bytes 65568 | tf_op jit(solution)/shard_map/all_to_all | solution.py:559
  117.4 2.5 %shard_map.111 = (f32[4,16,16,128]{3,2,1,0:T(8,128)S(1)}, f32[4,16,16,128]{3,2,1,0:T(8,128)S(1)}, bf16[1,16,16,128]{3,2,1,0:T(8,128)(2,1)S(1)}, bf16[1,16,16,128...) custom-call(f32[128,128]{1,0:T(8,128)S(1)} %bitcast.75, ...), custom_call_target="tpu_custom_call" | custom-call | flops 2000000 | bytes 2000000 | tf_op jit(solution)/shard_map/pallas_call | solution.py:33
  123.8 5.6 %collective-permute-start.8 = (bf16[4,1,16,128]{3,2,1,0:T(8,128)(2,1)S(1)}, bf16[4,1,16,128]{3,2,1,0:T(8,128)(2,1)S(1)}, u32[]{:S(2)}, u32[]{:S(2)}) collective-permute-start(bf16[4,1,16,128]{3,2,1,0:T(8,128)(2,1)S(1)} %get-tuple-element.67), channel_id=1, source_target_pairs={{0,1},{1,2},{2,3},{3,4},{4,5},{5,6},{6,7},{8,9},{9,10},{10,11},{11... | collective-permute-start | bytes 49160 | tf_op jit(solution)/shard_map/ppermute | solution.py:456
  131.3 3.1 %collective-permute-done.9.yh = bf16[4,1,16,128]{3,2,1,0:T(8,128)(2,1)S(1)} collective-permute-done((bf16[4,1,16,128]{3,2,1,0:T(8,128)(2,1)S(1)}, bf16[4,1,16,128]{3,2,1,0:T(8,128)(2,1)S(1)}, u32[]{:S(2)}, u32[]{:S(2)}) %collective-permute-start.9) | collective-permute-done | bytes 16416 | tf_op jit(solution)/shard_map/ppermute | solution.py:456
  135.4 3.0 %shard_map.112 = (f32[4,16,16,128]{3,2,1,0:T(8,128)S(1)}, f32[128,128]{1,0:T(8,128)S(1)}) custom-call(f32[4,16,16,128]{3,2,1,0:T(8,128)S(1)} %get-tuple-element.64.pot_in, bf16[1,16,16,128]{3,2,1,0:T(8,128)(2,1)S(1)} %collective-permute-done.6.xl, bf16[1,16,16,128]{3,2,1,0:T(8,128)(2,1)S(1)} %collective-permute-done.7.xh, ...), custom_call_target="tpu_custom_call" | custom-call | flops 2000000 | bytes 2000000 | tf_op jit(solution)/shard_map/pallas_call | solution.py:33
  138.4 15.3 %all_to_all.40 = f32[32,4,128]{2,1,0:T(4,128)S(1)} all-to-all(f32[32,4,128]{2,1,0:T(4,128)S(1)} %bitcast.82), channel_id=1, replica_groups=mesh['x'=4,'y'=8,'h'=2,'z'=4,'c'=2] {'x','y'}, dimensions={0} | all-to-all | bytes 131072 | tf_op jit(solution)/shard_map/all_to_all | solution.py:524
  154.6 3.9 %all-to-all-start.5 = ((bf16[32,32,128]{2,1,0:T(8,128)(2,1)}), bf16[32,32,128]{2,1,0:T(8,128)(2,1)S(1)}, u32[]{:S(2)}, u32[]{:S(2)}) async-start(bf16[32,32,128]{2,1,0:T(8,128)(2,1)} %shard_map.113), calls=%async_computation.5 | async-start | bytes 524288 | tf_op jit(solution)/shard_map/all_to_all | solution.py:530
  158.5 3.0 %collective-permute-start.10 = (bf16[512,128]{1,0:T(8,128)(2,1)S(1)}, bf16[512,128]{1,0:T(8,128)(2,1)S(1)}, u32[]{:S(2)}, u32[]{:S(2)}) collective-permute-start(bf16[512,128]{1,0:T(8,128)(2,1)S(1)} %bitcast.95), channel_id=1, source_target_pairs={{0,16},{16,32},{32,48},{48,64},{64,80},{80,96},{96,112},{112,128},... | collective-permute-start | bytes 393224 | tf_op jit(solution)/shard_map/ppermute | solution.py:456
  163.1 7.3 %all-to-all-done.5.arr = bf16[32,32,128]{2,1,0:T(8,128)(2,1)S(1)} async-done(((bf16[32,32,128]{2,1,0:T(8,128)(2,1)}), bf16[32,32,128]{2,1,0:T(8,128)(2,1)S(1)}, u32[]{:S(2)}, u32[]{:S(2)}) %all-to-all-start.5) | async-done | bytes 262176 | tf_op jit(solution)/shard_map/all_to_all | solution.py:530
  171.1 12.7 %shard_map.114 = f32[8,2,16,128]{3,2,1,0:T(8,128)} custom-call(bf16[32,32,128]{2,1,0:T(8,128)(2,1)} %copy-done.3, f32[3,1024]{1,0:T(4,128)} %reshape.108.t_ref, bf16[8192,1024]{1,0:T(8,128)(2,1)} %get-tuple-element.51.ka.kb.kc.kd, bf16[8192,1024]{1,0:T(8,128)(2,1)} %get-tuple-element.51.ka.kb.kc.kd, bf16[8192,1024]{1,0:T(8,128)(2,1)} %get-tuple-element.51.ka.kb.kc.kd, ...), custom_call_target="tpu_custom_call" | custom-call | flops 4000000000 | bytes 20000000 | tf_op jit(solution)/shard_map/pallas_call | solution.py:171
  183.8 5.6 %all-to-all-start.6 = ((f32[8,2,16,128]{3,2,1,0:T(8,128)}), f32[8,2,16,128]{3,2,1,0:T(8,128)S(1)}, u32[]{:S(2)}, u32[]{:S(2)}) async-start(f32[8,2,16,128]{3,2,1,0:T(8,128)} %shard_map.114), calls=%async_computation.6 | async-start | bytes 262144 | tf_op jit(solution)/shard_map/all_to_all | solution.py:554
  189.4 3.5 %collective-permute-start.12 = (bf16[192,128]{1,0:T(8,128)(2,1)S(1)}, bf16[192,128]{1,0:T(8,128)(2,1)S(1)}, u32[]{:S(2)}, u32[]{:S(2)}) collective-permute-start(bf16[192,128]{1,0:T(8,128)(2,1)S(1)} %bitcast.98), channel_id=1, source_target_pairs={{0,1},{1,2},{2,3},{3,4},{4,5},{5,6},{6,7},{8,9},{9,10},{10,11},{11... | collective-permute-start | bytes 147464 | tf_op jit(solution)/shard_map/ppermute | solution.py:456
  198.4 4.5 %all-to-all-start.7 = ((f32[32,4,128]{2,1,0:T(4,128)}), f32[32,4,128]{2,1,0:T(4,128)S(1)}, u32[]{:S(2)}, u32[]{:S(2)}) async-start(f32[32,4,128]{2,1,0:T(4,128)} %bitcast.33), calls=%async_computation.7 | async-start | bytes 131072 | tf_op jit(solution)/shard_map/all_to_all | solution.py:559
  202.9 4.0 %shard_map.116 = (f32[6,18,16,128]{3,2,1,0:T(8,128)S(1)}, f32[4,16,16,128]{3,2,1,0:T(8,128)S(1)}) custom-call(s32[8]{0:T(128)S(1)} %convert_element_type.58.flags_ref, f32[4,16,16,128]{3,2,1,0:T(8,128)S(1)} %get-tuple-element.74.pot.pot_in, bf16[2,16,16,128]{3,2,1,0:T(8,128)(2,1)S(1)} %bitcast.65, bf16[2,16,16,128]{3,2,1,0:T(8,128)(2,1)S(1)} %bitcast.68, ...), custom_call_target="tpu_custom_call" | custom-call | flops 2000000 | bytes 2000000 | tf_op jit(solution)/shard_map/pallas_call | solution.py:33
  206.9 5.5 %all-to-all-done.7 = f32[32,4,128]{2,1,0:T(4,128)S(1)} async-done(((f32[32,4,128]{2,1,0:T(4,128)}), f32[32,4,128]{2,1,0:T(4,128)S(1)}, u32[]{:S(2)}, u32[]{:S(2)}) %all-to-all-start.7) | async-done | bytes 65568 | tf_op jit(solution)/shard_map/all_to_all | solution.py:559
  212.3 2.5 %shard_map.117 = (f32[4,16,16,128]{3,2,1,0:T(8,128)S(1)}, f32[4,16,16,128]{3,2,1,0:T(8,128)S(1)}, bf16[1,16,16,128]{3,2,1,0:T(8,128)(2,1)S(1)}, bf16[1,16,16,128...) custom-call(f32[128,128]{1,0:T(8,128)S(1)} %bitcast.74, ...), custom_call_target="tpu_custom_call" | custom-call | flops 2000000 | bytes 2000000 | tf_op jit(solution)/shard_map/pallas_call | solution.py:33
  214.9 2.7 %collective-permute-start.16 = (bf16[4,1,16,128]{3,2,1,0:T(8,128)(2,1)S(1)}, bf16[4,1,16,128]{3,2,1,0:T(8,128)(2,1)S(1)}, u32[]{:S(2)}, u32[]{:S(2)}) collective-permute-start(bf16[4,1,16,128]{3,2,1,0:T(8,128)(2,1)S(1)} %get-tuple-element.88), channel_id=1, source_target_pairs={{0,1},{1,2},{2,3},{3,4},{4,5},{5,6},{6,7},{8,9},{9,10},{10,11},{11... | collective-permute-start | bytes 49160 | tf_op jit(solution)/shard_map/ppermute | solution.py:456
  219.5 2.9 %collective-permute-start.14 = (bf16[1,16,16,128]{3,2,1,0:T(8,128)(2,1)S(1)}, bf16[1,16,16,128]{3,2,1,0:T(8,128)(2,1)S(1)}, u32[]{:S(2)}, u32[]{:S(2)}) collective-permute-start(bf16[1,16,16,128]{3,2,1,0:T(8,128)(2,1)S(1)} %get-tuple-element.86), channel_id=1, source_target_pairs={{0,16},{16,32},{32,48},{48,64},{64,80},{80,96},{96,112},{112,128},... | collective-permute-start | bytes 196616 | tf_op jit(solution)/shard_map/ppermute | solution.py:456
  223.8 4.1 %collective-permute-done.15.xh = bf16[1,16,16,128]{3,2,1,0:T(8,128)(2,1)S(1)} collective-permute-done((bf16[1,16,16,128]{3,2,1,0:T(8,128)(2,1)S(1)}, bf16[1,16,16,128]{3,2,1,0:T(8,128)(2,1)S(1)}, u32[]{:S(2)}, u32[]{:S(2)}) %collective-permute-start.15) | collective-permute-done | bytes 65568 | tf_op jit(solution)/shard_map/ppermute | solution.py:456
  231.9 8.6 %collective-permute-done.18 = bf16[544,128]{1,0:T(8,128)(2,1)S(1)} collective-permute-done((bf16[544,128]{1,0:T(8,128)(2,1)S(1)}, bf16[544,128]{1,0:T(8,128)(2,1)S(1)}, u32[]{:S(2)}, u32[]{:S(2)}) %collective-permute-start.18) | collective-permute-done | bytes 139296 | tf_op jit(solution)/shard_map/ppermute | solution.py:460
  (106 shorter events, 43.7 us)
Async XLA Ops:
  2.0 29.0 %collective-permute-start.5 = (bf16[2,16,16,128]{3,2,1,0:T(8,128)(2,1)S(1)}, bf16[2,16,16,128]{3,2,1,0:T(8,128)(2,1)S(1)}, u32[]{:S(2)}, u32[]{:S(2)}) collective-permute-start(bf16[2,16,16,128]{3,2,1,0:T(8,128)(2,1)S(1)} %select_convert_fusion.1), channel_id=1, source_target_pairs={{0,8},{8,0},{1,9},{9,1},{2,10},{10,2},{3,11},{11,3},{4,12},{12,4},... | collective-permute-start | bytes 393224 | tf_op jit(solution)/shard_map/ppermute | solution.py:460
  17.2 13.9 %collective-permute-start = (f32[576,128]{1,0:T(8,128)S(1)}, f32[576,128]{1,0:T(8,128)S(1)}, u32[]{:S(2)}, u32[]{:S(2)}) collective-permute-start(f32[576,128]{1,0:T(8,128)S(1)} %pad_maximum_fusion), channel_id=1, source_target_pairs={{0,8},{8,0},{1,9},{9,1},{2,10},{10,2},{3,11},{11,3},{4,12},{12,4},... | collective-permute-start | bytes 884744 | tf_op jit(solution)/shard_map/ppermute | solution.py:460
  34.4 0.7 copy-start
  35.1 18.5 %all-to-all-start = ((f32[32,4,128]{2,1,0:T(4,128)}), f32[32,4,128]{2,1,0:T(4,128)S(1)}, u32[]{:S(2)}, u32[]{:S(2)}) async-start(f32[32,4,128]{2,1,0:T(4,128)} %bitcast.8), calls=%async_computation | async-start | bytes 131072 | tf_op jit(solution)/shard_map/all_to_all | solution.py:524
  54.6 13.5 %all-to-all-start.1 = ((bf16[32,32,128]{2,1,0:T(8,128)(2,1)}), bf16[32,32,128]{2,1,0:T(8,128)(2,1)S(1)}, u32[]{:S(2)}, u32[]{:S(2)}) async-start(bf16[32,32,128]{2,1,0:T(8,128)(2,1)} %shard_map.106), calls=%async_computation.1 | async-start | bytes 524288 | tf_op jit(solution)/shard_map/all_to_all | solution.py:530
  58.6 22.9 %collective-permute-start.1 = (bf16[528,128]{1,0:T(8,128)(2,1)S(1)}, bf16[528,128]{1,0:T(8,128)(2,1)S(1)}, u32[]{:S(2)}, u32[]{:S(2)}) collective-permute-start(bf16[528,128]{1,0:T(8,128)(2,1)S(1)} %pad_maximum_fusion.2), channel_id=1, source_target_pairs={{0,16},{16,32},{32,48},{48,64},{64,80},{80,96},{96,112},{112,128},... | collective-permute-start | bytes 405512 | tf_op jit(solution)/shard_map/ppermute | solution.py:456
  61.6 19.9 %collective-permute-start.2 = (bf16[528,128]{1,0:T(8,128)(2,1)S(1)}, bf16[528,128]{1,0:T(8,128)(2,1)S(1)}, u32[]{:S(2)}, u32[]{:S(2)}) collective-permute-start(bf16[528,128]{1,0:T(8,128)(2,1)S(1)} %pad_maximum_fusion.3), channel_id=1, source_target_pairs={{16,0},{32,16},{48,32},{64,48},{80,64},{96,80},{112,96},{128,112},... | collective-permute-start | bytes 405512 | tf_op jit(solution)/shard_map/ppermute | solution.py:456
  68.1 0.7 copy-start.2
  81.5 21.6 %all-to-all-start.2 = ((f32[8,2,16,128]{3,2,1,0:T(8,128)}), f32[8,2,16,128]{3,2,1,0:T(8,128)S(1)}, u32[]{:S(2)}, u32[]{:S(2)}) async-start(f32[8,2,16,128]{3,2,1,0:T(8,128)} %shard_map.108), calls=%async_computation.2 | async-start | bytes 262144 | tf_op jit(solution)/shard_map/all_to_all | solution.py:554
  97.5 7.1 %collective-permute-start.4 = (bf16[208,128]{1,0:T(8,128)(2,1)S(1)}, bf16[208,128]{1,0:T(8,128)(2,1)S(1)}, u32[]{:S(2)}, u32[]{:S(2)}) collective-permute-start(bf16[208,128]{1,0:T(8,128)(2,1)S(1)} %get-tuple-element.122), channel_id=1, source_target_pairs={{1,0},{2,1},{3,2},{4,3},{5,4},{6,5},{7,6},{9,8},{10,9},{11,10},{12... | collective-permute-start | bytes 159752 | tf_op jit(solution)/shard_map/ppermute | solution.py:456
  99.5 5.2 %collective-permute-start.3 = (bf16[208,128]{1,0:T(8,128)(2,1)S(1)}, bf16[208,128]{1,0:T(8,128)(2,1)S(1)}, u32[]{:S(2)}, u32[]{:S(2)}) collective-permute-start(bf16[208,128]{1,0:T(8,128)(2,1)S(1)} %get-tuple-element.123), channel_id=1, source_target_pairs={{0,1},{1,2},{2,3},{3,4},{4,5},{5,6},{6,7},{8,9},{9,10},{10,11},{11... | collective-permute-start | bytes 159752 | tf_op jit(solution)/shard_map/ppermute | solution.py:456
  104.7 12.7 %all-to-all-start.3 = ((f32[32,4,128]{2,1,0:T(4,128)}), f32[32,4,128]{2,1,0:T(4,128)S(1)}, u32[]{:S(2)}, u32[]{:S(2)}) async-start(f32[32,4,128]{2,1,0:T(4,128)} %bitcast.20), calls=%async_computation.3 | async-start | bytes 131072 | tf_op jit(solution)/shard_map/all_to_all | solution.py:559
  119.9 14.5 %collective-permute-start.6 = (bf16[1,16,16,128]{3,2,1,0:T(8,128)(2,1)S(1)}, bf16[1,16,16,128]{3,2,1,0:T(8,128)(2,1)S(1)}, u32[]{:S(2)}, u32[]{:S(2)}) collective-permute-start(bf16[1,16,16,128]{3,2,1,0:T(8,128)(2,1)S(1)} %get-tuple-element.65), channel_id=1, source_target_pairs={{0,16},{16,32},{32,48},{48,64},{64,80},{80,96},{96,112},{112,128},... | collective-permute-start | bytes 196616 | tf_op jit(solution)/shard_map/ppermute | solution.py:456
  122.5 12.0 %collective-permute-start.7 = (bf16[1,16,16,128]{3,2,1,0:T(8,128)(2,1)S(1)}, bf16[1,16,16,128]{3,2,1,0:T(8,128)(2,1)S(1)}, u32[]{:S(2)}, u32[]{:S(2)}) collective-permute-start(bf16[1,16,16,128]{3,2,1,0:T(8,128)(2,1)S(1)} %get-tuple-element.66), channel_id=1, source_target_pairs={{16,0},{32,16},{48,32},{64,48},{80,64},{96,80},{112,96},{128,112},... | collective-permute-start | bytes 196616 | tf_op jit(solution)/shard_map/ppermute | solution.py:456
  123.8 7.5 %collective-permute-start.8 = (bf16[4,1,16,128]{3,2,1,0:T(8,128)(2,1)S(1)}, bf16[4,1,16,128]{3,2,1,0:T(8,128)(2,1)S(1)}, u32[]{:S(2)}, u32[]{:S(2)}) collective-permute-start(bf16[4,1,16,128]{3,2,1,0:T(8,128)(2,1)S(1)} %get-tuple-element.67), channel_id=1, source_target_pairs={{0,1},{1,2},{2,3},{3,4},{4,5},{5,6},{6,7},{8,9},{9,10},{10,11},{11... | collective-permute-start | bytes 49160 | tf_op jit(solution)/shard_map/ppermute | solution.py:456
  129.4 5.1 %collective-permute-start.9 = (bf16[4,1,16,128]{3,2,1,0:T(8,128)(2,1)S(1)}, bf16[4,1,16,128]{3,2,1,0:T(8,128)(2,1)S(1)}, u32[]{:S(2)}, u32[]{:S(2)}) collective-permute-start(bf16[4,1,16,128]{3,2,1,0:T(8,128)(2,1)S(1)} %get-tuple-element.68), channel_id=1, source_target_pairs={{1,0},{2,1},{3,2},{4,3},{5,4},{6,5},{7,6},{9,8},{10,9},{11,10},{12... | collective-permute-start | bytes 49160 | tf_op jit(solution)/shard_map/ppermute | solution.py:456
  134.4 1.0 copy-start.1
  154.6 15.8 %all-to-all-start.5 = ((bf16[32,32,128]{2,1,0:T(8,128)(2,1)}), bf16[32,32,128]{2,1,0:T(8,128)(2,1)S(1)}, u32[]{:S(2)}, u32[]{:S(2)}) async-start(bf16[32,32,128]{2,1,0:T(8,128)(2,1)} %shard_map.113), calls=%async_computation.5 | async-start | bytes 524288 | tf_op jit(solution)/shard_map/all_to_all | solution.py:530
  158.5 25.2 %collective-permute-start.10 = (bf16[512,128]{1,0:T(8,128)(2,1)S(1)}, bf16[512,128]{1,0:T(8,128)(2,1)S(1)}, u32[]{:S(2)}, u32[]{:S(2)}) collective-permute-start(bf16[512,128]{1,0:T(8,128)(2,1)S(1)} %bitcast.95), channel_id=1, source_target_pairs={{0,16},{16,32},{32,48},{48,64},{64,80},{80,96},{96,112},{112,128},... | collective-permute-start | bytes 393224 | tf_op jit(solution)/shard_map/ppermute | solution.py:456
  161.6 22.2 %collective-permute-start.11 = (bf16[512,128]{1,0:T(8,128)(2,1)S(1)}, bf16[512,128]{1,0:T(8,128)(2,1)S(1)}, u32[]{:S(2)}, u32[]{:S(2)}) collective-permute-start(bf16[512,128]{1,0:T(8,128)(2,1)S(1)} %bitcast.94), channel_id=1, source_target_pairs={{16,0},{32,16},{48,32},{64,48},{80,64},{96,80},{112,96},{128,112},... | collective-permute-start | bytes 393224 | tf_op jit(solution)/shard_map/ppermute | solution.py:456
  170.4 0.7 copy-start.3
  183.8 11.4 %all-to-all-start.6 = ((f32[8,2,16,128]{3,2,1,0:T(8,128)}), f32[8,2,16,128]{3,2,1,0:T(8,128)S(1)}, u32[]{:S(2)}, u32[]{:S(2)}) async-start(f32[8,2,16,128]{3,2,1,0:T(8,128)} %shard_map.114), calls=%async_computation.6 | async-start | bytes 262144 | tf_op jit(solution)/shard_map/all_to_all | solution.py:554
  189.4 7.3 %collective-permute-start.12 = (bf16[192,128]{1,0:T(8,128)(2,1)S(1)}, bf16[192,128]{1,0:T(8,128)(2,1)S(1)}, u32[]{:S(2)}, u32[]{:S(2)}) collective-permute-start(bf16[192,128]{1,0:T(8,128)(2,1)S(1)} %bitcast.98), channel_id=1, source_target_pairs={{0,1},{1,2},{2,3},{3,4},{4,5},{5,6},{6,7},{8,9},{9,10},{10,11},{11... | collective-permute-start | bytes 147464 | tf_op jit(solution)/shard_map/ppermute | solution.py:456
  192.9 5.4 %collective-permute-start.13 = (bf16[192,128]{1,0:T(8,128)(2,1)S(1)}, bf16[192,128]{1,0:T(8,128)(2,1)S(1)}, u32[]{:S(2)}, u32[]{:S(2)}) collective-permute-start(bf16[192,128]{1,0:T(8,128)(2,1)S(1)} %bitcast.99), channel_id=1, source_target_pairs={{1,0},{2,1},{3,2},{4,3},{5,4},{6,5},{7,6},{9,8},{10,9},{11,10},{12... | collective-permute-start | bytes 147464 | tf_op jit(solution)/shard_map/ppermute | solution.py:456
  198.4 14.0 %all-to-all-start.7 = ((f32[32,4,128]{2,1,0:T(4,128)}), f32[32,4,128]{2,1,0:T(4,128)S(1)}, u32[]{:S(2)}, u32[]{:S(2)}) async-start(f32[32,4,128]{2,1,0:T(4,128)} %bitcast.33), calls=%async_computation.7 | async-start | bytes 131072 | tf_op jit(solution)/shard_map/all_to_all | solution.py:559
  214.9 8.9 %collective-permute-start.16 = (bf16[4,1,16,128]{3,2,1,0:T(8,128)(2,1)S(1)}, bf16[4,1,16,128]{3,2,1,0:T(8,128)(2,1)S(1)}, u32[]{:S(2)}, u32[]{:S(2)}) collective-permute-start(bf16[4,1,16,128]{3,2,1,0:T(8,128)(2,1)S(1)} %get-tuple-element.88), channel_id=1, source_target_pairs={{0,1},{1,2},{2,3},{3,4},{4,5},{5,6},{6,7},{8,9},{9,10},{10,11},{11... | collective-permute-start | bytes 49160 | tf_op jit(solution)/shard_map/ppermute | solution.py:456
  217.6 6.1 %collective-permute-start.17 = (bf16[4,1,16,128]{3,2,1,0:T(8,128)(2,1)S(1)}, bf16[4,1,16,128]{3,2,1,0:T(8,128)(2,1)S(1)}, u32[]{:S(2)}, u32[]{:S(2)}) collective-permute-start(bf16[4,1,16,128]{3,2,1,0:T(8,128)(2,1)S(1)} %get-tuple-element.89), channel_id=1, source_target_pairs={{1,0},{2,1},{3,2},{4,3},{5,4},{6,5},{7,6},{9,8},{10,9},{11,10},{12... | collective-permute-start | bytes 49160 | tf_op jit(solution)/shard_map/ppermute | solution.py:456
  219.5 4.2 %collective-permute-start.14 = (bf16[1,16,16,128]{3,2,1,0:T(8,128)(2,1)S(1)}, bf16[1,16,16,128]{3,2,1,0:T(8,128)(2,1)S(1)}, u32[]{:S(2)}, u32[]{:S(2)}) collective-permute-start(bf16[1,16,16,128]{3,2,1,0:T(8,128)(2,1)S(1)} %get-tuple-element.86), channel_id=1, source_target_pairs={{0,16},{16,32},{32,48},{48,64},{64,80},{80,96},{96,112},{112,128},... | collective-permute-start | bytes 196616 | tf_op jit(solution)/shard_map/ppermute | solution.py:456
  222.4 5.4 %collective-permute-start.15 = (bf16[1,16,16,128]{3,2,1,0:T(8,128)(2,1)S(1)}, bf16[1,16,16,128]{3,2,1,0:T(8,128)(2,1)S(1)}, u32[]{:S(2)}, u32[]{:S(2)}) collective-permute-start(bf16[1,16,16,128]{3,2,1,0:T(8,128)(2,1)S(1)} %get-tuple-element.87), channel_id=1, source_target_pairs={{16,0},{32,16},{48,32},{64,48},{80,64},{96,80},{112,96},{128,112},... | collective-permute-start | bytes 196616 | tf_op jit(solution)/shard_map/ppermute | solution.py:456
  229.7 10.8 %collective-permute-start.18 = (bf16[544,128]{1,0:T(8,128)(2,1)S(1)}, bf16[544,128]{1,0:T(8,128)(2,1)S(1)}, u32[]{:S(2)}, u32[]{:S(2)}) collective-permute-start(bf16[544,128]{1,0:T(8,128)(2,1)S(1)} %pad_maximum_fusion.1), channel_id=1, source_target_pairs={{0,8},{8,0},{1,9},{9,1},{2,10},{10,2},{3,11},{11,3},{4,12},{12,4},... | collective-permute-start | bytes 417800 | tf_op jit(solution)/shard_map/ppermute | solution.py:460
